TPU v7x, 32 devices: a whole 2x2x4 slice. The times are simulated.
32 devices in a mesh: comp: 2 (over x), tile: 16 (over z, y, core).
Axes of the slice: x: 2, y: 2, z: 4, core: 2. Of those that a mesh axis runs over, the one named last changes fastest.
Arguments:
- ocean_fields: float32 [2, 6, 64, 2048], P('comp', None, None, 'tile'), may hold values from -6 to 6, as said below
- tracers: float32 [19, 64, 2048], P(None, None, 'tile'), may hold values from -6 to 6
- reaction: float32 [19, 19], replicated, may hold values from -1.25 to 1.25
- wet_levels: int32 [2048], P('tile'), may hold values from 0 to 64, as said below
- neighbours: int32 [3, 2048], P(None, 'tile'), may hold values from 0 to 383, as said below
Outputs:
- ocean_out: float32 [2, 6, 64, 2048], P('comp', None, None, 'tile')
- chl_out: float32 [2, 64, 2048], P('comp', None, 'tile')
Inputs may be any that keep to these rules, and one draw needn't show every extreme that they name: `ocean_fields`: along the second dimension: temperature, salinity, eastward and northward velocity, a mixing index, and the shortwave flux, which lies between 0.2 and 2. `wet_levels`: 0 marks land; the share of land differs from tile to tile. `neighbours`: entry [k, c] gives the k-th neighbour of column c as a position in its tile's columns extended by 128 columns of each adjacent tile on both sides, the tiles closing into a loop: position p is the tile's column p - 128; no column is its own neighbour.
All inputs are finite; a program needn't handle non-finite values.
Results may differ from a plain program's by a relative error of at most 0.000061.
Values sent between devices are 32-bit elements; how exact they have to be, the bound alone decides.
No kernel may reach another device: no remote copies, remote signals or barrier semaphores. Data moves between devices by JAX's collectives and lax.ppermute only.
A program may use at most 64 MiB of HBM per device.

v0:
```python
import functools
import math

import jax
import jax.numpy as jnp
from jax import lax
from jax.experimental import pallas as pl
from jax.experimental.pallas import tpu as pltpu
from jax.sharding import PartitionSpec as P


ROTATE_COS = math.cos(0.3)
ROTATE_SIN = math.sin(0.3)
SUB = 8
AXES = ("comp", "tile")
ANGLES = [2.0 * math.pi * k / 3.0 for k in range(3)]
F32 = jnp.float32
BF16 = jnp.bfloat16
GRANT = 8 << 20


VMEM = pl.BlockSpec(memory_space=pltpu.VMEM)
SMEM = pl.BlockSpec(memory_space=pltpu.SMEM)
HBM = pl.BlockSpec(memory_space=pltpu.HBM)


class Plan:
    def __init__(self, nt, lev):
        self.nt, self.lev = nt, lev
        self.blocks = lev // SUB
        self.full = self.blocks // 2 - 1
        self.window = self.full + 2
        self.half = SUB // 2
        self.halves = SUB * nt * self.full
        self.wet = self.halves + self.half * nt
        self.p_rows = -(-(self.wet + self.half) // SUB) * SUB
        self.q_rows = (
            max(4 * lev, -(-(SUB + self.half) * nt // SUB) * SUB),
            max(4 * lev, 2 * SUB * nt),
        )

    def rs(self, comp):
        return list(range(1 - comp, self.window))

    def level(self, comp, r):
        return SUB * (r - 1) if comp == 0 else SUB * (self.full + r)

    def block(self, comp, second, p, q, j, r):
        if comp == 0:
            return p(SUB * (self.full * j + r - 1)) if r <= self.full else p(self.halves + self.half * j)
        if r < self.full:
            return p(SUB * (self.full * j + r))
        if second:
            return q(SUB * (2 * j + r - self.full))
        if r > self.full:
            return q(SUB * j)
        upper = p(self.halves + self.half * j)
        lower = q(SUB * self.nt + self.half * (j - 1))
        sub = lax.broadcasted_iota(jnp.int32, upper.shape, 0)
        return jnp.where(sub < self.half, upper, lower)


def rows_at(ref, base=0):
    return lambda offset: ref[base + offset : base + offset + SUB, :]


def edge_weights(eastward, northward):
    return [
        0.05 + 0.25 * jax.nn.sigmoid(eastward * math.cos(a) + northward * math.sin(a)) for a in ANGLES
    ]


def take_lanes(block, index):
    return jnp.take_along_axis(block, index, axis=1, mode="promise_in_bounds")


def shape_of(*dims):
    return jax.ShapeDtypeStruct(dims, F32)


def neighbours_of(nb_ref, odd):
    cols = nb_ref.shape[-1]
    core_side = jnp.where(odd == 1, 0, 2)
    index, in_core, in_cross = [], [], []
    for k in range(3):
        nb = jnp.broadcast_to(nb_ref[k : k + 1, :], (SUB, cols))
        side = nb // cols
        index.append(nb - side * cols)
        in_core.append(side == core_side)
        in_cross.append(side == 2 - core_side)
    return index, in_core, in_cross


def level_block(first, cols):
    return lax.broadcasted_iota(jnp.int32, (SUB, cols), 0).astype(F32) + float(first)


def link_weight(level, wet, mixing, last):
    nxt = level + 1.0
    return jnp.where((nxt < wet) & (nxt <= last), 0.02 + 0.13 * jax.nn.sigmoid(mixing), 0.0)


def wet_of(plan, ref):
    return jnp.broadcast_to(ref[plan.wet : plan.wet + 1, :], (SUB, ref.shape[1]))


def on_side(comp):
    return pl.when(lax.axis_index("comp") == comp)


def pack_kernel(plan, wet_ref, f_ref, t_ref, p_ref, q_ref, pq_ref, top_ref, chl_ref, wet_buf, half_buf, sems):
    nt, full, half, lev = plan.nt, plan.full, plan.half, plan.lev
    tall = SUB * full
    first = pl.multiple_of(lax.axis_index("comp") * tall, SUB)
    copies = [(wet_ref, wet_buf), (t_ref.at[:, pl.ds(pl.multiple_of(first + tall, SUB), SUB)], half_buf)]
    copies += [(t_ref.at[j, pl.ds(first, tall)], p_ref.at[pl.ds(tall * j, tall)]) for j in range(nt)]
    copies.append((t_ref.at[0], chl_ref))
    copies.append((f_ref.at[:, pl.ds(0, top_ref.shape[1])], top_ref))
    copies = [pltpu.make_async_copy(s, d, sems.at[i]) for i, (s, d) in enumerate(copies)]
    for c in copies:
        c.start()
    base = len(copies)
    ocean = [
        pltpu.make_async_copy(f_ref.at[i], q_ref.at[pl.ds(i * lev, lev)], sems.at[base + i]) for i in range(4)
    ]
    deep = [
        pltpu.make_async_copy(t_ref.at[j, pl.ds(lev - SUB, SUB)], q_ref.at[pl.ds(SUB * j, SUB)], sems.at[base + j])
        for j in range(nt)
    ]

    @on_side(0)
    def _():
        for c in ocean:
            c.start()

    @on_side(1)
    def _():
        for c in deep:
            c.start()

    for c in copies:
        c.wait()
    p_ref[plan.wet : plan.wet + half, :] = jnp.broadcast_to(wet_buf[...].astype(F32), (half, wet_buf.shape[1]))
    for j in range(nt):
        p_ref[plan.halves + half * j : plan.halves + half * (j + 1), :] = half_buf[j, 0:half, :]

    @on_side(0)
    def _():
        for c in ocean:
            c.wait()

    @on_side(1)
    def _():
        for c in deep:
            c.wait()
        for j in range(nt):
            at = SUB * nt + half * j
            q_ref[at : at + half, :] = half_buf[j, half:SUB, :]

    pq_ref[0 : plan.p_rows, :] = p_ref[...]
    pq_ref[plan.p_rows :, :] = q_ref[...]


def matrix_kernel(r_ref, out_ref):
    nt = r_ref.shape[0]
    rows, n = out_ref.shape
    p = lax.broadcasted_iota(jnp.int32, (n, nt), 0)
    spread = (p // SUB == lax.broadcasted_iota(jnp.int32, (n, nt), 1)).astype(F32)
    exact = functools.partial(
        lax.dot_general, precision=lax.Precision.HIGHEST, preferred_element_type=F32
    )
    tall = exact(spread, r_ref[...], (((1,), (0,)), ((), ())))
    full = exact(tall, spread, (((1,), (1,)), ((), ())))
    a = lax.broadcasted_iota(jnp.int32, (n, n), 0)
    b = lax.broadcasted_iota(jnp.int32, (n, n), 1)
    full = jnp.where(a % SUB == b % SUB, full, 0.0)
    high = full.astype(BF16)
    out_ref[0:n, :] = high
    out_ref[n:rows, :] = (full - high.astype(F32)).astype(BF16)


def near_kernel(plan, second, nb_ref, f_ref, ga_ref, gb_ref, pq_ref, core_ref, chl_ref, *refs):
    if second:
        chl_low_ref, *refs = refs
    part_ref, far_ref, aux_ref, opart_ref, ofar_ref, oaux_ref = refs[:6]
    chl_out_ref = refs[6] if second else None
    odd = lax.axis_index("tile") % 2
    cols = nb_ref.shape[-1]
    nt, p_rows = plan.nt, plan.p_rows
    index, in_core, in_cross = neighbours_of(nb_ref, odd)
    wet, wet_core = wet_of(plan, pq_ref), wet_of(plan, core_ref)
    near_wet = []
    for k in range(3):
        found = jnp.where(in_core[k], take_lanes(wet_core, index[k]), take_lanes(wet, index[k]))
        near_wet.append(jnp.where(in_cross[k], 0.0, found))
    last = float(plan.lev - 1)

    def split(level, ws):
        active = level < wet
        near = [jnp.where(active & (level < near_wet[k]), ws[k], 0.0) for k in range(3)]
        far = [jnp.where(active & in_cross[k], ws[k], 0.0) for k in range(3)]
        return near, far

    def moves(own, core, near, rest):
        totals = [o * r for o, r in zip(own, rest)]
        for k in range(3):
            for j in range(len(own)):
                v = jnp.where(in_core[k], take_lanes(core[j], index[k]), take_lanes(own[j], index[k]))
                totals[j] = totals[j] + near[j][k] * v
        return totals

    def tracers(comp):
        for r in plan.rs(comp):
            first = plan.level(comp, r)
            level = level_block(first, cols)
            g = [(gb_ref if comp else ga_ref)[i, first : first + SUB, :] for i in range(6)]
            near, far = split(level, edge_weights(g[2], g[3]))
            rest = 1.0 - (near[0] + near[1] + near[2])
            for k in range(3):
                far_ref[k, r] = far[k]
            aux_ref[0, r] = link_weight(level, wet, g[4], last)
            aux_ref[1, r] = 0.5 * g[5] * jax.nn.sigmoid(g[0] + 0.5 * g[1])
            own = [plan.block(comp, second, rows_at(pq_ref), rows_at(pq_ref, p_rows), j, r) for j in range(nt)]
            core = [plan.block(comp, second, rows_at(core_ref), rows_at(core_ref, p_rows), j, r) for j in range(nt)]
            for j, v in enumerate(moves(own, core, [near] * nt, [rest] * nt)):
                part_ref[j, r] = v

    @on_side(1)
    def _():
        tracers(1)

    @on_side(0)
    def _():
        tracers(0)
        top = f_ref[5, 0:1, :]
        cut = SUB * (plan.full + 1) - SUB + 2

        def chl_block(b):
            at = SUB * b
            if not second:
                return chl_ref[at : at + SUB, :]
            if b < plan.full:
                return chl_ref[at : at + SUB, :]
            v = chl_low_ref[0, at : at + SUB, :]
            if b > plan.full:
                return v
            return jnp.where(level_block(at, cols) < float(cut), chl_ref[plan.halves : plan.halves + SUB, :], v)

        run = jnp.zeros((1, cols), F32)
        for b in range(plan.blocks):
            x = chl_block(b)
            if second:
                chl_out_ref[SUB * b : SUB * (b + 1), :] = x
            absorbed = 0.01 + 0.3 * (jnp.maximum(x, 0.0) + jnp.log1p(jnp.exp(-jnp.abs(x))))
            level = level_block(SUB * b, cols)
            sub = lax.broadcasted_iota(jnp.int32, (SUB, cols), 0)
            cum = absorbed
            for d in (1, 2, 4):
                cum = cum + jnp.where(sub >= d, pltpu.roll(cum, d, 0), 0.0)
            depth = cum + run
            ceiling = jnp.exp(-(depth - absorbed))
            oaux_ref[1, b] = 4.0 * top * (ceiling - jnp.exp(-depth))
            oaux_ref[2, b] = jnp.where(level < wet, top * ceiling, 0.0)
            run = depth[SUB - 1 : SUB, :]

        for b in range(plan.blocks):
            at = SUB * b
            level = level_block(at, cols)
            f = [f_ref[i, at : at + SUB, :] for i in range(5)]
            near, far = split(level, edge_weights(f[2], f[3]))
            rest = 1.0 - (near[0] + near[1] + near[2])
            flat = [jnp.where(v > 0.0, 0.15, 0.0) for v in near]
            rest_flat = 1.0 - (flat[0] + flat[1] + flat[2])
            for k in range(3):
                ofar_ref[k, b] = far[k]
            oaux_ref[0, b] = link_weight(level, wet, f[4], last)
            core = [rows_at(core_ref, p_rows)(plan.lev * i + at) for i in range(4)]
            out = moves(f[:4], core, [near, near, flat, flat], [rest, rest, rest_flat, rest_flat])
            for i in range(4):
                opart_ref[i, b] = out[i]


def far_wet(index, in_cross, wet_cross):
    return [jnp.where(in_cross[k], take_lanes(wet_cross, index[k]), 0.0) for k in range(3)]


def far_moves(parts, own, cross, far, index):
    totals = [p - o * (f[0] + f[1] + f[2]) for p, o, f in zip(parts, own, far)]
    for k in range(3):
        for j in range(len(own)):
            totals[j] = totals[j] + far[j][k] * take_lanes(cross[j], index[k])
    return totals


class Far:
    def __init__(self, plan, comp, second, nb_ref, pq_ref, cross_p_ref, part_ref, far_ref, aux_ref, h_ref, l_ref):
        self.plan, self.comp, self.second = plan, comp, second
        self.cols = nb_ref.shape[-1]
        self.own_p, self.own_q = rows_at(pq_ref), rows_at(pq_ref, plan.p_rows)
        self.part, self.far, self.aux, self.h, self.l = part_ref, far_ref, aux_ref, h_ref, l_ref
        self.index, _, in_cross = neighbours_of(nb_ref, lax.axis_index("tile") % 2)
        self.wet = wet_of(plan, pq_ref)
        self.wets = far_wet(self.index, in_cross, wet_of(plan, cross_p_ref))

    def at(self, r):
        return SUB * (r + 1)

    def clear(self, before, after):
        zero = jnp.zeros((SUB, self.cols), F32)
        if before is not None:
            self.l[self.at(before) : self.at(before) + SUB, :] = zero
        for j in range(self.plan.nt):
            for r in (before, after):
                if r is not None:
                    self.h[j, self.at(r) : self.at(r) + SUB, :] = zero

    def move(self, r, p, q):
        plan, at = self.plan, self.at(r)
        level = level_block(plan.level(self.comp, r), self.cols)
        far = [jnp.where(level < self.wets[k], self.far[k, r], 0.0) for k in range(3)]
        self.l[at : at + SUB, :] = self.aux[0, r]
        js = range(plan.nt)
        parts = [self.part[j, r] for j in js]
        own = [plan.block(self.comp, self.second, self.own_p, self.own_q, j, r) for j in js]
        cross = [plan.block(self.comp, self.second, p, q, j, r) for j in js]
        for j, v in enumerate(far_moves(parts, own, cross, [far] * plan.nt, self.index)):
            self.h[j, at : at + SUB, :] = v

    def react(self, r, react_ref, put):
        plan, at = self.plan, self.at(r)
        active = (level_block(plan.level(self.comp, r), self.cols) < self.wet).astype(F32)
        down, up = self.l[at : at + SUB, :], self.l[at - 1 : at - 1 + SUB, :]
        ys, ts = [], []
        for j in range(plan.nt):
            v = self.h[j, at : at + SUB, :]
            y = v + down * (self.h[j, at + 1 : at + 1 + SUB, :] - v) - up * (v - self.h[j, at - 1 : at - 1 + SUB, :])
            ys.append(y)
            ts.append(jnp.tanh(y))
        growth = self.aux[1, r]
        if self.second:
            total = react_ref[0, 0] * ts[0]
            for j in range(1, plan.nt):
                total = total + react_ref[0, j] * ts[j]
            put(0, r, (ys[0] + growth * total) * active)
            return
        n = react_ref.shape[1]
        ts += [jnp.zeros_like(ts[0])] * (n // SUB - plan.nt)
        stack = jnp.concatenate(ts, axis=0)
        high = stack.astype(BF16)
        rest = (stack - high.astype(F32)).astype(BF16)
        both = jnp.dot(react_ref[...], high, preferred_element_type=F32)
        total = both[:n] + both[n:] + jnp.dot(react_ref[0:n, :], rest, preferred_element_type=F32)
        for i in range(plan.nt):
            put(i, r, (ys[i] + growth * total[i * SUB : (i + 1) * SUB]) * active)


def nothing(offset):
    raise ValueError("not there")


def upper_kernel(plan, react_ref, nb_ref, pq_ref, p_ref, part_ref, far_ref, aux_ref, out_ref, edge_ref, h_ref, l_ref):
    out_ref[plan.wet : plan.wet + plan.half, :] = pq_ref[plan.wet : plan.wet + plan.half, :]
    refs = (nb_ref, pq_ref, p_ref, part_ref, far_ref, aux_ref, h_ref, l_ref)
    p = rows_at(p_ref)

    @on_side(0)
    def _():
        work = Far(plan, 0, False, *refs)
        work.clear(0, plan.window)
        for r in plan.rs(0):
            work.move(r, p, nothing)

        def put(i, r, value):
            if r <= plan.full:
                at = SUB * (plan.full * i + r - 1)
                out_ref[at : at + SUB, :] = value
            else:
                at = plan.halves + plan.half * i
                out_ref[at : at + plan.half, :] = value[0 : plan.half]

        for r in plan.rs(0):
            work.react(r, react_ref, put)

    @on_side(1)
    def _():
        work = Far(plan, 1, False, *refs)
        work.clear(-1, None)
        lower = lambda offset: jnp.zeros((SUB, work.cols), F32)
        for r in range(plan.full + 1):
            work.move(r, p, lower)
        at = work.at(plan.full - 1)
        for j in range(plan.nt):
            edge_ref[j] = h_ref[j, at : at + SUB, :]

        def put(i, r, value):
            at = SUB * (plan.full * i + r)
            out_ref[at : at + SUB, :] = value

        for r in range(plan.full):
            work.react(r, react_ref, put)


def ocean_far(plan, nb_ref, f_ref, pq_ref, p_ref, q_ref, opart_ref, ofar_ref, oaux_ref, w_ref, l_ref, put):
    cols = nb_ref.shape[-1]
    index, _, in_cross = neighbours_of(nb_ref, lax.axis_index("tile") % 2)
    wet = wet_of(plan, pq_ref)
    wets = far_wet(index, in_cross, wet_of(plan, p_ref))
    zero = jnp.zeros((SUB, cols), F32)
    end = SUB * (plan.blocks + 1)
    l_ref[0:SUB, :] = zero
    for i in range(4):
        w_ref[i, 0:SUB, :] = zero
        w_ref[i, end : end + SUB, :] = zero
    for b in range(plan.blocks):
        at = SUB * b
        level = level_block(at, cols)
        far = [jnp.where(level < wets[k], ofar_ref[k, b], 0.0) for k in range(3)]
        flat = [jnp.where(v > 0.0, 0.15, 0.0) for v in far]
        there = slice(at + SUB, at + 2 * SUB)
        l_ref[there, :] = oaux_ref[0, b]
        parts = [opart_ref[i, b] for i in range(4)]
        own = [f_ref[i, at : at + SUB, :] for i in range(4)]
        cross = [rows_at(q_ref)(plan.lev * i + at) for i in range(4)]
        q = far_moves(parts, own, cross, [far, far, flat, flat], index)
        w_ref[0, there, :] = q[0]
        w_ref[1, there, :] = q[1]
        w_ref[2, there, :] = ROTATE_COS * q[2] + ROTATE_SIN * q[3]
        w_ref[3, there, :] = -ROTATE_SIN * q[2] + ROTATE_COS * q[3]
    warm = [None] * plan.blocks
    for b in range(plan.blocks):
        at = SUB * (b + 1)
        active = (level_block(SUB * b, cols) < wet).astype(F32)
        down, up = l_ref[at : at + SUB, :], l_ref[at - 1 : at - 1 + SUB, :]
        for i in range(4):
            v = w_ref[i, at : at + SUB, :]
            y = v + down * (w_ref[i, at + 1 : at + 1 + SUB, :] - v) - up * (v - w_ref[i, at - 1 : at - 1 + SUB, :])
            if i == 0:
                warm[b] = y + oaux_ref[1, b]
                put(0, b, warm[b] * active)
            else:
                put(i, b, y * active)
        put(5, b, oaux_ref[2, b])
    sub = lax.broadcasted_iota(jnp.int32, (SUB, cols), 0)
    for b in range(plan.blocks):
        active = (level_block(SUB * b, cols) < wet).astype(F32)
        lower = pltpu.roll(warm[b], SUB - 1, 0)
        if b + 1 < plan.blocks:
            lower = jnp.where(sub == SUB - 1, pltpu.roll(warm[b + 1], SUB - 1, 0), lower)
        else:
            lower = jnp.where(sub == SUB - 1, warm[b], lower)
        put(4, b, (warm[b] - lower) * active)


def lower_kernel(
    plan, react_ref, nb_ref, f_ref, pq_ref, p_ref, q_ref, part_ref, far_ref, aux_ref, opart_ref, ofar_ref, oaux_ref,
    done_ref, edge_ref, out_ref, both_ref, over_ref, h_ref, l_ref, w_ref, wl_ref,
):
    both_ref[0 : plan.p_rows, :] = done_ref[...]

    @on_side(0)
    def _():
        def put(i, b, value):
            at = SUB * b
            over_ref[i, at : at + SUB, :] = value
            if i < 4:
                for ref, base in ((out_ref, 0), (both_ref, plan.p_rows)):
                    ref[base + plan.lev * i + at : base + plan.lev * i + at + SUB, :] = value

        ocean_far(plan, nb_ref, f_ref, pq_ref, p_ref, q_ref, opart_ref, ofar_ref, oaux_ref, w_ref, wl_ref, put)

    @on_side(1)
    def _():
        work = Far(plan, 1, False, nb_ref, pq_ref, p_ref, part_ref, far_ref, aux_ref, h_ref, l_ref)
        work.clear(None, plan.window)
        before = work.at(plan.full - 1)
        l_ref[before : before + SUB, :] = aux_ref[0, plan.full - 1]
        for j in range(plan.nt):
            h_ref[j, before : before + SUB, :] = edge_ref[j]
        rs = (plan.full, plan.full + 1)
        for r in rs:
            work.move(r, rows_at(p_ref), rows_at(q_ref))

        def put(i, r, value):
            at = SUB * (2 * i + r - plan.full)
            out_ref[at : at + SUB, :] = value
            both_ref[plan.p_rows + at : plan.p_rows + at + SUB, :] = value
            if i == 0:
                over_ref[0, SUB * (plan.full + r) : SUB * (plan.full + r + 1), :] = value

        for r in rs:
            work.react(r, react_ref, put)
        for r in range(plan.full):
            over_ref[0, SUB * (plan.full + r) : SUB * (plan.full + r + 1), :] = done_ref[SUB * r : SUB * (r + 1), :]


def chl_kernel(plan, react_ref, nb_ref, pq_ref, p_ref, part_ref, far_ref, aux_ref, out_ref, h_ref, l_ref):
    @on_side(0)
    def _():
        work = Far(plan, 0, True, nb_ref, pq_ref, p_ref, part_ref, far_ref, aux_ref, h_ref, l_ref)
        work.clear(0, plan.window)
        for r in plan.rs(0):
            work.move(r, rows_at(p_ref), nothing)

        def put(i, r, value):
            out_ref[SUB * (r - 1) : SUB * r, :] = value

        for r in plan.rs(0):
            work.react(r, react_ref, put)


def last_kernel(
    plan, react_ref, nb_ref, f_ref, over_ref, pq_ref, p_ref, q_ref, part_ref, far_ref, aux_ref, opart_ref, ofar_ref,
    oaux_ref, chl_ref, upper_ref, out_ref, chl_out_ref, h_ref, l_ref, w_ref, wl_ref,
):
    @on_side(0)
    def _():
        def put(i, b, value):
            out_ref[i, SUB * b : SUB * (b + 1), :] = value

        chl_out_ref[...] = chl_ref[...]
        ocean_far(plan, nb_ref, f_ref, pq_ref, p_ref, q_ref, opart_ref, ofar_ref, oaux_ref, w_ref, wl_ref, put)

    @on_side(1)
    def _():
        out_ref[...] = over_ref[...]
        work = Far(plan, 1, True, nb_ref, pq_ref, p_ref, part_ref, far_ref, aux_ref, h_ref, l_ref)
        work.clear(-1, plan.window)
        for r in plan.rs(1):
            work.move(r, rows_at(p_ref), rows_at(q_ref))
        tall = SUB * plan.full
        chl_out_ref[0:tall, :] = upper_ref[0:tall, :]

        def put(i, r, value):
            at = tall + SUB * r
            if r == 0:
                sub = lax.broadcasted_iota(jnp.int32, value.shape, 0)
                value = jnp.where(sub < 2, upper_ref[at : at + SUB, :], value)
            chl_out_ref[at : at + SUB, :] = value

        for r in plan.rs(1):
            work.react(r, react_ref, put)


def call(kernel, outs, ins, specs=None, scratch=(), cost=1_000_000):
    return pl.pallas_call(
        kernel,
        out_shape=outs,
        in_specs=specs or [VMEM] * len(ins),
        out_specs=jax.tree.map(lambda _: VMEM, outs),
        scratch_shapes=list(scratch),
        compiler_params=pltpu.CompilerParams(vmem_limit_bytes=GRANT),
        cost_estimate=pl.CostEstimate(flops=cost, bytes_accessed=1_000_000, transcendentals=0),
    )(*ins)


def swaps(tiles, across):
    pairs = []
    for c in (0, 1):
        for t in range(tiles):
            other = (t + 1) % tiles if (t % 2 == 0) != across else (t - 1) % tiles
            pairs.append((c * tiles + t, c * tiles + other))
    return pairs


def over_comp(sources, tiles):
    return [(c * tiles + t, (1 - c) * tiles + t) for c in sources for t in range(tiles)]


def sent(v, pairs):
    return lax.ppermute(v, AXES, pairs)


def per_device(ocean_fields, tracers, reaction, wet_levels, neighbours):
    tiles = lax.axis_size("tile")
    nt, lev, cols = tracers.shape
    plan = Plan(nt, lev)
    blocks, window, p_rows = plan.blocks, plan.window, plan.p_rows
    fields = ocean_fields.reshape(-1, lev, cols)
    nf = fields.shape[0]
    top = SUB * (plan.full + 1)
    across, within = swaps(tiles, True), swaps(tiles, False)

    near_shapes = (
        shape_of(nt, window, SUB, cols),
        shape_of(3, window, SUB, cols),
        shape_of(2, window, SUB, cols),
        shape_of(4, blocks, SUB, cols),
        shape_of(3, blocks, SUB, cols),
        shape_of(3, blocks, SUB, cols),
    )
    h_scratch = (pltpu.VMEM((nt, (window + 2) * SUB, cols), F32), pltpu.VMEM(((window + 2) * SUB, cols), F32))
    w_scratch = (pltpu.VMEM((4, (blocks + 2) * SUB, cols), F32), pltpu.VMEM(((blocks + 2) * SUB, cols), F32))
    kernel = lambda f, *more: functools.partial(f, plan, *more)

    p, q, pq, top_fields, chl = call(
        kernel(pack_kernel),
        (
            shape_of(p_rows, cols),
            shape_of(plan.q_rows[0], cols),
            shape_of(p_rows + plan.q_rows[0], cols),
            shape_of(nf, top, cols),
            shape_of(lev, cols),
        ),
        tuple(
            pltpu.with_memory_space_constraint(v, pltpu.HBM) for v in (wet_levels.reshape(1, cols), fields, tracers)
        ),
        specs=[HBM] * 3,
        scratch=[
            pltpu.VMEM((1, cols), jnp.int32),
            pltpu.VMEM((nt, SUB, cols), F32),
            pltpu.SemaphoreType.DMA((2 * nt + 8,)),
        ],
    )
    cross_p = sent(p, across)
    lagged = sent(top_fields, over_comp((1,), tiles))
    core = sent(pq, within)
    cross_q = sent(q, across)
    n = -(-nt // 2) * 2 * SUB
    matrix = call(matrix_kernel, jax.ShapeDtypeStruct((2 * n, n), BF16), (reaction,))

    near = call(
        kernel(near_kernel, False),
        near_shapes,
        (neighbours, fields, lagged, fields, pq, core, chl),
        cost=8_000_000,
    )
    p_one, edge = call(
        kernel(upper_kernel),
        (shape_of(p_rows, cols), shape_of(nt, SUB, cols)),
        (matrix, neighbours, pq, cross_p, *near[:3]),
        scratch=h_scratch,
        cost=8_000_000,
    )
    cross_p_one = sent(p_one, across)
    q_one, pq_one, over_one = call(
        kernel(lower_kernel),
        (shape_of(plan.q_rows[1], cols), shape_of(p_rows + plan.q_rows[1], cols), shape_of(nf, lev, cols)),
        (matrix, neighbours, fields, pq, cross_p, cross_q, *near, p_one, edge),
        scratch=h_scratch + w_scratch,
        cost=8_000_000,
    )
    over = sent(over_one, over_comp((0, 1), tiles))
    core_one = sent(pq_one, within)
    cross_q_one = sent(q_one, across)

    *near, chl_one = call(
        kernel(near_kernel, True),
        near_shapes + (shape_of(lev, cols),),
        (neighbours, over_one, over_one, over, pq_one, core_one, p_one, over),
        cost=8_000_000,
    )
    upper = call(
        kernel(chl_kernel),
        shape_of(top, cols),
        (reaction, neighbours, pq_one, cross_p_one, *near[:3]),
        specs=[SMEM] + [VMEM] * 6,
        scratch=h_scratch,
        cost=8_000_000,
    )
    upper = sent(upper, over_comp((0,), tiles))
    ocean_out, chl_out = call(
        kernel(last_kernel),
        (shape_of(nf, lev, cols), shape_of(lev, cols)),
        (reaction, neighbours, over_one, over, pq_one, cross_p_one, cross_q_one, *near, chl_one, upper),
        specs=[SMEM] + [VMEM] * 14,
        scratch=h_scratch + w_scratch,
        cost=8_000_000,
    )
    return (ocean_out[None], chl_out[None])


def solution(mesh):
    return jax.shard_map(
        per_device,
        mesh=mesh,
        in_specs=(
            P("comp", None, None, "tile"),
            P(None, None, "tile"),
            P(),
            P("tile"),
            P(None, "tile"),
        ),
        out_specs=(P("comp", None, None, "tile"), P("comp", None, "tile")),
        check_vma=False,
    )
```

profile of v0, /device:TPU:0, one launch (start us, length us, event | category | flops | bytes accessed | tf_op | source)
XLA Modules:
  0.0 34.8 jit_solution(4033269483253083906)
XLA Ops:
  0.6 0.0 copy-start.1
  0.6 0.0 copy-start
  0.7 1.6 %shard_map.69 = (f32[536,128]{1,0:T(8,128)S(1)}, f32[256,128]{1,0:T(8,128)S(1)}, f32[792,128]{1,0:T(8,128)S(1)}, f32[6,32,128]{2,1,0:T(8,128)S(1)}, f32[64,128]{1,0:T(8,128)S(1)}) custom-call(s32[1,128]{1,0:T(1,128)} %bitcast.8, f32[6,64,128]{2,1,0:T(8,128)} %bitcast.4, f32[19,64,128]{2,1,0:T(8,128)} %t_ref.1), custom_call_target="tpu_custom_call" | custom-call | flops 1000000 | bytes 1000000 | tf_op jit(solution)/shard_map/pallas_call | solution.py:545
  2.3 0.6 %collective-permute-start.3 = (f32[792,128]{1,0:T(8,128)S(1)}, f32[792,128]{1,0:T(8,128)S(1)}, u32[]{:S(2)}, u32[]{:S(2)}) collective-permute-start(f32[792,128]{1,0:T(8,128)S(1)} %get-tuple-element.27.pq_ref), channel_id=1, source_target_pairs={{0,1},{1,0},{2,3},{3,2},{4,5},{5,4},{6,7},{7,6},{8,9},{9,8},{10,11... | collective-permute-start | bytes 1216520 | tf_op jit(solution)/shard_map/ppermute | solution.py:570
  2.8 5.7 %collective-permute-start = (f32[536,128]{1,0:T(8,128)S(1)}, f32[536,128]{1,0:T(8,128)S(1)}, u32[]{:S(2)}, u32[]{:S(2)}) collective-permute-start(f32[536,128]{1,0:T(8,128)S(1)} %get-tuple-element.28), channel_id=1, source_target_pairs={{0,15},{1,2},{2,1},{3,4},{4,3},{5,6},{6,5},{7,8},{8,7},{9,10},{10,... | collective-permute-start | bytes 823304 | tf_op jit(solution)/shard_map/ppermute | solution.py:570
  8.5 0.0 collective-permute-start.1
  8.5 1.3 %collective-permute-start.2 = (f32[6,32,128]{2,1,0:T(8,128)S(1)}, f32[6,32,128]{2,1,0:T(8,128)S(1)}, u32[]{:S(2)}, u32[]{:S(2)}) collective-permute-start(f32[6,32,128]{2,1,0:T(8,128)S(1)} %get-tuple-element.30), channel_id=1, source_target_pairs={{16,0},{17,1},{18,2},{19,3},{20,4},{21,5},{22,6},{23,7},{24,8},{25... | collective-permute-start | bytes 294920 | tf_op jit(solution)/shard_map/ppermute | solution.py:570
  9.8 0.0 copy-done.1
  9.8 0.0 copy-start.2
  9.8 0.6 %shard_map.68.react_ref = bf16[320,160]{1,0:T(8,128)(2,1)S(1)} custom-call(f32[19,19]{1,0:T(8,128)S(1)} %copy-done.1), custom_call_target="tpu_custom_call" | custom-call | flops 1000000 | bytes 1000000 | tf_op jit(solution)/shard_map/pallas_call | solution.py:545
  10.4 4.6 %collective-permute-done.2.ga_ref = f32[6,32,128]{2,1,0:T(8,128)S(1)} collective-permute-done((f32[6,32,128]{2,1,0:T(8,128)S(1)}, f32[6,32,128]{2,1,0:T(8,128)S(1)}, u32[]{:S(2)}, u32[]{:S(2)}) %collective-permute-start.2) | collective-permute-done | bytes 98336 | tf_op jit(solution)/shard_map/ppermute | solution.py:570
  15.0 0.0 collective-permute-done.3.core_ref
  15.0 0.0 copy-done
  15.0 0.0 copy-done.2
  15.0 1.0 %shard_map.70 = (f32[19,5,8,128]{3,2,1,0:T(8,128)S(1)}, f32[3,5,8,128]{3,2,1,0:T(8,128)S(1)}, f32[2,5,8,128]{3,2,1,0:T(8,128)S(1)}, f32[4,8,8,128]{3,2,1,0:T(8,1...) custom-call(s32[3,128]{1,0:T(4,128)S(1)} %copy-done.2, f32[6,64,128]{2,1,0:T(8,128)S(1)} %bitcast.5, ...), custom_call_target="tpu_custom_call" | custom-call | flops 8000000 | bytes 1000000 | tf_op jit(solution)/shard_map/pallas_call | solution.py:545
  16.0 0.0 collective-permute-done.p_ref
  16.0 1.0 %shard_map.71 = (f32[536,128]{1,0:T(8,128)S(1)}, f32[19,8,128]{2,1,0:T(8,128)S(1)}) custom-call(bf16[320,160]{1,0:T(8,128)(2,1)S(1)} %shard_map.68.react_ref, s32[3,128]{1,0:T(4,128)S(1)} %copy-done.2, f32[792,128]{1,0:T(8,128)S(1)} %get-tuple-element.27.pq_ref, f32[536,128]{1,0:T(8,128)S(1)} %collective-permute-done.p_ref, ...), custom_call_target="tpu_custom_call" | custom-call | flops 8000000 | bytes 1000000 | tf_op jit(solution)/shard_map/pallas_call | solution.py:545
  17.0 0.0 collective-permute-done.1.q_ref
  17.0 0.3 shard_map.72
  17.3 0.1 collective-permute-start.7
  17.4 3.6 %collective-permute-start.5 = (f32[536,128]{1,0:T(8,128)S(1)}, f32[536,128]{1,0:T(8,128)S(1)}, u32[]{:S(2)}, u32[]{:S(2)}) collective-permute-start(f32[536,128]{1,0:T(8,128)S(1)} %get-tuple-element.38.done_ref.chl_ref), channel_id=1, source_target_pairs={{0,15},{1,2},{2,1},{3,4},{4,3},{5,6},{6,5},{7,8},{8,7},{9,10},{10,... | collective-permute-start | bytes 823304 | tf_op jit(solution)/shard_map/ppermute | solution.py:570
  21.0 1.4 %collective-permute-start.4 = (f32[6,64,128]{2,1,0:T(8,128)S(1)}, f32[6,64,128]{2,1,0:T(8,128)S(1)}, u32[]{:S(2)}, u32[]{:S(2)}) collective-permute-start(f32[6,64,128]{2,1,0:T(8,128)S(1)} %get-tuple-element.40.f_ref.ga_ref), channel_id=1, source_target_pairs={{0,16},{1,17},{2,18},{3,19},{4,20},{5,21},{6,22},{7,23},{8,24},{9,... | collective-permute-start | bytes 589832 | tf_op jit(solution)/shard_map/ppermute | solution.py:570
  22.5 0.0 collective-permute-start.6
  22.5 4.2 %collective-permute-done.4.gb_ref.refs_0_.over_ref = f32[6,64,128]{2,1,0:T(8,128)S(1)} collective-permute-done((f32[6,64,128]{2,1,0:T(8,128)S(1)}, f32[6,64,128]{2,1,0:T(8,128)S(1)}, u32[]{:S(2)}, u32[]{:S(2)}) %collective-permute-start.4) | collective-permute-done | bytes 196640 | tf_op jit(solution)/shard_map/ppermute | solution.py:570
  26.7 0.0 collective-permute-done.7.core_ref
  26.7 1.0 %shard_map.73 = (f32[19,5,8,128]{3,2,1,0:T(8,128)S(1)}, f32[3,5,8,128]{3,2,1,0:T(8,128)S(1)}, f32[2,5,8,128]{3,2,1,0:T(8,128)S(1)}, f32[4,8,8,128]{3,2,1,0:T(8,1...) custom-call(s32[3,128]{1,0:T(4,128)S(1)} %copy-done.2, ...), custom_call_target="tpu_custom_call" | custom-call | flops 8000000 | bytes 1000000 | tf_op jit(solution)/shard_map/pallas_call | solution.py:545
  27.7 0.0 collective-permute-done.5.p_ref
  27.7 1.2 %shard_map.74 = f32[32,128]{1,0:T(8,128)S(1)} custom-call(f32[19,19]{1,0:T(8,128)S(1)} %copy-done.1, s32[3,128]{1,0:T(4,128)S(1)} %copy-done.2, f32[840,128]{1,0:T(8,128)S(1)} %get-tuple-element.41.pq_ref, f32[536,128]{1,0:T(8,128)S(1)} %collective-permute-done.5.p_ref, f32[19,5,8,128]{3,2,1,0:T(8,128)S(1)} %get-tuple-element.43.part_ref, ...), custom_call_target="tpu_custom_call" | custom-call | flops 8000000 | bytes 1000000 | tf_op jit(solution)/shard_map/pallas_call | solution.py:545
  28.9 2.8 %collective-permute-start.8 = (f32[32,128]{1,0:T(8,128)S(1)}, f32[32,128]{1,0:T(8,128)S(1)}, u32[]{:S(2)}, u32[]{:S(2)}) collective-permute-start(f32[32,128]{1,0:T(8,128)S(1)} %shard_map.74), channel_id=1, source_target_pairs={{0,16},{1,17},{2,18},{3,19},{4,20},{5,21},{6,22},{7,23},{8,24},{9,... | collective-permute-start | bytes 49160 | tf_op jit(solution)/shard_map/ppermute | solution.py:570
  31.7 0.0 collective-permute-done.6.q_ref
  31.7 1.4 %collective-permute-done.8.upper_ref = f32[32,128]{1,0:T(8,128)S(1)} collective-permute-done((f32[32,128]{1,0:T(8,128)S(1)}, f32[32,128]{1,0:T(8,128)S(1)}, u32[]{:S(2)}, u32[]{:S(2)}) %collective-permute-start.8) | collective-permute-done | bytes 16416 | tf_op jit(solution)/shard_map/ppermute | solution.py:570
  33.1 1.7 %shard_map.75 = (f32[6,64,128]{2,1,0:T(8,128)}, f32[64,128]{1,0:T(8,128)}) custom-call(f32[19,19]{1,0:T(8,128)S(1)} %copy-done.1, s32[3,128]{1,0:T(4,128)S(1)} %copy-done.2, f32[6,64,128]{2,1,0:T(8,128)S(1)} %get-tuple-element.40.f_ref.ga_ref, f32[6,64,128]{2,1,0:T(8,128)S(1)} %collective-permute-done.4.gb_ref.refs_0_.over_ref, ...), custom_call_target="tpu_custom_call" | custom-call | flops 8000000 | bytes 1000000 | tf_op jit(solution)/shard_map/pallas_call | solution.py:545
Async XLA Ops:
  0.6 9.2 %copy-start.1 = (f32[19,19]{1,0:T(8,128)S(1)}, f32[19,19]{1,0:T(8,128)}, u32[]{:S(2)}) copy-start(f32[19,19]{1,0:T(8,128)} %react_ref.3) | copy-start | bytes 4336
  0.6 14.4 %copy-start = (f32[1,6,64,128]{3,2,1,0:T(8,128)S(1)}, f32[1,6,64,128]{3,2,1,0:T(8,128)}, u32[]{:S(2)}) copy-start(f32[1,6,64,128]{3,2,1,0:T(8,128)} %param.5) | copy-start | bytes 589828
  2.3 12.8 %collective-permute-start.3 = (f32[792,128]{1,0:T(8,128)S(1)}, f32[792,128]{1,0:T(8,128)S(1)}, u32[]{:S(2)}, u32[]{:S(2)}) collective-permute-start(f32[792,128]{1,0:T(8,128)S(1)} %get-tuple-element.27.pq_ref), channel_id=1, source_target_pairs={{0,1},{1,0},{2,3},{3,2},{4,5},{5,4},{6,7},{7,6},{8,9},{9,8},{10,11... | collective-permute-start | bytes 1216520 | tf_op jit(solution)/shard_map/ppermute | solution.py:570
  2.8 13.2 %collective-permute-start = (f32[536,128]{1,0:T(8,128)S(1)}, f32[536,128]{1,0:T(8,128)S(1)}, u32[]{:S(2)}, u32[]{:S(2)}) collective-permute-start(f32[536,128]{1,0:T(8,128)S(1)} %get-tuple-element.28), channel_id=1, source_target_pairs={{0,15},{1,2},{2,1},{3,4},{4,3},{5,6},{6,5},{7,8},{8,7},{9,10},{10,... | collective-permute-start | bytes 823304 | tf_op jit(solution)/shard_map/ppermute | solution.py:570
  8.5 8.5 %collective-permute-start.1 = (f32[256,128]{1,0:T(8,128)S(1)}, f32[256,128]{1,0:T(8,128)S(1)}, u32[]{:S(2)}, u32[]{:S(2)}) collective-permute-start(f32[256,128]{1,0:T(8,128)S(1)} %get-tuple-element.29), channel_id=1, source_target_pairs={{0,15},{1,2},{2,1},{3,4},{4,3},{5,6},{6,5},{7,8},{8,7},{9,10},{10,... | collective-permute-start | bytes 393224 | tf_op jit(solution)/shard_map/ppermute | solution.py:570
  8.5 6.5 %collective-permute-start.2 = (f32[6,32,128]{2,1,0:T(8,128)S(1)}, f32[6,32,128]{2,1,0:T(8,128)S(1)}, u32[]{:S(2)}, u32[]{:S(2)}) collective-permute-start(f32[6,32,128]{2,1,0:T(8,128)S(1)} %get-tuple-element.30), channel_id=1, source_target_pairs={{16,0},{17,1},{18,2},{19,3},{20,4},{21,5},{22,6},{23,7},{24,8},{25... | collective-permute-start | bytes 294920 | tf_op jit(solution)/shard_map/ppermute | solution.py:570
  9.8 5.2 %copy-start.2 = (s32[3,128]{1,0:T(4,128)S(1)}, s32[3,128]{1,0:T(4,128)}, u32[]{:S(2)}) copy-start(s32[3,128]{1,0:T(4,128)} %nb_ref.11) | copy-start | bytes 4612
  17.3 9.4 %collective-permute-start.7 = (f32[840,128]{1,0:T(8,128)S(1)}, f32[840,128]{1,0:T(8,128)S(1)}, u32[]{:S(2)}, u32[]{:S(2)}) collective-permute-start(f32[840,128]{1,0:T(8,128)S(1)} %get-tuple-element.41.pq_ref), channel_id=1, source_target_pairs={{0,1},{1,0},{2,3},{3,2},{4,5},{5,4},{6,7},{7,6},{8,9},{9,8},{10,11... | collective-permute-start | bytes 1290248 | tf_op jit(solution)/shard_map/ppermute | solution.py:570
  17.4 10.3 %collective-permute-start.5 = (f32[536,128]{1,0:T(8,128)S(1)}, f32[536,128]{1,0:T(8,128)S(1)}, u32[]{:S(2)}, u32[]{:S(2)}) collective-permute-start(f32[536,128]{1,0:T(8,128)S(1)} %get-tuple-element.38.done_ref.chl_ref), channel_id=1, source_target_pairs={{0,15},{1,2},{2,1},{3,4},{4,3},{5,6},{6,5},{7,8},{8,7},{9,10},{10,... | collective-permute-start | bytes 823304 | tf_op jit(solution)/shard_map/ppermute | solution.py:570
  21.0 5.7 %collective-permute-start.4 = (f32[6,64,128]{2,1,0:T(8,128)S(1)}, f32[6,64,128]{2,1,0:T(8,128)S(1)}, u32[]{:S(2)}, u32[]{:S(2)}) collective-permute-start(f32[6,64,128]{2,1,0:T(8,128)S(1)} %get-tuple-element.40.f_ref.ga_ref), channel_id=1, source_target_pairs={{0,16},{1,17},{2,18},{3,19},{4,20},{5,21},{6,22},{7,23},{8,24},{9,... | collective-permute-start | bytes 589832 | tf_op jit(solution)/shard_map/ppermute | solution.py:570
  22.5 9.2 %collective-permute-start.6 = (f32[304,128]{1,0:T(8,128)S(1)}, f32[304,128]{1,0:T(8,128)S(1)}, u32[]{:S(2)}, u32[]{:S(2)}) collective-permute-start(f32[304,128]{1,0:T(8,128)S(1)} %get-tuple-element.42), channel_id=1, source_target_pairs={{0,15},{1,2},{2,1},{3,4},{4,3},{5,6},{6,5},{7,8},{8,7},{9,10},{10,... | collective-permute-start | bytes 466952 | tf_op jit(solution)/shard_map/ppermute | solution.py:570
  28.9 4.2 %collective-permute-start.8 = (f32[32,128]{1,0:T(8,128)S(1)}, f32[32,128]{1,0:T(8,128)S(1)}, u32[]{:S(2)}, u32[]{:S(2)}) collective-permute-start(f32[32,128]{1,0:T(8,128)S(1)} %shard_map.74), channel_id=1, source_target_pairs={{0,16},{1,17},{2,18},{3,19},{4,20},{5,21},{6,22},{7,23},{8,24},{9,... | collective-permute-start | bytes 49160 | tf_op jit(solution)/shard_map/ppermute | solution.py:570
where the time goes:
time: 35 us; the launch traced here: 34.8 us
  starting transfers between devices  15.4 us (44%)
  waiting for transfers between devices  10.3 us (29%)
  Pallas kernels  8.35 us (24%)
  between operations  0.77 us (2%)
    ppermute x9, starting transfers between devices, sent(): return lax.ppermute(v, AXES, pairs)  15.4 us
    ppermute x9, waiting for transfers between devices, sent(): return lax.ppermute(v, AXES, pairs)  10.3 us
    pallas_call x8, Pallas kernels, call(): pl.pallas_call(kernel, out_shape=outs, in_specs=specs or [VMEM] * len(ins...  8.35 us
  transfers between devices with their start and end apart: 9, of which 3 were waited for; matrix products, arithmetic and copies ran while one was open for 0% of the time, Pallas kernels for 13%

commit v1 on v0

--- a/solution.py
+++ b/solution.py
@@ -112,21 +112,20 @@
     nt, full, half, lev = plan.nt, plan.full, plan.half, plan.lev
     tall = SUB * full
     first = pl.multiple_of(lax.axis_index("comp") * tall, SUB)
-    copies = [(wet_ref, wet_buf), (t_ref.at[:, pl.ds(pl.multiple_of(first + tall, SUB), SUB)], half_buf)]
-    copies += [(t_ref.at[j, pl.ds(first, tall)], p_ref.at[pl.ds(tall * j, tall)]) for j in range(nt)]
-    copies.append((t_ref.at[0], chl_ref))
-    copies.append((f_ref.at[:, pl.ds(0, top_ref.shape[1])], top_ref))
+    copies = [
+        (t_ref.at[:, pl.ds(first, tall)], p_ref.at[pl.ds(0, plan.halves)].reshape(nt, tall, p_ref.shape[1])),
+        (t_ref.at[:, pl.ds(pl.multiple_of(first + tall, SUB), SUB)], half_buf),
+        (wet_ref, wet_buf),
+        (f_ref.at[:, pl.ds(0, top_ref.shape[1])], top_ref),
+        (t_ref.at[0], chl_ref),
+    ]
     copies = [pltpu.make_async_copy(s, d, sems.at[i]) for i, (s, d) in enumerate(copies)]
     for c in copies:
         c.start()
     base = len(copies)
-    ocean = [
-        pltpu.make_async_copy(f_ref.at[i], q_ref.at[pl.ds(i * lev, lev)], sems.at[base + i]) for i in range(4)
-    ]
-    deep = [
-        pltpu.make_async_copy(t_ref.at[j, pl.ds(lev - SUB, SUB)], q_ref.at[pl.ds(SUB * j, SUB)], sems.at[base + j])
-        for j in range(nt)
-    ]
+    slab = lambda n, rows: q_ref.at[pl.ds(0, n * rows)].reshape(n, rows, q_ref.shape[1])
+    ocean = [pltpu.make_async_copy(f_ref.at[pl.ds(0, 4)], slab(4, lev), sems.at[base])]
+    deep = [pltpu.make_async_copy(t_ref.at[:, pl.ds(lev - SUB, SUB)], slab(nt, SUB), sems.at[base])]
 
     @on_side(0)
     def _():
@@ -161,7 +160,7 @@
     pq_ref[plan.p_rows :, :] = q_ref[...]
 
 
-def matrix_kernel(r_ref, out_ref):
+def matrix_kernel(r_ref, out_ref, first_ref):
     nt = r_ref.shape[0]
     rows, n = out_ref.shape
     p = lax.broadcasted_iota(jnp.int32, (n, nt), 0)
@@ -177,6 +176,8 @@
     high = full.astype(BF16)
     out_ref[0:n, :] = high
     out_ref[n:rows, :] = (full - high.astype(F32)).astype(BF16)
+    ones = jnp.ones((1, first_ref.shape[1]), F32)
+    first_ref[...] = exact(r_ref[0:1, :], ones, (((0,), (0,)), ((), ())))
 
 
 def near_kernel(plan, second, nb_ref, f_ref, ga_ref, gb_ref, pq_ref, core_ref, chl_ref, *refs):
@@ -213,7 +214,8 @@
         for r in plan.rs(comp):
             first = plan.level(comp, r)
             level = level_block(first, cols)
-            g = [(gb_ref if comp else ga_ref)[i, first : first + SUB, :] for i in range(6)]
+            g_first = first - SUB * plan.full if comp and second else first
+            g = [(gb_ref if comp else ga_ref)[i, g_first : g_first + SUB, :] for i in range(6)]
             near, far = split(level, edge_weights(g[2], g[3]))
             rest = 1.0 - (near[0] + near[1] + near[2])
             for k in range(3):
@@ -241,7 +243,7 @@
                 return chl_ref[at : at + SUB, :]
             if b < plan.full:
                 return chl_ref[at : at + SUB, :]
-            v = chl_low_ref[0, at : at + SUB, :]
+            v = chl_low_ref[0, at - SUB * plan.full : at - SUB * plan.full + SUB, :]
             if b > plan.full:
                 return v
             return jnp.where(level_block(at, cols) < float(cut), chl_ref[plan.halves : plan.halves + SUB, :], v)
@@ -338,9 +340,9 @@
             ts.append(jnp.tanh(y))
         growth = self.aux[1, r]
         if self.second:
-            total = react_ref[0, 0] * ts[0]
+            total = react_ref[0:1, :] * ts[0]
             for j in range(1, plan.nt):
-                total = total + react_ref[0, j] * ts[j]
+                total = total + react_ref[j : j + 1, :] * ts[j]
             put(0, r, (ys[0] + growth * total) * active)
             return
         n = react_ref.shape[1]
@@ -453,7 +455,7 @@
 
 def lower_kernel(
     plan, react_ref, nb_ref, f_ref, pq_ref, p_ref, q_ref, part_ref, far_ref, aux_ref, opart_ref, ofar_ref, oaux_ref,
-    done_ref, edge_ref, out_ref, both_ref, over_ref, h_ref, l_ref, w_ref, wl_ref,
+    done_ref, edge_ref, out_ref, both_ref, ocean_ref, over_ref, rest_ref, h_ref, l_ref, w_ref, wl_ref,
 ):
     both_ref[0 : plan.p_rows, :] = done_ref[...]
 
@@ -461,7 +463,11 @@
     def _():
         def put(i, b, value):
             at = SUB * b
-            over_ref[i, at : at + SUB, :] = value
+            ocean_ref[i, at : at + SUB, :] = value
+            if b < plan.full:
+                rest_ref[i, at : at + SUB, :] = value
+            else:
+                over_ref[i, at - SUB * plan.full : at - SUB * plan.full + SUB, :] = value
             if i < 4:
                 for ref, base in ((out_ref, 0), (both_ref, plan.p_rows)):
                     ref[base + plan.lev * i + at : base + plan.lev * i + at + SUB, :] = value
@@ -485,12 +491,12 @@
             out_ref[at : at + SUB, :] = value
             both_ref[plan.p_rows + at : plan.p_rows + at + SUB, :] = value
             if i == 0:
-                over_ref[0, SUB * (plan.full + r) : SUB * (plan.full + r + 1), :] = value
+                over_ref[0, SUB * r : SUB * (r + 1), :] = value
 
         for r in rs:
             work.react(r, react_ref, put)
         for r in range(plan.full):
-            over_ref[0, SUB * (plan.full + r) : SUB * (plan.full + r + 1), :] = done_ref[SUB * r : SUB * (r + 1), :]
+            over_ref[0, SUB * r : SUB * (r + 1), :] = done_ref[SUB * r : SUB * (r + 1), :]
 
 
 def chl_kernel(plan, react_ref, nb_ref, pq_ref, p_ref, part_ref, far_ref, aux_ref, out_ref, h_ref, l_ref):
@@ -508,37 +514,46 @@
             work.react(r, react_ref, put)
 
 
-def last_kernel(
-    plan, react_ref, nb_ref, f_ref, over_ref, pq_ref, p_ref, q_ref, part_ref, far_ref, aux_ref, opart_ref, ofar_ref,
-    oaux_ref, chl_ref, upper_ref, out_ref, chl_out_ref, h_ref, l_ref, w_ref, wl_ref,
+def second_kernel(
+    plan, react_ref, nb_ref, f_ref, over_ref, rest_ref, pq_ref, p_ref, q_ref, part_ref, far_ref, aux_ref, opart_ref,
+    ofar_ref, oaux_ref, out_ref, mine_ref, h_ref, l_ref, w_ref, wl_ref,
 ):
     @on_side(0)
     def _():
         def put(i, b, value):
             out_ref[i, SUB * b : SUB * (b + 1), :] = value
 
-        chl_out_ref[...] = chl_ref[...]
         ocean_far(plan, nb_ref, f_ref, pq_ref, p_ref, q_ref, opart_ref, ofar_ref, oaux_ref, w_ref, wl_ref, put)
 
     @on_side(1)
     def _():
-        out_ref[...] = over_ref[...]
+        tall = SUB * plan.full
+        out_ref[:, 0:tall, :] = rest_ref[...]
+        out_ref[:, tall:, :] = over_ref[...]
         work = Far(plan, 1, True, nb_ref, pq_ref, p_ref, part_ref, far_ref, aux_ref, h_ref, l_ref)
         work.clear(-1, plan.window)
         for r in plan.rs(1):
             work.move(r, rows_at(p_ref), rows_at(q_ref))
-        tall = SUB * plan.full
-        chl_out_ref[0:tall, :] = upper_ref[0:tall, :]
 
         def put(i, r, value):
-            at = tall + SUB * r
-            if r == 0:
-                sub = lax.broadcasted_iota(jnp.int32, value.shape, 0)
-                value = jnp.where(sub < 2, upper_ref[at : at + SUB, :], value)
-            chl_out_ref[at : at + SUB, :] = value
+            mine_ref[SUB * r : SUB * (r + 1), :] = value
 
         for r in plan.rs(1):
             work.react(r, react_ref, put)
+
+
+def merge_kernel(plan, chl_ref, mine_ref, upper_ref, out_ref):
+    @on_side(0)
+    def _():
+        out_ref[...] = chl_ref[...]
+
+    @on_side(1)
+    def _():
+        tall = SUB * plan.full
+        sub = lax.broadcasted_iota(jnp.int32, (SUB, out_ref.shape[1]), 0)
+        out_ref[0:tall, :] = upper_ref[0:tall, :]
+        out_ref[tall : tall + SUB, :] = jnp.where(sub < 2, upper_ref[tall : tall + SUB, :], mine_ref[0:SUB, :])
+        out_ref[tall + SUB :, :] = mine_ref[SUB:, :]
 
 
 def call(kernel, outs, ins, specs=None, scratch=(), cost=1_000_000):
@@ -577,7 +592,7 @@
     blocks, window, p_rows = plan.blocks, plan.window, plan.p_rows
     fields = ocean_fields.reshape(-1, lev, cols)
     nf = fields.shape[0]
-    top = SUB * (plan.full + 1)
+    top, tall = SUB * (plan.full + 1), SUB * plan.full
     across, within = swaps(tiles, True), swaps(tiles, False)
 
     near_shapes = (
@@ -608,7 +623,7 @@
         scratch=[
             pltpu.VMEM((1, cols), jnp.int32),
             pltpu.VMEM((nt, SUB, cols), F32),
-            pltpu.SemaphoreType.DMA((2 * nt + 8,)),
+            pltpu.SemaphoreType.DMA((6,)),
         ],
     )
     cross_p = sent(p, across)
@@ -616,7 +631,9 @@
     core = sent(pq, within)
     cross_q = sent(q, across)
     n = -(-nt // 2) * 2 * SUB
-    matrix = call(matrix_kernel, jax.ShapeDtypeStruct((2 * n, n), BF16), (reaction,))
+    matrix, rates = call(
+        matrix_kernel, (jax.ShapeDtypeStruct((2 * n, n), BF16), shape_of(nt, cols)), (reaction,)
+    )
 
     near = call(
         kernel(near_kernel, False),
@@ -632,9 +649,15 @@
         cost=8_000_000,
     )
     cross_p_one = sent(p_one, across)
-    q_one, pq_one, over_one = call(
+    q_one, pq_one, ocean_one, over_one, rest_one = call(
         kernel(lower_kernel),
-        (shape_of(plan.q_rows[1], cols), shape_of(p_rows + plan.q_rows[1], cols), shape_of(nf, lev, cols)),
+        (
+            shape_of(plan.q_rows[1], cols),
+            shape_of(p_rows + plan.q_rows[1], cols),
+            shape_of(nf, lev, cols),
+            shape_of(nf, lev - tall, cols),
+            shape_of(nf, tall, cols),
+        ),
         (matrix, neighbours, fields, pq, cross_p, cross_q, *near, p_one, edge),
         scratch=h_scratch + w_scratch,
         cost=8_000_000,
@@ -642,30 +665,30 @@
     over = sent(over_one, over_comp((0, 1), tiles))
     core_one = sent(pq_one, within)
     cross_q_one = sent(q_one, across)
+    rest = sent(rest_one, over_comp((0,), tiles))
 
     *near, chl_one = call(
         kernel(near_kernel, True),
         near_shapes + (shape_of(lev, cols),),
-        (neighbours, over_one, over_one, over, pq_one, core_one, p_one, over),
+        (neighbours, ocean_one, ocean_one, over, pq_one, core_one, p_one, over),
         cost=8_000_000,
     )
     upper = call(
         kernel(chl_kernel),
         shape_of(top, cols),
-        (reaction, neighbours, pq_one, cross_p_one, *near[:3]),
-        specs=[SMEM] + [VMEM] * 6,
+        (rates, neighbours, pq_one, cross_p_one, *near[:3]),
         scratch=h_scratch,
         cost=8_000_000,
     )
     upper = sent(upper, over_comp((0,), tiles))
-    ocean_out, chl_out = call(
-        kernel(last_kernel),
-        (shape_of(nf, lev, cols), shape_of(lev, cols)),
-        (reaction, neighbours, over_one, over, pq_one, cross_p_one, cross_q_one, *near, chl_one, upper),
-        specs=[SMEM] + [VMEM] * 14,
+    ocean_out, mine = call(
+        kernel(second_kernel),
+        (shape_of(nf, lev, cols), shape_of(lev - tall, cols)),
+        (rates, neighbours, ocean_one, over, rest, pq_one, cross_p_one, cross_q_one, *near),
         scratch=h_scratch + w_scratch,
         cost=8_000_000,
     )
+    chl_out = call(kernel(merge_kernel), shape_of(lev, cols), (chl_one, mine, upper))
     return (ocean_out[None], chl_out[None])
 
 

time: 35 us -> 32.7 us (0.934)
  waiting for transfers between devices: 10.3 us -> 5.97 us
  starting transfers between devices: 15.4 us -> 18.5 us
  Pallas kernels: 8.35 us -> 7.2 us
    ppermute x9 -> x10, waiting for transfers between devices: 10.3 us -> 5.97 us  [sent(): return lax.ppermute(v, AXES, pairs)]
    ppermute x9 -> x10, starting transfers between devices: 15.4 us -> 18.5 us  [sent(): return lax.ppermute(v, AXES, pairs)]
    pallas_call x8 -> x9, Pallas kernels: 8.35 us -> 7.2 us  [call(): pl.pallas_call(kernel, out_shape=outs, in_specs=specs or [VMEM] * len(ins...]
  transfers between devices with their start and end apart: 9 -> 10, of which waited for: 3 -> 3; matrix products, arithmetic and copies ran while one was open for 0% -> 0% of each run, Pallas kernels for 13% -> 15%
where the time goes in v1:
time: 32.7 us; the launch traced here: 32.5 us
  starting transfers between devices  18.5 us (57%)
  Pallas kernels  7.2 us (22%)
  waiting for transfers between devices  5.97 us (18%)
  between operations  0.79 us (2%)
    ppermute x10, starting transfers between devices, sent(): return lax.ppermute(v, AXES, pairs)  18.5 us
    pallas_call x9, Pallas kernels, call(): pl.pallas_call(kernel, out_shape=outs, in_specs=specs or [VMEM] * len(ins...  7.2 us
    ppermute x10, waiting for transfers between devices, sent(): return lax.ppermute(v, AXES, pairs)  5.97 us
  transfers between devices with their start and end apart: 10, of which 3 were waited for; matrix products, arithmetic and copies ran while one was open for 0% of the time, Pallas kernels for 15%

profile of v1, /device:TPU:0, one launch (start us, length us, event | category | flops | bytes accessed | tf_op | source)
XLA Modules:
  0.0 32.5 jit_solution(9935873511555161528)
XLA Ops:
  0.6 0.0 copy-start.2
  0.7 1.3 %shard_map.69 = (f32[536,128]{1,0:T(8,128)S(1)}, f32[256,128]{1,0:T(8,128)S(1)}, f32[792,128]{1,0:T(8,128)S(1)}, f32[6,32,128]{2,1,0:T(8,128)S(1)}, f32[64,128]{1,0:T(8,128)S(1)}) custom-call(s32[1,128]{1,0:T(1,128)} %bitcast.9, f32[6,64,128]{2,1,0:T(8,128)} %bitcast.4, f32[19,64,128]{2,1,0:T(8,128)} %t_ref.1), custom_call_target="tpu_custom_call" | custom-call | flops 1000000 | bytes 1000000 | tf_op jit(solution)/shard_map/pallas_call | solution.py:560
  1.9 0.6 %collective-permute-start.3 = (f32[792,128]{1,0:T(8,128)S(1)}, f32[792,128]{1,0:T(8,128)S(1)}, u32[]{:S(2)}, u32[]{:S(2)}) collective-permute-start(f32[792,128]{1,0:T(8,128)S(1)} %get-tuple-element.33.pq_ref), channel_id=1, source_target_pairs={{0,1},{1,0},{2,3},{3,2},{4,5},{5,4},{6,7},{7,6},{8,9},{9,8},{10,11... | collective-permute-start | bytes 1216520 | tf_op jit(solution)/shard_map/ppermute | solution.py:585
  2.5 5.7 %collective-permute-start = (f32[536,128]{1,0:T(8,128)S(1)}, f32[536,128]{1,0:T(8,128)S(1)}, u32[]{:S(2)}, u32[]{:S(2)}) collective-permute-start(f32[536,128]{1,0:T(8,128)S(1)} %get-tuple-element.34), channel_id=1, source_target_pairs={{0,15},{1,2},{2,1},{3,4},{4,3},{5,6},{6,5},{7,8},{8,7},{9,10},{10,... | collective-permute-start | bytes 823304 | tf_op jit(solution)/shard_map/ppermute | solution.py:585
  8.1 0.0 collective-permute-start.1
  8.2 1.3 %collective-permute-start.2 = (f32[6,32,128]{2,1,0:T(8,128)S(1)}, f32[6,32,128]{2,1,0:T(8,128)S(1)}, u32[]{:S(2)}, u32[]{:S(2)}) collective-permute-start(f32[6,32,128]{2,1,0:T(8,128)S(1)} %get-tuple-element.36), channel_id=1, source_target_pairs={{16,0},{17,1},{18,2},{19,3},{20,4},{21,5},{22,6},{23,7},{24,8},{25... | collective-permute-start | bytes 294920 | tf_op jit(solution)/shard_map/ppermute | solution.py:585
  9.5 0.0 copy-done.2
  9.5 0.0 copy-start.1
  9.5 0.6 %shard_map.68 = (bf16[320,160]{1,0:T(8,128)(2,1)S(1)}, f32[19,128]{1,0:T(8,128)S(1)}) custom-call(f32[19,19]{1,0:T(8,128)S(1)} %copy-done.2), custom_call_target="tpu_custom_call" | custom-call | flops 1000000 | bytes 1000000 | tf_op jit(solution)/shard_map/pallas_call | solution.py:560
  10.1 4.6 %collective-permute-done.2.ga_ref = f32[6,32,128]{2,1,0:T(8,128)S(1)} collective-permute-done((f32[6,32,128]{2,1,0:T(8,128)S(1)}, f32[6,32,128]{2,1,0:T(8,128)S(1)}, u32[]{:S(2)}, u32[]{:S(2)}) %collective-permute-start.2) | collective-permute-done | bytes 98336 | tf_op jit(solution)/shard_map/ppermute | solution.py:585
  14.7 0.0 collective-permute-done.3.core_ref
  14.7 1.0 %shard_map.70 = (f32[19,5,8,128]{3,2,1,0:T(8,128)S(1)}, f32[3,5,8,128]{3,2,1,0:T(8,128)S(1)}, f32[2,5,8,128]{3,2,1,0:T(8,128)S(1)}, f32[4,8,8,128]{3,2,1,0:T(8,1...) custom-call(s32[3,128]{1,0:T(4,128)S(1)} %copy-done.1, f32[6,64,128]{2,1,0:T(8,128)S(1)} %bitcast.5, ...), custom_call_target="tpu_custom_call" | custom-call | flops 8000000 | bytes 1000000 | tf_op jit(solution)/shard_map/pallas_call | solution.py:560
  15.7 0.0 collective-permute-done.p_ref
  15.7 1.0 %shard_map.71 = (f32[536,128]{1,0:T(8,128)S(1)}, f32[19,8,128]{2,1,0:T(8,128)S(1)}) custom-call(bf16[320,160]{1,0:T(8,128)(2,1)S(1)} %get-tuple-element.32.react_ref, s32[3,128]{1,0:T(4,128)S(1)} %copy-done.1, f32[792,128]{1,0:T(8,128)S(1)} %get-tuple-element.33.pq_ref, f32[536,128]{1,0:T(8,128)S(1)} %collective-permute-done.p_ref, ...), custom_call_target="tpu_custom_call" | custom-call | flops 8000000 | bytes 1000000 | tf_op jit(solution)/shard_map/pallas_call | solution.py:560
  16.7 0.0 collective-permute-done.1.q_ref
  16.7 0.3 %shard_map.72 = (f32[304,128]{1,0:T(8,128)S(1)}, f32[840,128]{1,0:T(8,128)S(1)}, f32[6,64,128]{2,1,0:T(8,128)S(1)}, f32[6,40,128]{2,1,0:T(8,128)S(1)}, f32[6,24,128]{2,1,0:T(8,128)S(1)}) custom-call(bf16[320,160]{1,0:T(8,128)(2,1)S(1)} %get-tuple-element.32.react_ref, s32[3,128]{1,0:T(4,128)S(1)} %copy-done.1, f32[6,64,128]{2,1,0:T(8,128)S(1)} %bitcast.7, ...), custom_call_target="tpu_custom_call" | custom-call | flops 8000000 | bytes 1000000 | tf_op jit(solution)/shard_map/pallas_call | solution.py:560
  17.0 0.1 collective-permute-start.8
  17.1 3.6 %collective-permute-start.6 = (f32[536,128]{1,0:T(8,128)S(1)}, f32[536,128]{1,0:T(8,128)S(1)}, u32[]{:S(2)}, u32[]{:S(2)}) collective-permute-start(f32[536,128]{1,0:T(8,128)S(1)} %get-tuple-element.44.done_ref.chl_ref), channel_id=1, source_target_pairs={{0,15},{1,2},{2,1},{3,4},{4,3},{5,6},{6,5},{7,8},{8,7},{9,10},{10,... | collective-permute-start | bytes 823304 | tf_op jit(solution)/shard_map/ppermute | solution.py:585
  20.7 0.9 %collective-permute-start.7 = (f32[304,128]{1,0:T(8,128)S(1)}, f32[304,128]{1,0:T(8,128)S(1)}, u32[]{:S(2)}, u32[]{:S(2)}) collective-permute-start(f32[304,128]{1,0:T(8,128)S(1)} %get-tuple-element.50), channel_id=1, source_target_pairs={{0,15},{1,2},{2,1},{3,4},{4,3},{5,6},{6,5},{7,8},{8,7},{9,10},{10,... | collective-permute-start | bytes 466952 | tf_op jit(solution)/shard_map/ppermute | solution.py:585
  21.6 0.7 %collective-permute-start.4 = (f32[6,40,128]{2,1,0:T(8,128)S(1)}, f32[6,40,128]{2,1,0:T(8,128)S(1)}, u32[]{:S(2)}, u32[]{:S(2)}) collective-permute-start(f32[6,40,128]{2,1,0:T(8,128)S(1)} %get-tuple-element.47), channel_id=1, source_target_pairs={{0,16},{1,17},{2,18},{3,19},{4,20},{5,21},{6,22},{7,23},{8,24},{9,... | collective-permute-start | bytes 368648 | tf_op jit(solution)/shard_map/ppermute | solution.py:585
  22.3 3.2 %collective-permute-start.5 = (f32[6,24,128]{2,1,0:T(8,128)S(1)}, f32[6,24,128]{2,1,0:T(8,128)S(1)}, u32[]{:S(2)}, u32[]{:S(2)}) collective-permute-start(f32[6,24,128]{2,1,0:T(8,128)S(1)} %get-tuple-element.48), channel_id=1, source_target_pairs={{0,16},{1,17},{2,18},{3,19},{4,20},{5,21},{6,22},{7,23},{8,24},{9,... | collective-permute-start | bytes 221192 | tf_op jit(solution)/shard_map/ppermute | solution.py:585
  25.5 0.9 %collective-permute-done.4.gb_ref.refs_0_.over_ref = f32[6,40,128]{2,1,0:T(8,128)S(1)} collective-permute-done((f32[6,40,128]{2,1,0:T(8,128)S(1)}, f32[6,40,128]{2,1,0:T(8,128)S(1)}, u32[]{:S(2)}, u32[]{:S(2)}) %collective-permute-start.4) | collective-permute-done | bytes 122912 | tf_op jit(solution)/shard_map/ppermute | solution.py:585
  26.5 0.0 collective-permute-done.8.core_ref
  26.5 1.0 %shard_map.73 = (f32[19,5,8,128]{3,2,1,0:T(8,128)S(1)}, f32[3,5,8,128]{3,2,1,0:T(8,128)S(1)}, f32[2,5,8,128]{3,2,1,0:T(8,128)S(1)}, f32[4,8,8,128]{3,2,1,0:T(8,1...) custom-call(s32[3,128]{1,0:T(4,128)S(1)} %copy-done.1, ...), custom_call_target="tpu_custom_call" | custom-call | flops 8000000 | bytes 1000000 | tf_op jit(solution)/shard_map/pallas_call | solution.py:560
  27.5 0.0 collective-permute-done.6.p_ref
  27.5 0.5 %shard_map.75 = f32[32,128]{1,0:T(8,128)S(1)} custom-call(f32[19,128]{1,0:T(8,128)S(1)} %get-tuple-element.31.react_ref, s32[3,128]{1,0:T(4,128)S(1)} %copy-done.1, f32[840,128]{1,0:T(8,128)S(1)} %get-tuple-element.49.pq_ref, f32[536,128]{1,0:T(8,128)S(1)} %collective-permute-done.6.p_ref, f32[19,5,8,128]{3,2,1,0:T(8,128)S(1)} %get-tuple-element.51.part_ref, ...), custom_call_target="tpu_custom_call" | custom-call | flops 8000000 | bytes 1000000 | tf_op jit(solution)/shard_map/pallas_call | solution.py:560
  27.9 2.5 %collective-permute-start.9 = (f32[32,128]{1,0:T(8,128)S(1)}, f32[32,128]{1,0:T(8,128)S(1)}, u32[]{:S(2)}, u32[]{:S(2)}) collective-permute-start(f32[32,128]{1,0:T(8,128)S(1)} %shard_map.75), channel_id=1, source_target_pairs={{0,16},{1,17},{2,18},{3,19},{4,20},{5,21},{6,22},{7,23},{8,24},{9,... | collective-permute-start | bytes 49160 | tf_op jit(solution)/shard_map/ppermute | solution.py:585
  30.5 0.0 collective-permute-done.5.rest_ref
  30.5 0.0 collective-permute-done.7.q_ref
  30.5 1.0 %shard_map.74 = (f32[6,64,128]{2,1,0:T(8,128)}, f32[40,128]{1,0:T(8,128)S(1)}) custom-call(f32[19,128]{1,0:T(8,128)S(1)} %get-tuple-element.31.react_ref, s32[3,128]{1,0:T(4,128)S(1)} %copy-done.1, f32[6,64,128]{2,1,0:T(8,128)S(1)} %get-tuple-element.46.f_ref.ga_ref, f32[6,40,128]{2,1,0:T(8,128)S(1)} %collective-permute-done.4.gb_ref.refs_0_.over_ref, ...), custom_call_target="tpu_custom_call" | custom-call | flops 8000000 | bytes 1000000 | tf_op jit(solution)/shard_map/pallas_call | solution.py:560
  31.5 0.4 %collective-permute-done.9.upper_ref = f32[32,128]{1,0:T(8,128)S(1)} collective-permute-done((f32[32,128]{1,0:T(8,128)S(1)}, f32[32,128]{1,0:T(8,128)S(1)}, u32[]{:S(2)}, u32[]{:S(2)}) %collective-permute-start.9) | collective-permute-done | bytes 16416 | tf_op jit(solution)/shard_map/ppermute | solution.py:585
  31.9 0.6 %shard_map.76 = f32[64,128]{1,0:T(8,128)} custom-call(f32[64,128]{1,0:T(8,128)S(1)} %get-tuple-element.58.chl_ref, f32[40,128]{1,0:T(8,128)S(1)} %get-tuple-element.59.mine_ref, f32[32,128]{1,0:T(8,128)S(1)} %collective-permute-done.9.upper_ref), custom_call_target="tpu_custom_call" | custom-call | flops 1000000 | bytes 1000000 | tf_op jit(solution)/shard_map/pallas_call | solution.py:560
  (3 shorter events, 0.0 us)
Async XLA Ops:
  0.6 8.8 %copy-start.2 = (f32[19,19]{1,0:T(8,128)S(1)}, f32[19,19]{1,0:T(8,128)}, u32[]{:S(2)}) copy-start(f32[19,19]{1,0:T(8,128)} %r_ref.1) | copy-start | bytes 4336
  0.6 14.0 %copy-start = (f32[1,6,64,128]{3,2,1,0:T(8,128)S(1)}, f32[1,6,64,128]{3,2,1,0:T(8,128)}, u32[]{:S(2)}) copy-start(f32[1,6,64,128]{3,2,1,0:T(8,128)} %param.5) | copy-start | bytes 589828
  1.9 12.8 %collective-permute-start.3 = (f32[792,128]{1,0:T(8,128)S(1)}, f32[792,128]{1,0:T(8,128)S(1)}, u32[]{:S(2)}, u32[]{:S(2)}) collective-permute-start(f32[792,128]{1,0:T(8,128)S(1)} %get-tuple-element.33.pq_ref), channel_id=1, source_target_pairs={{0,1},{1,0},{2,3},{3,2},{4,5},{5,4},{6,7},{7,6},{8,9},{9,8},{10,11... | collective-permute-start | bytes 1216520 | tf_op jit(solution)/shard_map/ppermute | solution.py:585
  2.5 13.2 %collective-permute-start = (f32[536,128]{1,0:T(8,128)S(1)}, f32[536,128]{1,0:T(8,128)S(1)}, u32[]{:S(2)}, u32[]{:S(2)}) collective-permute-start(f32[536,128]{1,0:T(8,128)S(1)} %get-tuple-element.34), channel_id=1, source_target_pairs={{0,15},{1,2},{2,1},{3,4},{4,3},{5,6},{6,5},{7,8},{8,7},{9,10},{10,... | collective-permute-start | bytes 823304 | tf_op jit(solution)/shard_map/ppermute | solution.py:585
  8.1 8.5 %collective-permute-start.1 = (f32[256,128]{1,0:T(8,128)S(1)}, f32[256,128]{1,0:T(8,128)S(1)}, u32[]{:S(2)}, u32[]{:S(2)}) collective-permute-start(f32[256,128]{1,0:T(8,128)S(1)} %get-tuple-element.35), channel_id=1, source_target_pairs={{0,15},{1,2},{2,1},{3,4},{4,3},{5,6},{6,5},{7,8},{8,7},{9,10},{10,... | collective-permute-start | bytes 393224 | tf_op jit(solution)/shard_map/ppermute | solution.py:585
  8.2 6.5 %collective-permute-start.2 = (f32[6,32,128]{2,1,0:T(8,128)S(1)}, f32[6,32,128]{2,1,0:T(8,128)S(1)}, u32[]{:S(2)}, u32[]{:S(2)}) collective-permute-start(f32[6,32,128]{2,1,0:T(8,128)S(1)} %get-tuple-element.36), channel_id=1, source_target_pairs={{16,0},{17,1},{18,2},{19,3},{20,4},{21,5},{22,6},{23,7},{24,8},{25... | collective-permute-start | bytes 294920 | tf_op jit(solution)/shard_map/ppermute | solution.py:585
  9.5 5.2 %copy-start.1 = (s32[3,128]{1,0:T(4,128)S(1)}, s32[3,128]{1,0:T(4,128)}, u32[]{:S(2)}) copy-start(s32[3,128]{1,0:T(4,128)} %nb_ref.11) | copy-start | bytes 4612
  17.0 9.5 %collective-permute-start.8 = (f32[840,128]{1,0:T(8,128)S(1)}, f32[840,128]{1,0:T(8,128)S(1)}, u32[]{:S(2)}, u32[]{:S(2)}) collective-permute-start(f32[840,128]{1,0:T(8,128)S(1)} %get-tuple-element.49.pq_ref), channel_id=1, source_target_pairs={{0,1},{1,0},{2,3},{3,2},{4,5},{5,4},{6,7},{7,6},{8,9},{9,8},{10,11... | collective-permute-start | bytes 1290248 | tf_op jit(solution)/shard_map/ppermute | solution.py:585
  17.1 10.4 %collective-permute-start.6 = (f32[536,128]{1,0:T(8,128)S(1)}, f32[536,128]{1,0:T(8,128)S(1)}, u32[]{:S(2)}, u32[]{:S(2)}) collective-permute-start(f32[536,128]{1,0:T(8,128)S(1)} %get-tuple-element.44.done_ref.chl_ref), channel_id=1, source_target_pairs={{0,15},{1,2},{2,1},{3,4},{4,3},{5,6},{6,5},{7,8},{8,7},{9,10},{10,... | collective-permute-start | bytes 823304 | tf_op jit(solution)/shard_map/ppermute | solution.py:585
  20.7 9.7 %collective-permute-start.7 = (f32[304,128]{1,0:T(8,128)S(1)}, f32[304,128]{1,0:T(8,128)S(1)}, u32[]{:S(2)}, u32[]{:S(2)}) collective-permute-start(f32[304,128]{1,0:T(8,128)S(1)} %get-tuple-element.50), channel_id=1, source_target_pairs={{0,15},{1,2},{2,1},{3,4},{4,3},{5,6},{6,5},{7,8},{8,7},{9,10},{10,... | collective-permute-start | bytes 466952 | tf_op jit(solution)/shard_map/ppermute | solution.py:585
  21.6 4.9 %collective-permute-start.4 = (f32[6,40,128]{2,1,0:T(8,128)S(1)}, f32[6,40,128]{2,1,0:T(8,128)S(1)}, u32[]{:S(2)}, u32[]{:S(2)}) collective-permute-start(f32[6,40,128]{2,1,0:T(8,128)S(1)} %get-tuple-element.47), channel_id=1, source_target_pairs={{0,16},{1,17},{2,18},{3,19},{4,20},{5,21},{6,22},{7,23},{8,24},{9,... | collective-permute-start | bytes 368648 | tf_op jit(solution)/shard_map/ppermute | solution.py:585
  22.3 8.1 %collective-permute-start.5 = (f32[6,24,128]{2,1,0:T(8,128)S(1)}, f32[6,24,128]{2,1,0:T(8,128)S(1)}, u32[]{:S(2)}, u32[]{:S(2)}) collective-permute-start(f32[6,24,128]{2,1,0:T(8,128)S(1)} %get-tuple-element.48), channel_id=1, source_target_pairs={{0,16},{1,17},{2,18},{3,19},{4,20},{5,21},{6,22},{7,23},{8,24},{9,... | collective-permute-start | bytes 221192 | tf_op jit(solution)/shard_map/ppermute | solution.py:585
  27.9 3.9 %collective-permute-start.9 = (f32[32,128]{1,0:T(8,128)S(1)}, f32[32,128]{1,0:T(8,128)S(1)}, u32[]{:S(2)}, u32[]{:S(2)}) collective-permute-start(f32[32,128]{1,0:T(8,128)S(1)} %shard_map.75), channel_id=1, source_target_pairs={{0,16},{1,17},{2,18},{3,19},{4,20},{5,21},{6,22},{7,23},{8,24},{9,... | collective-permute-start | bytes 49160 | tf_op jit(solution)/shard_map/ppermute | solution.py:585

commit v2 on v1

--- a/solution.py
+++ b/solution.py
@@ -100,6 +100,10 @@
     return jnp.where((nxt < wet) & (nxt <= last), 0.02 + 0.13 * jax.nn.sigmoid(mixing), 0.0)
 
 
+def growth_rate(temperature, salinity, light):
+    return 0.5 * light * jax.nn.sigmoid(temperature + 0.5 * salinity)
+
+
 def wet_of(plan, ref):
     return jnp.broadcast_to(ref[plan.wet : plan.wet + 1, :], (SUB, ref.shape[1]))
 
@@ -108,7 +112,7 @@
     return pl.when(lax.axis_index("comp") == comp)
 
 
-def pack_kernel(plan, wet_ref, f_ref, t_ref, p_ref, q_ref, pq_ref, top_ref, chl_ref, wet_buf, half_buf, sems):
+def pack_kernel(plan, wet_ref, f_ref, t_ref, p_ref, q_ref, pq_ref, top_ref, chl_ref, wet_buf, half_buf, top_buf, sems):
     nt, full, half, lev = plan.nt, plan.full, plan.half, plan.lev
     tall = SUB * full
     first = pl.multiple_of(lax.axis_index("comp") * tall, SUB)
@@ -116,7 +120,7 @@
         (t_ref.at[:, pl.ds(first, tall)], p_ref.at[pl.ds(0, plan.halves)].reshape(nt, tall, p_ref.shape[1])),
         (t_ref.at[:, pl.ds(pl.multiple_of(first + tall, SUB), SUB)], half_buf),
         (wet_ref, wet_buf),
-        (f_ref.at[:, pl.ds(0, top_ref.shape[1])], top_ref),
+        (f_ref.at[:, pl.ds(0, top_ref.shape[1])], top_buf),
         (t_ref.at[0], chl_ref),
     ]
     copies = [pltpu.make_async_copy(s, d, sems.at[i]) for i, (s, d) in enumerate(copies)]
@@ -152,6 +156,8 @@
     def _():
         for c in deep:
             c.wait()
+        top_ref[0] = growth_rate(top_buf[0], top_buf[1], top_buf[5])
+        top_ref[1:4] = top_buf[2:5]
         for j in range(nt):
             at = SUB * nt + half * j
             q_ref[at : at + half, :] = half_buf[j, half:SUB, :]
@@ -214,14 +220,17 @@
         for r in plan.rs(comp):
             first = plan.level(comp, r)
             level = level_block(first, cols)
-            g_first = first - SUB * plan.full if comp and second else first
-            g = [(gb_ref if comp else ga_ref)[i, g_first : g_first + SUB, :] for i in range(6)]
-            near, far = split(level, edge_weights(g[2], g[3]))
+            passed = comp == int(second)
+            ref, at = (gb_ref if comp else ga_ref), first - SUB * plan.full * int(passed and comp)
+            g = [ref[i, at : at + SUB, :] for i in range(4 if passed else 6)]
+            if not passed:
+                g = [growth_rate(g[0], g[1], g[5])] + g[2:5]
+            near, far = split(level, edge_weights(g[1], g[2]))
             rest = 1.0 - (near[0] + near[1] + near[2])
             for k in range(3):
                 far_ref[k, r] = far[k]
-            aux_ref[0, r] = link_weight(level, wet, g[4], last)
-            aux_ref[1, r] = 0.5 * g[5] * jax.nn.sigmoid(g[0] + 0.5 * g[1])
+            aux_ref[0, r] = link_weight(level, wet, g[3], last)
+            aux_ref[1, r] = g[0]
             own = [plan.block(comp, second, rows_at(pq_ref), rows_at(pq_ref, p_rows), j, r) for j in range(nt)]
             core = [plan.block(comp, second, rows_at(core_ref), rows_at(core_ref, p_rows), j, r) for j in range(nt)]
             for j, v in enumerate(moves(own, core, [near] * nt, [rest] * nt)):
@@ -455,7 +464,7 @@
 
 def lower_kernel(
     plan, react_ref, nb_ref, f_ref, pq_ref, p_ref, q_ref, part_ref, far_ref, aux_ref, opart_ref, ofar_ref, oaux_ref,
-    done_ref, edge_ref, out_ref, both_ref, ocean_ref, over_ref, rest_ref, h_ref, l_ref, w_ref, wl_ref,
+    done_ref, edge_ref, out_ref, both_ref, ocean_ref, over_ref, h_ref, l_ref, w_ref, wl_ref,
 ):
     both_ref[0 : plan.p_rows, :] = done_ref[...]
 
@@ -464,15 +473,15 @@
         def put(i, b, value):
             at = SUB * b
             ocean_ref[i, at : at + SUB, :] = value
-            if b < plan.full:
-                rest_ref[i, at : at + SUB, :] = value
-            else:
-                over_ref[i, at - SUB * plan.full : at - SUB * plan.full + SUB, :] = value
+            if 2 <= i < 5 and b >= plan.full:
+                over_ref[i - 1, at - SUB * plan.full : at - SUB * plan.full + SUB, :] = value
             if i < 4:
                 for ref, base in ((out_ref, 0), (both_ref, plan.p_rows)):
                     ref[base + plan.lev * i + at : base + plan.lev * i + at + SUB, :] = value
 
         ocean_far(plan, nb_ref, f_ref, pq_ref, p_ref, q_ref, opart_ref, ofar_ref, oaux_ref, w_ref, wl_ref, put)
+        tall = SUB * plan.full
+        over_ref[0] = growth_rate(ocean_ref[0, tall:, :], ocean_ref[1, tall:, :], ocean_ref[5, tall:, :])
 
     @on_side(1)
     def _():
@@ -515,7 +524,7 @@
 
 
 def second_kernel(
-    plan, react_ref, nb_ref, f_ref, over_ref, rest_ref, pq_ref, p_ref, q_ref, part_ref, far_ref, aux_ref, opart_ref,
+    plan, react_ref, nb_ref, f_ref, rest_ref, pq_ref, p_ref, q_ref, part_ref, far_ref, aux_ref, opart_ref,
     ofar_ref, oaux_ref, out_ref, mine_ref, h_ref, l_ref, w_ref, wl_ref,
 ):
     @on_side(0)
@@ -527,9 +536,7 @@
 
     @on_side(1)
     def _():
-        tall = SUB * plan.full
-        out_ref[:, 0:tall, :] = rest_ref[...]
-        out_ref[:, tall:, :] = over_ref[...]
+        out_ref[...] = rest_ref[...]
         work = Far(plan, 1, True, nb_ref, pq_ref, p_ref, part_ref, far_ref, aux_ref, h_ref, l_ref)
         work.clear(-1, plan.window)
         for r in plan.rs(1):
@@ -613,7 +620,7 @@
             shape_of(p_rows, cols),
             shape_of(plan.q_rows[0], cols),
             shape_of(p_rows + plan.q_rows[0], cols),
-            shape_of(nf, top, cols),
+            shape_of(4, top, cols),
             shape_of(lev, cols),
         ),
         tuple(
@@ -623,6 +630,7 @@
         scratch=[
             pltpu.VMEM((1, cols), jnp.int32),
             pltpu.VMEM((nt, SUB, cols), F32),
+            pltpu.VMEM((nf, top, cols), F32),
             pltpu.SemaphoreType.DMA((6,)),
         ],
     )
@@ -649,14 +657,13 @@
         cost=8_000_000,
     )
     cross_p_one = sent(p_one, across)
-    q_one, pq_one, ocean_one, over_one, rest_one = call(
+    q_one, pq_one, ocean_one, over_one = call(
         kernel(lower_kernel),
         (
             shape_of(plan.q_rows[1], cols),
             shape_of(p_rows + plan.q_rows[1], cols),
             shape_of(nf, lev, cols),
-            shape_of(nf, lev - tall, cols),
-            shape_of(nf, tall, cols),
+            shape_of(4, lev - tall, cols),
         ),
         (matrix, neighbours, fields, pq, cross_p, cross_q, *near, p_one, edge),
         scratch=h_scratch + w_scratch,
@@ -665,7 +672,7 @@
     over = sent(over_one, over_comp((0, 1), tiles))
     core_one = sent(pq_one, within)
     cross_q_one = sent(q_one, across)
-    rest = sent(rest_one, over_comp((0,), tiles))
+    rest = sent(ocean_one, over_comp((0,), tiles))
 
     *near, chl_one = call(
         kernel(near_kernel, True),
@@ -684,7 +691,7 @@
     ocean_out, mine = call(
         kernel(second_kernel),
         (shape_of(nf, lev, cols), shape_of(lev - tall, cols)),
-        (rates, neighbours, ocean_one, over, rest, pq_one, cross_p_one, cross_q_one, *near),
+        (rates, neighbours, ocean_one, rest, pq_one, cross_p_one, cross_q_one, *near),
         scratch=h_scratch + w_scratch,
         cost=8_000_000,
     )

time: 32.7 us -> 35.6 us (1.089)
  waiting for transfers between devices: 5.97 us -> 9.09 us
    ppermute x10, waiting for transfers between devices: 5.97 us -> 9.09 us  [sent(): return lax.ppermute(v, AXES, pairs)]
  transfers between devices with their start and end apart: 10 -> 10, of which waited for: 3 -> 3; matrix products, arithmetic and copies ran while one was open for 0% -> 0% of each run, Pallas kernels for 15% -> 14%
where the time goes in v2:
time: 35.6 us; the launch traced here: 35.4 us
  starting transfers between devices  18.3 us (51%)
  waiting for transfers between devices  9.09 us (26%)
  Pallas kernels  7.2 us (20%)
  between operations  0.8 us (2%)
    ppermute x10, starting transfers between devices, sent(): return lax.ppermute(v, AXES, pairs)  18.3 us
    ppermute x10, waiting for transfers between devices, sent(): return lax.ppermute(v, AXES, pairs)  9.09 us
    pallas_call x9, Pallas kernels, call(): pl.pallas_call(kernel, out_shape=outs, in_specs=specs or [VMEM] * len(ins...  7.2 us
  transfers between devices with their start and end apart: 10, of which 3 were waited for; matrix products, arithmetic and copies ran while one was open for 0% of the time, Pallas kernels for 14%

profile of v2, /device:TPU:0, one launch (start us, length us, event | category | flops | bytes accessed | tf_op | source)
XLA Modules:
  0.0 35.4 jit_solution(10762423718112146017)
XLA Ops:
  0.7 1.3 %shard_map.69 = (f32[536,128]{1,0:T(8,128)S(1)}, f32[256,128]{1,0:T(8,128)S(1)}, f32[792,128]{1,0:T(8,128)S(1)}, f32[4,32,128]{2,1,0:T(8,128)S(1)}, f32[64,128]{1,0:T(8,128)S(1)}) custom-call(s32[1,128]{1,0:T(1,128)} %bitcast.9, f32[6,64,128]{2,1,0:T(8,128)} %bitcast.4, f32[19,64,128]{2,1,0:T(8,128)} %t_ref.1), custom_call_target="tpu_custom_call" | custom-call | flops 1000000 | bytes 1000000 | tf_op jit(solution)/shard_map/pallas_call | solution.py:567
  1.9 0.6 %collective-permute-start.3 = (f32[792,128]{1,0:T(8,128)S(1)}, f32[792,128]{1,0:T(8,128)S(1)}, u32[]{:S(2)}, u32[]{:S(2)}) collective-permute-start(f32[792,128]{1,0:T(8,128)S(1)} %get-tuple-element.32.pq_ref), channel_id=1, source_target_pairs={{0,1},{1,0},{2,3},{3,2},{4,5},{5,4},{6,7},{7,6},{8,9},{9,8},{10,11... | collective-permute-start | bytes 1216520 | tf_op jit(solution)/shard_map/ppermute | solution.py:592
  2.5 5.7 %collective-permute-start = (f32[536,128]{1,0:T(8,128)S(1)}, f32[536,128]{1,0:T(8,128)S(1)}, u32[]{:S(2)}, u32[]{:S(2)}) collective-permute-start(f32[536,128]{1,0:T(8,128)S(1)} %get-tuple-element.33), channel_id=1, source_target_pairs={{0,15},{1,2},{2,1},{3,4},{4,3},{5,6},{6,5},{7,8},{8,7},{9,10},{10,... | collective-permute-start | bytes 823304 | tf_op jit(solution)/shard_map/ppermute | solution.py:592
  8.1 0.0 collective-permute-start.1
  8.2 1.3 %collective-permute-start.2 = (f32[4,32,128]{2,1,0:T(8,128)S(1)}, f32[4,32,128]{2,1,0:T(8,128)S(1)}, u32[]{:S(2)}, u32[]{:S(2)}) collective-permute-start(f32[4,32,128]{2,1,0:T(8,128)S(1)} %get-tuple-element.35), channel_id=1, source_target_pairs={{16,0},{17,1},{18,2},{19,3},{20,4},{21,5},{22,6},{23,7},{24,8},{25... | collective-permute-start | bytes 196616 | tf_op jit(solution)/shard_map/ppermute | solution.py:592
  9.5 0.0 copy-done.2
  9.5 0.0 copy-start.1
  9.5 0.6 %shard_map.68 = (bf16[320,160]{1,0:T(8,128)(2,1)S(1)}, f32[19,128]{1,0:T(8,128)S(1)}) custom-call(f32[19,19]{1,0:T(8,128)S(1)} %copy-done.2), custom_call_target="tpu_custom_call" | custom-call | flops 1000000 | bytes 1000000 | tf_op jit(solution)/shard_map/pallas_call | solution.py:567
  10.1 4.2 %collective-permute-done.2.ga_ref = f32[4,32,128]{2,1,0:T(8,128)S(1)} collective-permute-done((f32[4,32,128]{2,1,0:T(8,128)S(1)}, f32[4,32,128]{2,1,0:T(8,128)S(1)}, u32[]{:S(2)}, u32[]{:S(2)}) %collective-permute-start.2) | collective-permute-done | bytes 65568 | tf_op jit(solution)/shard_map/ppermute | solution.py:592
  14.3 0.0 collective-permute-done.3.core_ref
  14.3 0.0 copy-done
  14.3 1.0 %shard_map.70 = (f32[19,5,8,128]{3,2,1,0:T(8,128)S(1)}, f32[3,5,8,128]{3,2,1,0:T(8,128)S(1)}, f32[2,5,8,128]{3,2,1,0:T(8,128)S(1)}, f32[4,8,8,128]{3,2,1,0:T(8,1...) custom-call(s32[3,128]{1,0:T(4,128)S(1)} %copy-done.1, f32[6,64,128]{2,1,0:T(8,128)S(1)} %bitcast.5, ...), custom_call_target="tpu_custom_call" | custom-call | flops 8000000 | bytes 1000000 | tf_op jit(solution)/shard_map/pallas_call | solution.py:567
  15.3 0.0 collective-permute-done.p_ref
  15.3 1.0 %shard_map.71 = (f32[536,128]{1,0:T(8,128)S(1)}, f32[19,8,128]{2,1,0:T(8,128)S(1)}) custom-call(bf16[320,160]{1,0:T(8,128)(2,1)S(1)} %get-tuple-element.31.react_ref, s32[3,128]{1,0:T(4,128)S(1)} %copy-done.1, f32[792,128]{1,0:T(8,128)S(1)} %get-tuple-element.32.pq_ref, f32[536,128]{1,0:T(8,128)S(1)} %collective-permute-done.p_ref, ...), custom_call_target="tpu_custom_call" | custom-call | flops 8000000 | bytes 1000000 | tf_op jit(solution)/shard_map/pallas_call | solution.py:567
  16.3 0.0 collective-permute-done.1.q_ref
  16.3 0.3 shard_map.72
  16.7 0.1 collective-permute-start.8
  16.7 3.6 %collective-permute-start.5 = (f32[536,128]{1,0:T(8,128)S(1)}, f32[536,128]{1,0:T(8,128)S(1)}, u32[]{:S(2)}, u32[]{:S(2)}) collective-permute-start(f32[536,128]{1,0:T(8,128)S(1)} %get-tuple-element.43.done_ref.chl_ref), channel_id=1, source_target_pairs={{0,15},{1,2},{2,1},{3,4},{4,3},{5,6},{6,5},{7,8},{8,7},{9,10},{10,... | collective-permute-start | bytes 823304 | tf_op jit(solution)/shard_map/ppermute | solution.py:592
  20.4 3.7 %collective-permute-start.4 = (f32[6,64,128]{2,1,0:T(8,128)S(1)}, f32[6,64,128]{2,1,0:T(8,128)S(1)}, u32[]{:S(2)}, u32[]{:S(2)}) collective-permute-start(f32[6,64,128]{2,1,0:T(8,128)S(1)} %get-tuple-element.45.f_ref.ga_ref), channel_id=1, source_target_pairs={{0,16},{1,17},{2,18},{3,19},{4,20},{5,21},{6,22},{7,23},{8,24},{9,... | collective-permute-start | bytes 589832 | tf_op jit(solution)/shard_map/ppermute | solution.py:592
  24.0 0.1 collective-permute-start.6
  24.1 0.1 collective-permute-start.7
  24.2 4.4 %collective-permute-done.7.gb_ref.refs_0_ = f32[4,40,128]{2,1,0:T(8,128)S(1)} collective-permute-done((f32[4,40,128]{2,1,0:T(8,128)S(1)}, f32[4,40,128]{2,1,0:T(8,128)S(1)}, u32[]{:S(2)}, u32[]{:S(2)}) %collective-permute-start.7) | collective-permute-done | bytes 81952 | tf_op jit(solution)/shard_map/ppermute | solution.py:592
  28.6 0.0 collective-permute-done.8.core_ref
  28.6 1.0 %shard_map.73 = (f32[19,5,8,128]{3,2,1,0:T(8,128)S(1)}, f32[3,5,8,128]{3,2,1,0:T(8,128)S(1)}, f32[2,5,8,128]{3,2,1,0:T(8,128)S(1)}, f32[4,8,8,128]{3,2,1,0:T(8,1...) custom-call(s32[3,128]{1,0:T(4,128)S(1)} %copy-done.1, ...), custom_call_target="tpu_custom_call" | custom-call | flops 8000000 | bytes 1000000 | tf_op jit(solution)/shard_map/pallas_call | solution.py:567
  29.6 0.0 collective-permute-done.5.p_ref
  29.6 0.5 %shard_map.75 = f32[32,128]{1,0:T(8,128)S(1)} custom-call(f32[19,128]{1,0:T(8,128)S(1)} %get-tuple-element.30.react_ref, s32[3,128]{1,0:T(4,128)S(1)} %copy-done.1, f32[840,128]{1,0:T(8,128)S(1)} %get-tuple-element.46.pq_ref, f32[536,128]{1,0:T(8,128)S(1)} %collective-permute-done.5.p_ref, f32[19,5,8,128]{3,2,1,0:T(8,128)S(1)} %get-tuple-element.49.part_ref, ...), custom_call_target="tpu_custom_call" | custom-call | flops 8000000 | bytes 1000000 | tf_op jit(solution)/shard_map/pallas_call | solution.py:567
  30.1 3.2 %collective-permute-start.9 = (f32[32,128]{1,0:T(8,128)S(1)}, f32[32,128]{1,0:T(8,128)S(1)}, u32[]{:S(2)}, u32[]{:S(2)}) collective-permute-start(f32[32,128]{1,0:T(8,128)S(1)} %shard_map.75), channel_id=1, source_target_pairs={{0,16},{1,17},{2,18},{3,19},{4,20},{5,21},{6,22},{7,23},{8,24},{9,... | collective-permute-start | bytes 49160 | tf_op jit(solution)/shard_map/ppermute | solution.py:592
  33.3 0.0 collective-permute-done.6.q_ref
  33.3 0.0 collective-permute-done.4.rest_ref
  33.4 1.0 %shard_map.74 = (f32[6,64,128]{2,1,0:T(8,128)}, f32[40,128]{1,0:T(8,128)S(1)}) custom-call(f32[19,128]{1,0:T(8,128)S(1)} %get-tuple-element.30.react_ref, s32[3,128]{1,0:T(4,128)S(1)} %copy-done.1, f32[6,64,128]{2,1,0:T(8,128)S(1)} %get-tuple-element.45.f_ref.ga_ref, f32[6,64,128]{2,1,0:T(8,128)S(1)} %collective-permute-done.4.rest_ref, ...), custom_call_target="tpu_custom_call" | custom-call | flops 8000000 | bytes 1000000 | tf_op jit(solution)/shard_map/pallas_call | solution.py:567
  34.4 0.4 %collective-permute-done.9.upper_ref = f32[32,128]{1,0:T(8,128)S(1)} collective-permute-done((f32[32,128]{1,0:T(8,128)S(1)}, f32[32,128]{1,0:T(8,128)S(1)}, u32[]{:S(2)}, u32[]{:S(2)}) %collective-permute-start.9) | collective-permute-done | bytes 16416 | tf_op jit(solution)/shard_map/ppermute | solution.py:592
  34.8 0.6 %shard_map.76 = f32[64,128]{1,0:T(8,128)} custom-call(f32[64,128]{1,0:T(8,128)S(1)} %get-tuple-element.56.chl_ref, f32[40,128]{1,0:T(8,128)S(1)} %get-tuple-element.57.mine_ref, f32[32,128]{1,0:T(8,128)S(1)} %collective-permute-done.9.upper_ref), custom_call_target="tpu_custom_call" | custom-call | flops 1000000 | bytes 1000000 | tf_op jit(solution)/shard_map/pallas_call | solution.py:567
  (3 shorter events, 0.0 us)
Async XLA Ops:
  0.6 8.8 %copy-start.2 = (f32[19,19]{1,0:T(8,128)S(1)}, f32[19,19]{1,0:T(8,128)}, u32[]{:S(2)}) copy-start(f32[19,19]{1,0:T(8,128)} %r_ref.1) | copy-start | bytes 4336
  0.6 13.7 %copy-start = (f32[1,6,64,128]{3,2,1,0:T(8,128)S(1)}, f32[1,6,64,128]{3,2,1,0:T(8,128)}, u32[]{:S(2)}) copy-start(f32[1,6,64,128]{3,2,1,0:T(8,128)} %param.5) | copy-start | bytes 589828
  1.9 12.4 %collective-permute-start.3 = (f32[792,128]{1,0:T(8,128)S(1)}, f32[792,128]{1,0:T(8,128)S(1)}, u32[]{:S(2)}, u32[]{:S(2)}) collective-permute-start(f32[792,128]{1,0:T(8,128)S(1)} %get-tuple-element.32.pq_ref), channel_id=1, source_target_pairs={{0,1},{1,0},{2,3},{3,2},{4,5},{5,4},{6,7},{7,6},{8,9},{9,8},{10,11... | collective-permute-start | bytes 1216520 | tf_op jit(solution)/shard_map/ppermute | solution.py:592
  2.5 12.8 %collective-permute-start = (f32[536,128]{1,0:T(8,128)S(1)}, f32[536,128]{1,0:T(8,128)S(1)}, u32[]{:S(2)}, u32[]{:S(2)}) collective-permute-start(f32[536,128]{1,0:T(8,128)S(1)} %get-tuple-element.33), channel_id=1, source_target_pairs={{0,15},{1,2},{2,1},{3,4},{4,3},{5,6},{6,5},{7,8},{8,7},{9,10},{10,... | collective-permute-start | bytes 823304 | tf_op jit(solution)/shard_map/ppermute | solution.py:592
  8.1 8.2 %collective-permute-start.1 = (f32[256,128]{1,0:T(8,128)S(1)}, f32[256,128]{1,0:T(8,128)S(1)}, u32[]{:S(2)}, u32[]{:S(2)}) collective-permute-start(f32[256,128]{1,0:T(8,128)S(1)} %get-tuple-element.34), channel_id=1, source_target_pairs={{0,15},{1,2},{2,1},{3,4},{4,3},{5,6},{6,5},{7,8},{8,7},{9,10},{10,... | collective-permute-start | bytes 393224 | tf_op jit(solution)/shard_map/ppermute | solution.py:592
  8.2 6.1 %collective-permute-start.2 = (f32[4,32,128]{2,1,0:T(8,128)S(1)}, f32[4,32,128]{2,1,0:T(8,128)S(1)}, u32[]{:S(2)}, u32[]{:S(2)}) collective-permute-start(f32[4,32,128]{2,1,0:T(8,128)S(1)} %get-tuple-element.35), channel_id=1, source_target_pairs={{16,0},{17,1},{18,2},{19,3},{20,4},{21,5},{22,6},{23,7},{24,8},{25... | collective-permute-start | bytes 196616 | tf_op jit(solution)/shard_map/ppermute | solution.py:592
  9.5 4.9 %copy-start.1 = (s32[3,128]{1,0:T(4,128)S(1)}, s32[3,128]{1,0:T(4,128)}, u32[]{:S(2)}) copy-start(s32[3,128]{1,0:T(4,128)} %nb_ref.11) | copy-start | bytes 4612
  16.7 12.0 %collective-permute-start.8 = (f32[840,128]{1,0:T(8,128)S(1)}, f32[840,128]{1,0:T(8,128)S(1)}, u32[]{:S(2)}, u32[]{:S(2)}) collective-permute-start(f32[840,128]{1,0:T(8,128)S(1)} %get-tuple-element.46.pq_ref), channel_id=1, source_target_pairs={{0,1},{1,0},{2,3},{3,2},{4,5},{5,4},{6,7},{7,6},{8,9},{9,8},{10,11... | collective-permute-start | bytes 1290248 | tf_op jit(solution)/shard_map/ppermute | solution.py:592
  16.7 12.9 %collective-permute-start.5 = (f32[536,128]{1,0:T(8,128)S(1)}, f32[536,128]{1,0:T(8,128)S(1)}, u32[]{:S(2)}, u32[]{:S(2)}) collective-permute-start(f32[536,128]{1,0:T(8,128)S(1)} %get-tuple-element.43.done_ref.chl_ref), channel_id=1, source_target_pairs={{0,15},{1,2},{2,1},{3,4},{4,3},{5,6},{6,5},{7,8},{8,7},{9,10},{10,... | collective-permute-start | bytes 823304 | tf_op jit(solution)/shard_map/ppermute | solution.py:592
  20.4 13.0 %collective-permute-start.4 = (f32[6,64,128]{2,1,0:T(8,128)S(1)}, f32[6,64,128]{2,1,0:T(8,128)S(1)}, u32[]{:S(2)}, u32[]{:S(2)}) collective-permute-start(f32[6,64,128]{2,1,0:T(8,128)S(1)} %get-tuple-element.45.f_ref.ga_ref), channel_id=1, source_target_pairs={{0,16},{1,17},{2,18},{3,19},{4,20},{5,21},{6,22},{7,23},{8,24},{9,... | collective-permute-start | bytes 589832 | tf_op jit(solution)/shard_map/ppermute | solution.py:592
  24.0 9.3 %collective-permute-start.6 = (f32[304,128]{1,0:T(8,128)S(1)}, f32[304,128]{1,0:T(8,128)S(1)}, u32[]{:S(2)}, u32[]{:S(2)}) collective-permute-start(f32[304,128]{1,0:T(8,128)S(1)} %get-tuple-element.47), channel_id=1, source_target_pairs={{0,15},{1,2},{2,1},{3,4},{4,3},{5,6},{6,5},{7,8},{8,7},{9,10},{10,... | collective-permute-start | bytes 466952 | tf_op jit(solution)/shard_map/ppermute | solution.py:592
  24.1 4.5 %collective-permute-start.7 = (f32[4,40,128]{2,1,0:T(8,128)S(1)}, f32[4,40,128]{2,1,0:T(8,128)S(1)}, u32[]{:S(2)}, u32[]{:S(2)}) collective-permute-start(f32[4,40,128]{2,1,0:T(8,128)S(1)} %get-tuple-element.48), channel_id=1, source_target_pairs={{0,16},{1,17},{2,18},{3,19},{4,20},{5,21},{6,22},{7,23},{8,24},{9,... | collective-permute-start | bytes 245768 | tf_op jit(solution)/shard_map/ppermute | solution.py:592
  30.1 4.7 %collective-permute-start.9 = (f32[32,128]{1,0:T(8,128)S(1)}, f32[32,128]{1,0:T(8,128)S(1)}, u32[]{:S(2)}, u32[]{:S(2)}) collective-permute-start(f32[32,128]{1,0:T(8,128)S(1)} %shard_map.75), channel_id=1, source_target_pairs={{0,16},{1,17},{2,18},{3,19},{4,20},{5,21},{6,22},{7,23},{8,24},{9,... | collective-permute-start | bytes 49160 | tf_op jit(solution)/shard_map/ppermute | solution.py:592

commit v3 on v2

--- a/solution.py
+++ b/solution.py
@@ -44,6 +44,10 @@
 
     def level(self, comp, r):
         return SUB * (r - 1) if comp == 0 else SUB * (self.full + r)
+
+    def rest(self, i):
+        tall = SUB * self.full
+        return (0, self.lev, 2 * self.lev, 2 * self.lev + tall, 2 * self.lev + 2 * tall, 2 * self.lev + 3 * tall)[i]
 
     def block(self, comp, second, p, q, j, r):
         if comp == 0:
@@ -464,7 +468,7 @@
 
 def lower_kernel(
     plan, react_ref, nb_ref, f_ref, pq_ref, p_ref, q_ref, part_ref, far_ref, aux_ref, opart_ref, ofar_ref, oaux_ref,
-    done_ref, edge_ref, out_ref, both_ref, ocean_ref, over_ref, h_ref, l_ref, w_ref, wl_ref,
+    done_ref, edge_ref, out_ref, both_ref, ocean_ref, over_ref, rest_ref, h_ref, l_ref, w_ref, wl_ref,
 ):
     both_ref[0 : plan.p_rows, :] = done_ref[...]
 
@@ -475,6 +479,8 @@
             ocean_ref[i, at : at + SUB, :] = value
             if 2 <= i < 5 and b >= plan.full:
                 over_ref[i - 1, at - SUB * plan.full : at - SUB * plan.full + SUB, :] = value
+            else:
+                rest_ref[plan.rest(i) + at : plan.rest(i) + at + SUB, :] = value
             if i < 4:
                 for ref, base in ((out_ref, 0), (both_ref, plan.p_rows)):
                     ref[base + plan.lev * i + at : base + plan.lev * i + at + SUB, :] = value
@@ -524,7 +530,7 @@
 
 
 def second_kernel(
-    plan, react_ref, nb_ref, f_ref, rest_ref, pq_ref, p_ref, q_ref, part_ref, far_ref, aux_ref, opart_ref,
+    plan, react_ref, nb_ref, f_ref, pq_ref, p_ref, q_ref, part_ref, far_ref, aux_ref, opart_ref,
     ofar_ref, oaux_ref, out_ref, mine_ref, h_ref, l_ref, w_ref, wl_ref,
 ):
     @on_side(0)
@@ -536,7 +542,6 @@
 
     @on_side(1)
     def _():
-        out_ref[...] = rest_ref[...]
         work = Far(plan, 1, True, nb_ref, pq_ref, p_ref, part_ref, far_ref, aux_ref, h_ref, l_ref)
         work.clear(-1, plan.window)
         for r in plan.rs(1):
@@ -549,18 +554,27 @@
             work.react(r, react_ref, put)
 
 
-def merge_kernel(plan, chl_ref, mine_ref, upper_ref, out_ref):
+def merge_kernel(plan, ocean_ref, over_ref, rest_ref, chl_ref, mine_ref, upper_ref, out_ref, chl_out_ref):
+    tall = SUB * plan.full
+
     @on_side(0)
     def _():
-        out_ref[...] = chl_ref[...]
+        out_ref[...] = ocean_ref[...]
+        chl_out_ref[...] = chl_ref[...]
 
     @on_side(1)
     def _():
-        tall = SUB * plan.full
-        sub = lax.broadcasted_iota(jnp.int32, (SUB, out_ref.shape[1]), 0)
-        out_ref[0:tall, :] = upper_ref[0:tall, :]
-        out_ref[tall : tall + SUB, :] = jnp.where(sub < 2, upper_ref[tall : tall + SUB, :], mine_ref[0:SUB, :])
-        out_ref[tall + SUB :, :] = mine_ref[SUB:, :]
+        for i in range(6):
+            at = plan.rest(i)
+            if 2 <= i < 5:
+                out_ref[i, 0:tall, :] = rest_ref[at : at + tall, :]
+                out_ref[i, tall:, :] = over_ref[i - 1]
+            else:
+                out_ref[i] = rest_ref[at : at + plan.lev, :]
+        sub = lax.broadcasted_iota(jnp.int32, (SUB, chl_out_ref.shape[1]), 0)
+        chl_out_ref[0:tall, :] = upper_ref[0:tall, :]
+        chl_out_ref[tall : tall + SUB, :] = jnp.where(sub < 2, upper_ref[tall : tall + SUB, :], mine_ref[0:SUB, :])
+        chl_out_ref[tall + SUB :, :] = mine_ref[SUB:, :]
 
 
 def call(kernel, outs, ins, specs=None, scratch=(), cost=1_000_000):
@@ -657,13 +671,14 @@
         cost=8_000_000,
     )
     cross_p_one = sent(p_one, across)
-    q_one, pq_one, ocean_one, over_one = call(
+    q_one, pq_one, ocean_one, over_one, rest_one = call(
         kernel(lower_kernel),
         (
             shape_of(plan.q_rows[1], cols),
             shape_of(p_rows + plan.q_rows[1], cols),
             shape_of(nf, lev, cols),
             shape_of(4, lev - tall, cols),
+            shape_of(3 * (lev + tall), cols),
         ),
         (matrix, neighbours, fields, pq, cross_p, cross_q, *near, p_one, edge),
         scratch=h_scratch + w_scratch,
@@ -672,7 +687,7 @@
     over = sent(over_one, over_comp((0, 1), tiles))
     core_one = sent(pq_one, within)
     cross_q_one = sent(q_one, across)
-    rest = sent(ocean_one, over_comp((0,), tiles))
+    rest = sent(rest_one, over_comp((0,), tiles))
 
     *near, chl_one = call(
         kernel(near_kernel, True),
@@ -688,14 +703,18 @@
         cost=8_000_000,
     )
     upper = sent(upper, over_comp((0,), tiles))
-    ocean_out, mine = call(
+    ocean_two, mine = call(
         kernel(second_kernel),
         (shape_of(nf, lev, cols), shape_of(lev - tall, cols)),
-        (rates, neighbours, ocean_one, rest, pq_one, cross_p_one, cross_q_one, *near),
+        (rates, neighbours, ocean_one, pq_one, cross_p_one, cross_q_one, *near),
         scratch=h_scratch + w_scratch,
         cost=8_000_000,
     )
-    chl_out = call(kernel(merge_kernel), shape_of(lev, cols), (chl_one, mine, upper))
+    ocean_out, chl_out = call(
+        kernel(merge_kernel),
+        (shape_of(nf, lev, cols), shape_of(lev, cols)),
+        (ocean_two, over, rest, chl_one, mine, upper),
+    )
     return (ocean_out[None], chl_out[None])
 
 

time: 35.6 us -> 35.2 us (0.989)
  waiting for transfers between devices: 9.09 us -> 9.76 us
  Pallas kernels: 7.2 us -> 6.6 us
  starting transfers between devices: 18.3 us -> 17.8 us
    ppermute x10, waiting for transfers between devices: 9.09 us -> 9.76 us  [sent(): return lax.ppermute(v, AXES, pairs)]
    pallas_call x9, Pallas kernels: 7.2 us -> 6.6 us  [call(): pl.pallas_call(kernel, out_shape=outs, in_specs=specs or [VMEM] * len(ins...]
    ppermute x10, starting transfers between devices: 18.3 us -> 17.8 us  [sent(): return lax.ppermute(v, AXES, pairs)]
  transfers between devices with their start and end apart: 10 -> 10, of which waited for: 3 -> 3; matrix products, arithmetic and copies ran while one was open for 0% -> 0% of each run, Pallas kernels for 14% -> 12%
where the time goes in v3:
time: 35.2 us; the launch traced here: 35 us
  starting transfers between devices  17.8 us (51%)
  waiting for transfers between devices  9.76 us (28%)
  Pallas kernels  6.6 us (19%)
  between operations  0.8 us (2%)
    ppermute x10, starting transfers between devices, sent(): return lax.ppermute(v, AXES, pairs)  17.8 us
    ppermute x10, waiting for transfers between devices, sent(): return lax.ppermute(v, AXES, pairs)  9.76 us
    pallas_call x9, Pallas kernels, call(): pl.pallas_call(kernel, out_shape=outs, in_specs=specs or [VMEM] * len(ins...  6.6 us
  transfers between devices with their start and end apart: 10, of which 3 were waited for; matrix products, arithmetic and copies ran while one was open for 0% of the time, Pallas kernels for 12%

profile of v3, /device:TPU:0, one launch (start us, length us, event | category | flops | bytes accessed | tf_op | source)
XLA Modules:
  0.0 35.0 jit_solution(12014723167030402044)
XLA Ops:
  0.7 1.3 %shard_map.69 = (f32[536,128]{1,0:T(8,128)S(1)}, f32[256,128]{1,0:T(8,128)S(1)}, f32[792,128]{1,0:T(8,128)S(1)}, f32[4,32,128]{2,1,0:T(8,128)S(1)}, f32[64,128]{1,0:T(8,128)S(1)}) custom-call(s32[1,128]{1,0:T(1,128)} %bitcast.8, f32[6,64,128]{2,1,0:T(8,128)} %bitcast.4, f32[19,64,128]{2,1,0:T(8,128)} %t_ref.1), custom_call_target="tpu_custom_call" | custom-call | flops 1000000 | bytes 1000000 | tf_op jit(solution)/shard_map/pallas_call | solution.py:581
  1.9 0.6 %collective-permute-start.3 = (f32[792,128]{1,0:T(8,128)S(1)}, f32[792,128]{1,0:T(8,128)S(1)}, u32[]{:S(2)}, u32[]{:S(2)}) collective-permute-start(f32[792,128]{1,0:T(8,128)S(1)} %get-tuple-element.35.pq_ref), channel_id=1, source_target_pairs={{0,1},{1,0},{2,3},{3,2},{4,5},{5,4},{6,7},{7,6},{8,9},{9,8},{10,11... | collective-permute-start | bytes 1216520 | tf_op jit(solution)/shard_map/ppermute | solution.py:606
  2.5 5.7 %collective-permute-start = (f32[536,128]{1,0:T(8,128)S(1)}, f32[536,128]{1,0:T(8,128)S(1)}, u32[]{:S(2)}, u32[]{:S(2)}) collective-permute-start(f32[536,128]{1,0:T(8,128)S(1)} %get-tuple-element.36), channel_id=1, source_target_pairs={{0,15},{1,2},{2,1},{3,4},{4,3},{5,6},{6,5},{7,8},{8,7},{9,10},{10,... | collective-permute-start | bytes 823304 | tf_op jit(solution)/shard_map/ppermute | solution.py:606
  8.1 0.0 collective-permute-start.1
  8.2 1.3 %collective-permute-start.2 = (f32[4,32,128]{2,1,0:T(8,128)S(1)}, f32[4,32,128]{2,1,0:T(8,128)S(1)}, u32[]{:S(2)}, u32[]{:S(2)}) collective-permute-start(f32[4,32,128]{2,1,0:T(8,128)S(1)} %get-tuple-element.38), channel_id=1, source_target_pairs={{16,0},{17,1},{18,2},{19,3},{20,4},{21,5},{22,6},{23,7},{24,8},{25... | collective-permute-start | bytes 196616 | tf_op jit(solution)/shard_map/ppermute | solution.py:606
  9.5 0.0 copy-done.2
  9.5 0.0 copy-start.1
  9.5 0.6 %shard_map.68 = (bf16[320,160]{1,0:T(8,128)(2,1)S(1)}, f32[19,128]{1,0:T(8,128)S(1)}) custom-call(f32[19,19]{1,0:T(8,128)S(1)} %copy-done.2), custom_call_target="tpu_custom_call" | custom-call | flops 1000000 | bytes 1000000 | tf_op jit(solution)/shard_map/pallas_call | solution.py:581
  10.1 4.2 %collective-permute-done.2.ga_ref = f32[4,32,128]{2,1,0:T(8,128)S(1)} collective-permute-done((f32[4,32,128]{2,1,0:T(8,128)S(1)}, f32[4,32,128]{2,1,0:T(8,128)S(1)}, u32[]{:S(2)}, u32[]{:S(2)}) %collective-permute-start.2) | collective-permute-done | bytes 65568 | tf_op jit(solution)/shard_map/ppermute | solution.py:606
  14.3 0.0 collective-permute-done.3.core_ref
  14.3 0.0 copy-done
  14.3 1.0 %shard_map.70 = (f32[19,5,8,128]{3,2,1,0:T(8,128)S(1)}, f32[3,5,8,128]{3,2,1,0:T(8,128)S(1)}, f32[2,5,8,128]{3,2,1,0:T(8,128)S(1)}, f32[4,8,8,128]{3,2,1,0:T(8,1...) custom-call(s32[3,128]{1,0:T(4,128)S(1)} %copy-done.1, f32[6,64,128]{2,1,0:T(8,128)S(1)} %bitcast.5, ...), custom_call_target="tpu_custom_call" | custom-call | flops 8000000 | bytes 1000000 | tf_op jit(solution)/shard_map/pallas_call | solution.py:581
  15.3 0.0 collective-permute-done.p_ref
  15.3 1.0 %shard_map.71 = (f32[536,128]{1,0:T(8,128)S(1)}, f32[19,8,128]{2,1,0:T(8,128)S(1)}) custom-call(bf16[320,160]{1,0:T(8,128)(2,1)S(1)} %get-tuple-element.34.react_ref, s32[3,128]{1,0:T(4,128)S(1)} %copy-done.1, f32[792,128]{1,0:T(8,128)S(1)} %get-tuple-element.35.pq_ref, f32[536,128]{1,0:T(8,128)S(1)} %collective-permute-done.p_ref, ...), custom_call_target="tpu_custom_call" | custom-call | flops 8000000 | bytes 1000000 | tf_op jit(solution)/shard_map/pallas_call | solution.py:581
  16.3 0.0 collective-permute-done.1.q_ref
  16.3 0.3 shard_map.72
  16.7 0.1 collective-permute-start.7
  16.7 3.6 %collective-permute-start.4 = (f32[536,128]{1,0:T(8,128)S(1)}, f32[536,128]{1,0:T(8,128)S(1)}, u32[]{:S(2)}, u32[]{:S(2)}) collective-permute-start(f32[536,128]{1,0:T(8,128)S(1)} %get-tuple-element.46.done_ref.chl_ref), channel_id=1, source_target_pairs={{0,15},{1,2},{2,1},{3,4},{4,3},{5,6},{6,5},{7,8},{8,7},{9,10},{10,... | collective-permute-start | bytes 823304 | tf_op jit(solution)/shard_map/ppermute | solution.py:606
  20.4 0.9 %collective-permute-start.5 = (f32[304,128]{1,0:T(8,128)S(1)}, f32[304,128]{1,0:T(8,128)S(1)}, u32[]{:S(2)}, u32[]{:S(2)}) collective-permute-start(f32[304,128]{1,0:T(8,128)S(1)} %get-tuple-element.50), channel_id=1, source_target_pairs={{0,15},{1,2},{2,1},{3,4},{4,3},{5,6},{6,5},{7,8},{8,7},{9,10},{10,... | collective-permute-start | bytes 466952 | tf_op jit(solution)/shard_map/ppermute | solution.py:606
  21.3 3.0 %collective-permute-start.8 = (f32[264,128]{1,0:T(8,128)S(1)}, f32[264,128]{1,0:T(8,128)S(1)}, u32[]{:S(2)}, u32[]{:S(2)}) collective-permute-start(f32[264,128]{1,0:T(8,128)S(1)} %get-tuple-element.59), channel_id=1, source_target_pairs={{0,16},{1,17},{2,18},{3,19},{4,20},{5,21},{6,22},{7,23},{8,24},{9,... | collective-permute-start | bytes 405512 | tf_op jit(solution)/shard_map/ppermute | solution.py:606
  24.2 0.1 collective-permute-start.6
  24.3 4.4 %collective-permute-done.6.gb_ref.refs_0_.over_ref = f32[4,40,128]{2,1,0:T(8,128)S(1)} collective-permute-done((f32[4,40,128]{2,1,0:T(8,128)S(1)}, f32[4,40,128]{2,1,0:T(8,128)S(1)}, u32[]{:S(2)}, u32[]{:S(2)}) %collective-permute-start.6) | collective-permute-done | bytes 81952 | tf_op jit(solution)/shard_map/ppermute | solution.py:606
  28.7 0.0 collective-permute-done.7.core_ref
  28.7 1.0 %shard_map.73 = (f32[19,5,8,128]{3,2,1,0:T(8,128)S(1)}, f32[3,5,8,128]{3,2,1,0:T(8,128)S(1)}, f32[2,5,8,128]{3,2,1,0:T(8,128)S(1)}, f32[4,8,8,128]{3,2,1,0:T(8,1...) custom-call(s32[3,128]{1,0:T(4,128)S(1)} %copy-done.1, ...), custom_call_target="tpu_custom_call" | custom-call | flops 8000000 | bytes 1000000 | tf_op jit(solution)/shard_map/pallas_call | solution.py:581
  29.7 0.0 collective-permute-done.4.p_ref
  29.7 0.5 %shard_map.75 = f32[32,128]{1,0:T(8,128)S(1)} custom-call(f32[19,128]{1,0:T(8,128)S(1)} %get-tuple-element.33.react_ref, s32[3,128]{1,0:T(4,128)S(1)} %copy-done.1, f32[840,128]{1,0:T(8,128)S(1)} %get-tuple-element.49.pq_ref, f32[536,128]{1,0:T(8,128)S(1)} %collective-permute-done.4.p_ref, f32[19,5,8,128]{3,2,1,0:T(8,128)S(1)} %get-tuple-element.52.part_ref, ...), custom_call_target="tpu_custom_call" | custom-call | flops 8000000 | bytes 1000000 | tf_op jit(solution)/shard_map/pallas_call | solution.py:581
  30.2 2.7 %collective-permute-start.9 = (f32[32,128]{1,0:T(8,128)S(1)}, f32[32,128]{1,0:T(8,128)S(1)}, u32[]{:S(2)}, u32[]{:S(2)}) collective-permute-start(f32[32,128]{1,0:T(8,128)S(1)} %shard_map.75), channel_id=1, source_target_pairs={{0,16},{1,17},{2,18},{3,19},{4,20},{5,21},{6,22},{7,23},{8,24},{9,... | collective-permute-start | bytes 49160 | tf_op jit(solution)/shard_map/ppermute | solution.py:606
  32.9 0.0 collective-permute-done.5.q_ref
  32.9 0.3 shard_map.74
  33.2 0.0 collective-permute-done.8.rest_ref
  33.2 1.1 %collective-permute-done.9.upper_ref = f32[32,128]{1,0:T(8,128)S(1)} collective-permute-done((f32[32,128]{1,0:T(8,128)S(1)}, f32[32,128]{1,0:T(8,128)S(1)}, u32[]{:S(2)}, u32[]{:S(2)}) %collective-permute-start.9) | collective-permute-done | bytes 16416 | tf_op jit(solution)/shard_map/ppermute | solution.py:606
  34.3 0.7 %shard_map.76 = (f32[6,64,128]{2,1,0:T(8,128)}, f32[64,128]{1,0:T(8,128)}) custom-call(f32[6,64,128]{2,1,0:T(8,128)S(1)} %get-tuple-element.58.ocean_ref, f32[4,40,128]{2,1,0:T(8,128)S(1)} %collective-permute-done.6.gb_ref.refs_0_.over_ref, f32[264,128]{1,0:T(8,128)S(1)} %collective-permute-done.8.rest_ref, f32[64,128]{1,0:T(8,128)S(1)} %get-tuple-element.60.chl_ref, ...), custom_call_target="tpu_custom_call" | custom-call | flops 1000000 | bytes 1000000 | tf_op jit(solution)/shard_map/pallas_call | solution.py:581
  (3 shorter events, 0.0 us)
Async XLA Ops:
  0.6 8.8 %copy-start.2 = (f32[19,19]{1,0:T(8,128)S(1)}, f32[19,19]{1,0:T(8,128)}, u32[]{:S(2)}) copy-start(f32[19,19]{1,0:T(8,128)} %r_ref.1) | copy-start | bytes 4336
  0.6 13.7 %copy-start = (f32[1,6,64,128]{3,2,1,0:T(8,128)S(1)}, f32[1,6,64,128]{3,2,1,0:T(8,128)}, u32[]{:S(2)}) copy-start(f32[1,6,64,128]{3,2,1,0:T(8,128)} %param.5) | copy-start | bytes 589828
  1.9 12.4 %collective-permute-start.3 = (f32[792,128]{1,0:T(8,128)S(1)}, f32[792,128]{1,0:T(8,128)S(1)}, u32[]{:S(2)}, u32[]{:S(2)}) collective-permute-start(f32[792,128]{1,0:T(8,128)S(1)} %get-tuple-element.35.pq_ref), channel_id=1, source_target_pairs={{0,1},{1,0},{2,3},{3,2},{4,5},{5,4},{6,7},{7,6},{8,9},{9,8},{10,11... | collective-permute-start | bytes 1216520 | tf_op jit(solution)/shard_map/ppermute | solution.py:606
  2.5 12.8 %collective-permute-start = (f32[536,128]{1,0:T(8,128)S(1)}, f32[536,128]{1,0:T(8,128)S(1)}, u32[]{:S(2)}, u32[]{:S(2)}) collective-permute-start(f32[536,128]{1,0:T(8,128)S(1)} %get-tuple-element.36), channel_id=1, source_target_pairs={{0,15},{1,2},{2,1},{3,4},{4,3},{5,6},{6,5},{7,8},{8,7},{9,10},{10,... | collective-permute-start | bytes 823304 | tf_op jit(solution)/shard_map/ppermute | solution.py:606
  8.1 8.2 %collective-permute-start.1 = (f32[256,128]{1,0:T(8,128)S(1)}, f32[256,128]{1,0:T(8,128)S(1)}, u32[]{:S(2)}, u32[]{:S(2)}) collective-permute-start(f32[256,128]{1,0:T(8,128)S(1)} %get-tuple-element.37), channel_id=1, source_target_pairs={{0,15},{1,2},{2,1},{3,4},{4,3},{5,6},{6,5},{7,8},{8,7},{9,10},{10,... | collective-permute-start | bytes 393224 | tf_op jit(solution)/shard_map/ppermute | solution.py:606
  8.2 6.1 %collective-permute-start.2 = (f32[4,32,128]{2,1,0:T(8,128)S(1)}, f32[4,32,128]{2,1,0:T(8,128)S(1)}, u32[]{:S(2)}, u32[]{:S(2)}) collective-permute-start(f32[4,32,128]{2,1,0:T(8,128)S(1)} %get-tuple-element.38), channel_id=1, source_target_pairs={{16,0},{17,1},{18,2},{19,3},{20,4},{21,5},{22,6},{23,7},{24,8},{25... | collective-permute-start | bytes 196616 | tf_op jit(solution)/shard_map/ppermute | solution.py:606
  9.5 4.9 %copy-start.1 = (s32[3,128]{1,0:T(4,128)S(1)}, s32[3,128]{1,0:T(4,128)}, u32[]{:S(2)}) copy-start(s32[3,128]{1,0:T(4,128)} %nb_ref.11) | copy-start | bytes 4612
  16.7 12.1 %collective-permute-start.7 = (f32[840,128]{1,0:T(8,128)S(1)}, f32[840,128]{1,0:T(8,128)S(1)}, u32[]{:S(2)}, u32[]{:S(2)}) collective-permute-start(f32[840,128]{1,0:T(8,128)S(1)} %get-tuple-element.49.pq_ref), channel_id=1, source_target_pairs={{0,1},{1,0},{2,3},{3,2},{4,5},{5,4},{6,7},{7,6},{8,9},{9,8},{10,11... | collective-permute-start | bytes 1290248 | tf_op jit(solution)/shard_map/ppermute | solution.py:606
  16.7 13.0 %collective-permute-start.4 = (f32[536,128]{1,0:T(8,128)S(1)}, f32[536,128]{1,0:T(8,128)S(1)}, u32[]{:S(2)}, u32[]{:S(2)}) collective-permute-start(f32[536,128]{1,0:T(8,128)S(1)} %get-tuple-element.46.done_ref.chl_ref), channel_id=1, source_target_pairs={{0,15},{1,2},{2,1},{3,4},{4,3},{5,6},{6,5},{7,8},{8,7},{9,10},{10,... | collective-permute-start | bytes 823304 | tf_op jit(solution)/shard_map/ppermute | solution.py:606
  20.4 12.5 %collective-permute-start.5 = (f32[304,128]{1,0:T(8,128)S(1)}, f32[304,128]{1,0:T(8,128)S(1)}, u32[]{:S(2)}, u32[]{:S(2)}) collective-permute-start(f32[304,128]{1,0:T(8,128)S(1)} %get-tuple-element.50), channel_id=1, source_target_pairs={{0,15},{1,2},{2,1},{3,4},{4,3},{5,6},{6,5},{7,8},{8,7},{9,10},{10,... | collective-permute-start | bytes 466952 | tf_op jit(solution)/shard_map/ppermute | solution.py:606
  21.3 12.0 %collective-permute-start.8 = (f32[264,128]{1,0:T(8,128)S(1)}, f32[264,128]{1,0:T(8,128)S(1)}, u32[]{:S(2)}, u32[]{:S(2)}) collective-permute-start(f32[264,128]{1,0:T(8,128)S(1)} %get-tuple-element.59), channel_id=1, source_target_pairs={{0,16},{1,17},{2,18},{3,19},{4,20},{5,21},{6,22},{7,23},{8,24},{9,... | collective-permute-start | bytes 405512 | tf_op jit(solution)/shard_map/ppermute | solution.py:606
  24.2 4.5 %collective-permute-start.6 = (f32[4,40,128]{2,1,0:T(8,128)S(1)}, f32[4,40,128]{2,1,0:T(8,128)S(1)}, u32[]{:S(2)}, u32[]{:S(2)}) collective-permute-start(f32[4,40,128]{2,1,0:T(8,128)S(1)} %get-tuple-element.51), channel_id=1, source_target_pairs={{0,16},{1,17},{2,18},{3,19},{4,20},{5,21},{6,22},{7,23},{8,24},{9,... | collective-permute-start | bytes 245768 | tf_op jit(solution)/shard_map/ppermute | solution.py:606
  30.2 4.1 %collective-permute-start.9 = (f32[32,128]{1,0:T(8,128)S(1)}, f32[32,128]{1,0:T(8,128)S(1)}, u32[]{:S(2)}, u32[]{:S(2)}) collective-permute-start(f32[32,128]{1,0:T(8,128)S(1)} %shard_map.75), channel_id=1, source_target_pairs={{0,16},{1,17},{2,18},{3,19},{4,20},{5,21},{6,22},{7,23},{8,24},{9,... | collective-permute-start | bytes 49160 | tf_op jit(solution)/shard_map/ppermute | solution.py:606

commit v4 on v3

--- a/solution.py
+++ b/solution.py
@@ -598,8 +598,8 @@
     return pairs
 
 
-def over_comp(sources, tiles):
-    return [(c * tiles + t, (1 - c) * tiles + t) for c in sources for t in range(tiles)]
+def over_comp(tiles):
+    return [(c * tiles + t, (1 - c) * tiles + t) for c in (0, 1) for t in range(tiles)]
 
 
 def sent(v, pairs):
@@ -649,7 +649,7 @@
         ],
     )
     cross_p = sent(p, across)
-    lagged = sent(top_fields, over_comp((1,), tiles))
+    lagged = sent(top_fields, over_comp(tiles))
     core = sent(pq, within)
     cross_q = sent(q, across)
     n = -(-nt // 2) * 2 * SUB
@@ -684,10 +684,10 @@
         scratch=h_scratch + w_scratch,
         cost=8_000_000,
     )
-    over = sent(over_one, over_comp((0, 1), tiles))
+    over = sent(over_one, over_comp(tiles))
     core_one = sent(pq_one, within)
     cross_q_one = sent(q_one, across)
-    rest = sent(rest_one, over_comp((0,), tiles))
+    rest = sent(rest_one, over_comp(tiles))
 
     *near, chl_one = call(
         kernel(near_kernel, True),
@@ -702,7 +702,7 @@
         scratch=h_scratch,
         cost=8_000_000,
     )
-    upper = sent(upper, over_comp((0,), tiles))
+    upper = sent(upper, over_comp(tiles))
     ocean_two, mine = call(
         kernel(second_kernel),
         (shape_of(nf, lev, cols), shape_of(lev - tall, cols)),

time: 35.2 us -> 32.9 us (0.935)
  starting transfers between devices: 17.8 us -> 15.4 us
    ppermute x10, starting transfers between devices: 17.8 us -> 15.4 us  [sent(): return lax.ppermute(v, AXES, pairs)]
  transfers between devices with their start and end apart: 10 -> 10, of which waited for: 3 -> 4; matrix products, arithmetic and copies ran while one was open for 0% -> 0% of each run, Pallas kernels for 12% -> 13%
where the time goes in v4:
time: 32.9 us; the launch traced here: 32.7 us
  starting transfers between devices  15.4 us (47%)
  waiting for transfers between devices  10 us (30%)
  Pallas kernels  6.58 us (20%)
  between operations  0.74 us (2%)
    ppermute x10, starting transfers between devices, sent(): return lax.ppermute(v, AXES, pairs)  15.4 us
    ppermute x10, waiting for transfers between devices, sent(): return lax.ppermute(v, AXES, pairs)  10 us
    pallas_call x9, Pallas kernels, call(): pl.pallas_call(kernel, out_shape=outs, in_specs=specs or [VMEM] * len(ins...  6.58 us
  transfers between devices with their start and end apart: 10, of which 4 were waited for; matrix products, arithmetic and copies ran while one was open for 0% of the time, Pallas kernels for 13%

profile of v4, /device:TPU:0, one launch (start us, length us, event | category | flops | bytes accessed | tf_op | source)
XLA Modules:
  0.0 32.7 jit_solution(10867642460892546073)
XLA Ops:
  0.6 0.0 copy-start.2
  0.6 0.0 copy-start
  0.7 1.3 %shard_map.69 = (f32[536,128]{1,0:T(8,128)S(1)}, f32[256,128]{1,0:T(8,128)S(1)}, f32[792,128]{1,0:T(8,128)S(1)}, f32[4,32,128]{2,1,0:T(8,128)S(1)}, f32[64,128]{1,0:T(8,128)S(1)}) custom-call(s32[1,128]{1,0:T(1,128)} %bitcast.8, f32[6,64,128]{2,1,0:T(8,128)} %bitcast.4, f32[19,64,128]{2,1,0:T(8,128)} %t_ref.1), custom_call_target="tpu_custom_call" | custom-call | flops 1000000 | bytes 1000000 | tf_op jit(solution)/shard_map/pallas_call | solution.py:581
  1.9 0.6 %collective-permute-start.3 = (f32[792,128]{1,0:T(8,128)S(1)}, f32[792,128]{1,0:T(8,128)S(1)}, u32[]{:S(2)}, u32[]{:S(2)}) collective-permute-start(f32[792,128]{1,0:T(8,128)S(1)} %get-tuple-element.35.pq_ref), channel_id=1, source_target_pairs={{0,1},{1,0},{2,3},{3,2},{4,5},{5,4},{6,7},{7,6},{8,9},{9,8},{10,11... | collective-permute-start | bytes 1216520 | tf_op jit(solution)/shard_map/ppermute | solution.py:606
  2.5 5.7 %collective-permute-start = (f32[536,128]{1,0:T(8,128)S(1)}, f32[536,128]{1,0:T(8,128)S(1)}, u32[]{:S(2)}, u32[]{:S(2)}) collective-permute-start(f32[536,128]{1,0:T(8,128)S(1)} %get-tuple-element.36), channel_id=1, source_target_pairs={{0,15},{1,2},{2,1},{3,4},{4,3},{5,6},{6,5},{7,8},{8,7},{9,10},{10,... | collective-permute-start | bytes 823304 | tf_op jit(solution)/shard_map/ppermute | solution.py:606
  8.1 0.0 collective-permute-start.1
  8.2 1.5 %collective-permute-start.2 = (f32[4,32,128]{2,1,0:T(8,128)S(1)}, f32[4,32,128]{2,1,0:T(8,128)S(1)}, u32[]{:S(2)}, u32[]{:S(2)}) collective-permute-start(f32[4,32,128]{2,1,0:T(8,128)S(1)} %get-tuple-element.38), channel_id=1, source_target_pairs={{0,16},{1,17},{2,18},{3,19},{4,20},{5,21},{6,22},{7,23},{8,24},{9,... | collective-permute-start | bytes 196616 | tf_op jit(solution)/shard_map/ppermute | solution.py:606
  9.7 0.6 %shard_map.68 = (bf16[320,160]{1,0:T(8,128)(2,1)S(1)}, f32[19,128]{1,0:T(8,128)S(1)}) custom-call(f32[19,19]{1,0:T(8,128)S(1)} %copy-done.2), custom_call_target="tpu_custom_call" | custom-call | flops 1000000 | bytes 1000000 | tf_op jit(solution)/shard_map/pallas_call | solution.py:581
  10.3 2.2 %collective-permute-done.2.ga_ref = f32[4,32,128]{2,1,0:T(8,128)S(1)} collective-permute-done((f32[4,32,128]{2,1,0:T(8,128)S(1)}, f32[4,32,128]{2,1,0:T(8,128)S(1)}, u32[]{:S(2)}, u32[]{:S(2)}) %collective-permute-start.2) | collective-permute-done | bytes 65568 | tf_op jit(solution)/shard_map/ppermute | solution.py:606
  12.4 0.0 collective-permute-done.3.core_ref
  12.4 0.0 copy-done
  12.5 1.0 %shard_map.70 = (f32[19,5,8,128]{3,2,1,0:T(8,128)S(1)}, f32[3,5,8,128]{3,2,1,0:T(8,128)S(1)}, f32[2,5,8,128]{3,2,1,0:T(8,128)S(1)}, f32[4,8,8,128]{3,2,1,0:T(8,1...) custom-call(s32[3,128]{1,0:T(4,128)S(1)} %copy-done.1, f32[6,64,128]{2,1,0:T(8,128)S(1)} %bitcast.5, ...), custom_call_target="tpu_custom_call" | custom-call | flops 8000000 | bytes 1000000 | tf_op jit(solution)/shard_map/pallas_call | solution.py:581
  13.4 0.0 collective-permute-done.p_ref
  13.5 1.0 %shard_map.71 = (f32[536,128]{1,0:T(8,128)S(1)}, f32[19,8,128]{2,1,0:T(8,128)S(1)}) custom-call(bf16[320,160]{1,0:T(8,128)(2,1)S(1)} %get-tuple-element.34.react_ref, s32[3,128]{1,0:T(4,128)S(1)} %copy-done.1, f32[792,128]{1,0:T(8,128)S(1)} %get-tuple-element.35.pq_ref, f32[536,128]{1,0:T(8,128)S(1)} %collective-permute-done.p_ref, ...), custom_call_target="tpu_custom_call" | custom-call | flops 8000000 | bytes 1000000 | tf_op jit(solution)/shard_map/pallas_call | solution.py:581
  14.4 0.9 %collective-permute-done.1.q_ref = f32[256,128]{1,0:T(8,128)S(1)} collective-permute-done((f32[256,128]{1,0:T(8,128)S(1)}, f32[256,128]{1,0:T(8,128)S(1)}, u32[]{:S(2)}, u32[]{:S(2)}) %collective-permute-start.1) | collective-permute-done | bytes 131104 | tf_op jit(solution)/shard_map/ppermute | solution.py:606
  15.3 0.3 shard_map.72
  15.6 0.1 collective-permute-start.7
  15.7 4.6 %collective-permute-start.4 = (f32[536,128]{1,0:T(8,128)S(1)}, f32[536,128]{1,0:T(8,128)S(1)}, u32[]{:S(2)}, u32[]{:S(2)}) collective-permute-start(f32[536,128]{1,0:T(8,128)S(1)} %get-tuple-element.46.done_ref.chl_ref), channel_id=1, source_target_pairs={{0,15},{1,2},{2,1},{3,4},{4,3},{5,6},{6,5},{7,8},{8,7},{9,10},{10,... | collective-permute-start | bytes 823304 | tf_op jit(solution)/shard_map/ppermute | solution.py:606
  20.3 0.0 collective-permute-start.5
  20.3 2.0 %collective-permute-start.8 = (f32[264,128]{1,0:T(8,128)S(1)}, f32[264,128]{1,0:T(8,128)S(1)}, u32[]{:S(2)}, u32[]{:S(2)}) collective-permute-start(f32[264,128]{1,0:T(8,128)S(1)} %get-tuple-element.59), channel_id=1, source_target_pairs={{0,16},{1,17},{2,18},{3,19},{4,20},{5,21},{6,22},{7,23},{8,24},{9,... | collective-permute-start | bytes 405512 | tf_op jit(solution)/shard_map/ppermute | solution.py:606
  22.3 0.0 collective-permute-start.6
  22.4 4.4 %collective-permute-done.6.gb_ref.refs_0_.over_ref = f32[4,40,128]{2,1,0:T(8,128)S(1)} collective-permute-done((f32[4,40,128]{2,1,0:T(8,128)S(1)}, f32[4,40,128]{2,1,0:T(8,128)S(1)}, u32[]{:S(2)}, u32[]{:S(2)}) %collective-permute-start.6) | collective-permute-done | bytes 81952 | tf_op jit(solution)/shard_map/ppermute | solution.py:606
  26.8 0.0 collective-permute-done.7.core_ref
  26.8 1.0 %shard_map.73 = (f32[19,5,8,128]{3,2,1,0:T(8,128)S(1)}, f32[3,5,8,128]{3,2,1,0:T(8,128)S(1)}, f32[2,5,8,128]{3,2,1,0:T(8,128)S(1)}, f32[4,8,8,128]{3,2,1,0:T(8,1...) custom-call(s32[3,128]{1,0:T(4,128)S(1)} %copy-done.1, ...), custom_call_target="tpu_custom_call" | custom-call | flops 8000000 | bytes 1000000 | tf_op jit(solution)/shard_map/pallas_call | solution.py:581
  27.7 0.0 collective-permute-done.4.p_ref
  27.8 0.5 %shard_map.75 = f32[32,128]{1,0:T(8,128)S(1)} custom-call(f32[19,128]{1,0:T(8,128)S(1)} %get-tuple-element.33.react_ref, s32[3,128]{1,0:T(4,128)S(1)} %copy-done.1, f32[840,128]{1,0:T(8,128)S(1)} %get-tuple-element.49.pq_ref, f32[536,128]{1,0:T(8,128)S(1)} %collective-permute-done.4.p_ref, f32[19,5,8,128]{3,2,1,0:T(8,128)S(1)} %get-tuple-element.52.part_ref, ...), custom_call_target="tpu_custom_call" | custom-call | flops 8000000 | bytes 1000000 | tf_op jit(solution)/shard_map/pallas_call | solution.py:581
  28.2 0.9 %collective-permute-start.9 = (f32[32,128]{1,0:T(8,128)S(1)}, f32[32,128]{1,0:T(8,128)S(1)}, u32[]{:S(2)}, u32[]{:S(2)}) collective-permute-start(f32[32,128]{1,0:T(8,128)S(1)} %shard_map.75), channel_id=1, source_target_pairs={{0,16},{1,17},{2,18},{3,19},{4,20},{5,21},{6,22},{7,23},{8,24},{9,... | collective-permute-start | bytes 49160 | tf_op jit(solution)/shard_map/ppermute | solution.py:606
  29.1 0.0 collective-permute-done.5.q_ref
  29.1 0.3 shard_map.74
  29.5 0.0 collective-permute-done.8.rest_ref
  29.5 2.5 %collective-permute-done.9.upper_ref = f32[32,128]{1,0:T(8,128)S(1)} collective-permute-done((f32[32,128]{1,0:T(8,128)S(1)}, f32[32,128]{1,0:T(8,128)S(1)}, u32[]{:S(2)}, u32[]{:S(2)}) %collective-permute-start.9) | collective-permute-done | bytes 16416 | tf_op jit(solution)/shard_map/ppermute | solution.py:606
  32.0 0.7 %shard_map.76 = (f32[6,64,128]{2,1,0:T(8,128)}, f32[64,128]{1,0:T(8,128)}) custom-call(f32[6,64,128]{2,1,0:T(8,128)S(1)} %get-tuple-element.58.ocean_ref, f32[4,40,128]{2,1,0:T(8,128)S(1)} %collective-permute-done.6.gb_ref.refs_0_.over_ref, f32[264,128]{1,0:T(8,128)S(1)} %collective-permute-done.8.rest_ref, f32[64,128]{1,0:T(8,128)S(1)} %get-tuple-element.60.chl_ref, ...), custom_call_target="tpu_custom_call" | custom-call | flops 1000000 | bytes 1000000 | tf_op jit(solution)/shard_map/pallas_call | solution.py:581
  (3 shorter events, 0.0 us)
Async XLA Ops:
  0.6 9.0 %copy-start.2 = (f32[19,19]{1,0:T(8,128)S(1)}, f32[19,19]{1,0:T(8,128)}, u32[]{:S(2)}) copy-start(f32[19,19]{1,0:T(8,128)} %r_ref.1) | copy-start | bytes 4336
  0.6 11.8 %copy-start = (f32[1,6,64,128]{3,2,1,0:T(8,128)S(1)}, f32[1,6,64,128]{3,2,1,0:T(8,128)}, u32[]{:S(2)}) copy-start(f32[1,6,64,128]{3,2,1,0:T(8,128)} %param.5) | copy-start | bytes 589828
  1.9 10.5 %collective-permute-start.3 = (f32[792,128]{1,0:T(8,128)S(1)}, f32[792,128]{1,0:T(8,128)S(1)}, u32[]{:S(2)}, u32[]{:S(2)}) collective-permute-start(f32[792,128]{1,0:T(8,128)S(1)} %get-tuple-element.35.pq_ref), channel_id=1, source_target_pairs={{0,1},{1,0},{2,3},{3,2},{4,5},{5,4},{6,7},{7,6},{8,9},{9,8},{10,11... | collective-permute-start | bytes 1216520 | tf_op jit(solution)/shard_map/ppermute | solution.py:606
  2.5 11.0 %collective-permute-start = (f32[536,128]{1,0:T(8,128)S(1)}, f32[536,128]{1,0:T(8,128)S(1)}, u32[]{:S(2)}, u32[]{:S(2)}) collective-permute-start(f32[536,128]{1,0:T(8,128)S(1)} %get-tuple-element.36), channel_id=1, source_target_pairs={{0,15},{1,2},{2,1},{3,4},{4,3},{5,6},{6,5},{7,8},{8,7},{9,10},{10,... | collective-permute-start | bytes 823304 | tf_op jit(solution)/shard_map/ppermute | solution.py:606
  8.1 7.2 %collective-permute-start.1 = (f32[256,128]{1,0:T(8,128)S(1)}, f32[256,128]{1,0:T(8,128)S(1)}, u32[]{:S(2)}, u32[]{:S(2)}) collective-permute-start(f32[256,128]{1,0:T(8,128)S(1)} %get-tuple-element.37), channel_id=1, source_target_pairs={{0,15},{1,2},{2,1},{3,4},{4,3},{5,6},{6,5},{7,8},{8,7},{9,10},{10,... | collective-permute-start | bytes 393224 | tf_op jit(solution)/shard_map/ppermute | solution.py:606
  8.2 4.3 %collective-permute-start.2 = (f32[4,32,128]{2,1,0:T(8,128)S(1)}, f32[4,32,128]{2,1,0:T(8,128)S(1)}, u32[]{:S(2)}, u32[]{:S(2)}) collective-permute-start(f32[4,32,128]{2,1,0:T(8,128)S(1)} %get-tuple-element.38), channel_id=1, source_target_pairs={{0,16},{1,17},{2,18},{3,19},{4,20},{5,21},{6,22},{7,23},{8,24},{9,... | collective-permute-start | bytes 196616 | tf_op jit(solution)/shard_map/ppermute | solution.py:606
  9.7 2.8 %copy-start.1 = (s32[3,128]{1,0:T(4,128)S(1)}, s32[3,128]{1,0:T(4,128)}, u32[]{:S(2)}) copy-start(s32[3,128]{1,0:T(4,128)} %nb_ref.11) | copy-start | bytes 4612
  15.6 11.1 %collective-permute-start.7 = (f32[840,128]{1,0:T(8,128)S(1)}, f32[840,128]{1,0:T(8,128)S(1)}, u32[]{:S(2)}, u32[]{:S(2)}) collective-permute-start(f32[840,128]{1,0:T(8,128)S(1)} %get-tuple-element.49.pq_ref), channel_id=1, source_target_pairs={{0,1},{1,0},{2,3},{3,2},{4,5},{5,4},{6,7},{7,6},{8,9},{9,8},{10,11... | collective-permute-start | bytes 1290248 | tf_op jit(solution)/shard_map/ppermute | solution.py:606
  15.7 12.0 %collective-permute-start.4 = (f32[536,128]{1,0:T(8,128)S(1)}, f32[536,128]{1,0:T(8,128)S(1)}, u32[]{:S(2)}, u32[]{:S(2)}) collective-permute-start(f32[536,128]{1,0:T(8,128)S(1)} %get-tuple-element.46.done_ref.chl_ref), channel_id=1, source_target_pairs={{0,15},{1,2},{2,1},{3,4},{4,3},{5,6},{6,5},{7,8},{8,7},{9,10},{10,... | collective-permute-start | bytes 823304 | tf_op jit(solution)/shard_map/ppermute | solution.py:606
  20.3 8.9 %collective-permute-start.5 = (f32[304,128]{1,0:T(8,128)S(1)}, f32[304,128]{1,0:T(8,128)S(1)}, u32[]{:S(2)}, u32[]{:S(2)}) collective-permute-start(f32[304,128]{1,0:T(8,128)S(1)} %get-tuple-element.50), channel_id=1, source_target_pairs={{0,15},{1,2},{2,1},{3,4},{4,3},{5,6},{6,5},{7,8},{8,7},{9,10},{10,... | collective-permute-start | bytes 466952 | tf_op jit(solution)/shard_map/ppermute | solution.py:606
  20.3 9.1 %collective-permute-start.8 = (f32[264,128]{1,0:T(8,128)S(1)}, f32[264,128]{1,0:T(8,128)S(1)}, u32[]{:S(2)}, u32[]{:S(2)}) collective-permute-start(f32[264,128]{1,0:T(8,128)S(1)} %get-tuple-element.59), channel_id=1, source_target_pairs={{0,16},{1,17},{2,18},{3,19},{4,20},{5,21},{6,22},{7,23},{8,24},{9,... | collective-permute-start | bytes 405512 | tf_op jit(solution)/shard_map/ppermute | solution.py:606
  22.3 4.4 %collective-permute-start.6 = (f32[4,40,128]{2,1,0:T(8,128)S(1)}, f32[4,40,128]{2,1,0:T(8,128)S(1)}, u32[]{:S(2)}, u32[]{:S(2)}) collective-permute-start(f32[4,40,128]{2,1,0:T(8,128)S(1)} %get-tuple-element.51), channel_id=1, source_target_pairs={{0,16},{1,17},{2,18},{3,19},{4,20},{5,21},{6,22},{7,23},{8,24},{9,... | collective-permute-start | bytes 245768 | tf_op jit(solution)/shard_map/ppermute | solution.py:606
  28.2 3.8 %collective-permute-start.9 = (f32[32,128]{1,0:T(8,128)S(1)}, f32[32,128]{1,0:T(8,128)S(1)}, u32[]{:S(2)}, u32[]{:S(2)}) collective-permute-start(f32[32,128]{1,0:T(8,128)S(1)} %shard_map.75), channel_id=1, source_target_pairs={{0,16},{1,17},{2,18},{3,19},{4,20},{5,21},{6,22},{7,23},{8,24},{9,... | collective-permute-start | bytes 49160 | tf_op jit(solution)/shard_map/ppermute | solution.py:606

commit v5 on v4

--- a/solution.py
+++ b/solution.py
@@ -34,10 +34,8 @@
         self.halves = SUB * nt * self.full
         self.wet = self.halves + self.half * nt
         self.p_rows = -(-(self.wet + self.half) // SUB) * SUB
-        self.q_rows = (
-            max(4 * lev, -(-(SUB + self.half) * nt // SUB) * SUB),
-            max(4 * lev, 2 * SUB * nt),
-        )
+        self.edges = (SUB + self.half) * nt
+        self.q_rows = max(4 * lev, -(-(self.edges + nt + SUB) // SUB) * SUB)
 
     def rs(self, comp):
         return list(range(1 - comp, self.window))
@@ -54,13 +52,15 @@
             return p(SUB * (self.full * j + r - 1)) if r <= self.full else p(self.halves + self.half * j)
         if r < self.full:
             return p(SUB * (self.full * j + r))
-        if second:
-            return q(SUB * (2 * j + r - self.full))
         if r > self.full:
             return q(SUB * j)
         upper = p(self.halves + self.half * j)
         lower = q(SUB * self.nt + self.half * (j - 1))
         sub = lax.broadcasted_iota(jnp.int32, upper.shape, 0)
+        if second:
+            edge = self.half - 1
+            lower = jnp.where(sub == edge, q(self.edges + j - edge), lower)
+            return jnp.where(sub < edge, upper, lower)
         return jnp.where(sub < self.half, upper, lower)
 
 
@@ -399,7 +399,7 @@
     @on_side(1)
     def _():
         work = Far(plan, 1, False, *refs)
-        work.clear(-1, None)
+        work.clear(-1, plan.full + 1)
         lower = lambda offset: jnp.zeros((SUB, work.cols), F32)
         for r in range(plan.full + 1):
             work.move(r, p, lower)
@@ -408,10 +408,14 @@
             edge_ref[j] = h_ref[j, at : at + SUB, :]
 
         def put(i, r, value):
-            at = SUB * (plan.full * i + r)
-            out_ref[at : at + SUB, :] = value
-
-        for r in range(plan.full):
+            if r < plan.full:
+                at = SUB * (plan.full * i + r)
+                out_ref[at : at + SUB, :] = value
+            else:
+                at = plan.halves + plan.half * i
+                out_ref[at : at + plan.half, :] = value[0 : plan.half]
+
+        for r in range(plan.full + 1):
             work.react(r, react_ref, put)
 
 
@@ -502,9 +506,14 @@
             work.move(r, rows_at(p_ref), rows_at(q_ref))
 
         def put(i, r, value):
-            at = SUB * (2 * i + r - plan.full)
-            out_ref[at : at + SUB, :] = value
-            both_ref[plan.p_rows + at : plan.p_rows + at + SUB, :] = value
+            for ref, base in ((out_ref, 0), (both_ref, plan.p_rows)):
+                if r > plan.full:
+                    ref[base + SUB * i : base + SUB * (i + 1), :] = value
+                else:
+                    at = base + SUB * plan.nt + plan.half * i
+                    ref[at : at + plan.half, :] = value[plan.half :]
+                    at = base + plan.edges + i
+                    ref[at : at + 1, :] = value[plan.half - 1 : plan.half]
             if i == 0:
                 over_ref[0, SUB * r : SUB * (r + 1), :] = value
 
@@ -632,8 +641,8 @@
         kernel(pack_kernel),
         (
             shape_of(p_rows, cols),
-            shape_of(plan.q_rows[0], cols),
-            shape_of(p_rows + plan.q_rows[0], cols),
+            shape_of(plan.q_rows, cols),
+            shape_of(p_rows + plan.q_rows, cols),
             shape_of(4, top, cols),
             shape_of(lev, cols),
         ),
@@ -674,8 +683,8 @@
     q_one, pq_one, ocean_one, over_one, rest_one = call(
         kernel(lower_kernel),
         (
-            shape_of(plan.q_rows[1], cols),
-            shape_of(p_rows + plan.q_rows[1], cols),
+            shape_of(plan.q_rows, cols),
+            shape_of(p_rows + plan.q_rows, cols),
             shape_of(nf, lev, cols),
             shape_of(4, lev - tall, cols),
             shape_of(3 * (lev + tall), cols),

time: 32.9 us -> 32.7 us (level)
  transfers between devices with their start and end apart: 10 -> 10, of which waited for: 4 -> 5; matrix products, arithmetic and copies ran while one was open for 0% -> 0% of each run, Pallas kernels for 13% -> 13%
where the time goes in v5:
time: 32.7 us; the launch traced here: 32.5 us
  starting transfers between devices  15.3 us (47%)
  waiting for transfers between devices  9.85 us (30%)
  Pallas kernels  6.58 us (20%)
  between operations  0.74 us (2%)
    ppermute x10, starting transfers between devices, sent(): return lax.ppermute(v, AXES, pairs)  15.3 us
    ppermute x10, waiting for transfers between devices, sent(): return lax.ppermute(v, AXES, pairs)  9.85 us
    pallas_call x9, Pallas kernels, call(): pl.pallas_call(kernel, out_shape=outs, in_specs=specs or [VMEM] * len(ins...  6.58 us
  transfers between devices with their start and end apart: 10, of which 5 were waited for; matrix products, arithmetic and copies ran while one was open for 0% of the time, Pallas kernels for 13%

profile of v5, /device:TPU:0, one launch (start us, length us, event | category | flops | bytes accessed | tf_op | source)
XLA Modules:
  0.0 32.5 jit_solution(3700847643268769871)
XLA Ops:
  0.6 0.0 copy-start.2
  0.6 0.0 copy-start
  0.7 1.3 %shard_map.69 = (f32[536,128]{1,0:T(8,128)S(1)}, f32[256,128]{1,0:T(8,128)S(1)}, f32[792,128]{1,0:T(8,128)S(1)}, f32[4,32,128]{2,1,0:T(8,128)S(1)}, f32[64,128]{1,0:T(8,128)S(1)}) custom-call(s32[1,128]{1,0:T(1,128)} %bitcast.8, f32[6,64,128]{2,1,0:T(8,128)} %bitcast.4, f32[19,64,128]{2,1,0:T(8,128)} %t_ref.1), custom_call_target="tpu_custom_call" | custom-call | flops 1000000 | bytes 1000000 | tf_op jit(solution)/shard_map/pallas_call | solution.py:590
  1.9 0.6 %collective-permute-start.3 = (f32[792,128]{1,0:T(8,128)S(1)}, f32[792,128]{1,0:T(8,128)S(1)}, u32[]{:S(2)}, u32[]{:S(2)}) collective-permute-start(f32[792,128]{1,0:T(8,128)S(1)} %get-tuple-element.35.pq_ref), channel_id=1, source_target_pairs={{0,1},{1,0},{2,3},{3,2},{4,5},{5,4},{6,7},{7,6},{8,9},{9,8},{10,11... | collective-permute-start | bytes 1216520 | tf_op jit(solution)/shard_map/ppermute | solution.py:615
  2.5 5.7 %collective-permute-start = (f32[536,128]{1,0:T(8,128)S(1)}, f32[536,128]{1,0:T(8,128)S(1)}, u32[]{:S(2)}, u32[]{:S(2)}) collective-permute-start(f32[536,128]{1,0:T(8,128)S(1)} %get-tuple-element.36), channel_id=1, source_target_pairs={{0,15},{1,2},{2,1},{3,4},{4,3},{5,6},{6,5},{7,8},{8,7},{9,10},{10,... | collective-permute-start | bytes 823304 | tf_op jit(solution)/shard_map/ppermute | solution.py:615
  8.1 0.0 collective-permute-start.1
  8.2 1.5 %collective-permute-start.2 = (f32[4,32,128]{2,1,0:T(8,128)S(1)}, f32[4,32,128]{2,1,0:T(8,128)S(1)}, u32[]{:S(2)}, u32[]{:S(2)}) collective-permute-start(f32[4,32,128]{2,1,0:T(8,128)S(1)} %get-tuple-element.38), channel_id=1, source_target_pairs={{0,16},{1,17},{2,18},{3,19},{4,20},{5,21},{6,22},{7,23},{8,24},{9,... | collective-permute-start | bytes 196616 | tf_op jit(solution)/shard_map/ppermute | solution.py:615
  9.7 0.6 %shard_map.68 = (bf16[320,160]{1,0:T(8,128)(2,1)S(1)}, f32[19,128]{1,0:T(8,128)S(1)}) custom-call(f32[19,19]{1,0:T(8,128)S(1)} %copy-done.2), custom_call_target="tpu_custom_call" | custom-call | flops 1000000 | bytes 1000000 | tf_op jit(solution)/shard_map/pallas_call | solution.py:590
  10.3 2.2 %collective-permute-done.2.ga_ref = f32[4,32,128]{2,1,0:T(8,128)S(1)} collective-permute-done((f32[4,32,128]{2,1,0:T(8,128)S(1)}, f32[4,32,128]{2,1,0:T(8,128)S(1)}, u32[]{:S(2)}, u32[]{:S(2)}) %collective-permute-start.2) | collective-permute-done | bytes 65568 | tf_op jit(solution)/shard_map/ppermute | solution.py:615
  12.4 0.0 collective-permute-done.3.core_ref
  12.4 0.0 copy-done
  12.5 1.0 %shard_map.70 = (f32[19,5,8,128]{3,2,1,0:T(8,128)S(1)}, f32[3,5,8,128]{3,2,1,0:T(8,128)S(1)}, f32[2,5,8,128]{3,2,1,0:T(8,128)S(1)}, f32[4,8,8,128]{3,2,1,0:T(8,1...) custom-call(s32[3,128]{1,0:T(4,128)S(1)} %copy-done.1, f32[6,64,128]{2,1,0:T(8,128)S(1)} %bitcast.5, ...), custom_call_target="tpu_custom_call" | custom-call | flops 8000000 | bytes 1000000 | tf_op jit(solution)/shard_map/pallas_call | solution.py:590
  13.4 0.0 collective-permute-done.p_ref
  13.5 1.0 %shard_map.71 = (f32[536,128]{1,0:T(8,128)S(1)}, f32[19,8,128]{2,1,0:T(8,128)S(1)}) custom-call(bf16[320,160]{1,0:T(8,128)(2,1)S(1)} %get-tuple-element.34.react_ref, s32[3,128]{1,0:T(4,128)S(1)} %copy-done.1, f32[792,128]{1,0:T(8,128)S(1)} %get-tuple-element.35.pq_ref, f32[536,128]{1,0:T(8,128)S(1)} %collective-permute-done.p_ref, ...), custom_call_target="tpu_custom_call" | custom-call | flops 8000000 | bytes 1000000 | tf_op jit(solution)/shard_map/pallas_call | solution.py:590
  14.4 0.9 %collective-permute-done.1.q_ref = f32[256,128]{1,0:T(8,128)S(1)} collective-permute-done((f32[256,128]{1,0:T(8,128)S(1)}, f32[256,128]{1,0:T(8,128)S(1)}, u32[]{:S(2)}, u32[]{:S(2)}) %collective-permute-start.1) | collective-permute-done | bytes 131104 | tf_op jit(solution)/shard_map/ppermute | solution.py:615
  15.3 0.3 shard_map.72
  15.6 0.1 collective-permute-start.7
  15.7 4.6 %collective-permute-start.4 = (f32[536,128]{1,0:T(8,128)S(1)}, f32[536,128]{1,0:T(8,128)S(1)}, u32[]{:S(2)}, u32[]{:S(2)}) collective-permute-start(f32[536,128]{1,0:T(8,128)S(1)} %get-tuple-element.46.done_ref.chl_ref), channel_id=1, source_target_pairs={{0,15},{1,2},{2,1},{3,4},{4,3},{5,6},{6,5},{7,8},{8,7},{9,10},{10,... | collective-permute-start | bytes 823304 | tf_op jit(solution)/shard_map/ppermute | solution.py:615
  20.3 1.8 %collective-permute-start.8 = (f32[264,128]{1,0:T(8,128)S(1)}, f32[264,128]{1,0:T(8,128)S(1)}, u32[]{:S(2)}, u32[]{:S(2)}) collective-permute-start(f32[264,128]{1,0:T(8,128)S(1)} %get-tuple-element.59), channel_id=1, source_target_pairs={{0,16},{1,17},{2,18},{3,19},{4,20},{5,21},{6,22},{7,23},{8,24},{9,... | collective-permute-start | bytes 405512 | tf_op jit(solution)/shard_map/ppermute | solution.py:615
  22.1 0.0 collective-permute-start.5
  22.1 0.2 collective-permute-start.6
  22.3 4.2 %collective-permute-done.6.gb_ref.refs_0_.over_ref = f32[4,40,128]{2,1,0:T(8,128)S(1)} collective-permute-done((f32[4,40,128]{2,1,0:T(8,128)S(1)}, f32[4,40,128]{2,1,0:T(8,128)S(1)}, u32[]{:S(2)}, u32[]{:S(2)}) %collective-permute-start.6) | collective-permute-done | bytes 81952 | tf_op jit(solution)/shard_map/ppermute | solution.py:615
  26.6 0.0 collective-permute-done.7.core_ref
  26.6 1.0 %shard_map.73 = (f32[19,5,8,128]{3,2,1,0:T(8,128)S(1)}, f32[3,5,8,128]{3,2,1,0:T(8,128)S(1)}, f32[2,5,8,128]{3,2,1,0:T(8,128)S(1)}, f32[4,8,8,128]{3,2,1,0:T(8,1...) custom-call(s32[3,128]{1,0:T(4,128)S(1)} %copy-done.1, ...), custom_call_target="tpu_custom_call" | custom-call | flops 8000000 | bytes 1000000 | tf_op jit(solution)/shard_map/pallas_call | solution.py:590
  27.5 0.0 collective-permute-done.4.p_ref
  27.6 0.5 %shard_map.75 = f32[32,128]{1,0:T(8,128)S(1)} custom-call(f32[19,128]{1,0:T(8,128)S(1)} %get-tuple-element.33.react_ref, s32[3,128]{1,0:T(4,128)S(1)} %copy-done.1, f32[792,128]{1,0:T(8,128)S(1)} %get-tuple-element.49.pq_ref, f32[536,128]{1,0:T(8,128)S(1)} %collective-permute-done.4.p_ref, f32[19,5,8,128]{3,2,1,0:T(8,128)S(1)} %get-tuple-element.52.part_ref, ...), custom_call_target="tpu_custom_call" | custom-call | flops 8000000 | bytes 1000000 | tf_op jit(solution)/shard_map/pallas_call | solution.py:590
  28.0 0.9 %collective-permute-start.9 = (f32[32,128]{1,0:T(8,128)S(1)}, f32[32,128]{1,0:T(8,128)S(1)}, u32[]{:S(2)}, u32[]{:S(2)}) collective-permute-start(f32[32,128]{1,0:T(8,128)S(1)} %shard_map.75), channel_id=1, source_target_pairs={{0,16},{1,17},{2,18},{3,19},{4,20},{5,21},{6,22},{7,23},{8,24},{9,... | collective-permute-start | bytes 49160 | tf_op jit(solution)/shard_map/ppermute | solution.py:615
  28.9 0.3 collective-permute-done.5.q_ref
  29.2 0.3 shard_map.74
  29.5 0.0 collective-permute-done.8.rest_ref
  29.5 2.3 %collective-permute-done.9.upper_ref = f32[32,128]{1,0:T(8,128)S(1)} collective-permute-done((f32[32,128]{1,0:T(8,128)S(1)}, f32[32,128]{1,0:T(8,128)S(1)}, u32[]{:S(2)}, u32[]{:S(2)}) %collective-permute-start.9) | collective-permute-done | bytes 16416 | tf_op jit(solution)/shard_map/ppermute | solution.py:615
  31.8 0.7 %shard_map.76 = (f32[6,64,128]{2,1,0:T(8,128)}, f32[64,128]{1,0:T(8,128)}) custom-call(f32[6,64,128]{2,1,0:T(8,128)S(1)} %get-tuple-element.58.ocean_ref, f32[4,40,128]{2,1,0:T(8,128)S(1)} %collective-permute-done.6.gb_ref.refs_0_.over_ref, f32[264,128]{1,0:T(8,128)S(1)} %collective-permute-done.8.rest_ref, f32[64,128]{1,0:T(8,128)S(1)} %get-tuple-element.60.chl_ref, ...), custom_call_target="tpu_custom_call" | custom-call | flops 1000000 | bytes 1000000 | tf_op jit(solution)/shard_map/pallas_call | solution.py:590
  (3 shorter events, 0.0 us)
Async XLA Ops:
  0.6 9.0 %copy-start.2 = (f32[19,19]{1,0:T(8,128)S(1)}, f32[19,19]{1,0:T(8,128)}, u32[]{:S(2)}) copy-start(f32[19,19]{1,0:T(8,128)} %r_ref.1) | copy-start | bytes 4336
  0.6 11.8 %copy-start = (f32[1,6,64,128]{3,2,1,0:T(8,128)S(1)}, f32[1,6,64,128]{3,2,1,0:T(8,128)}, u32[]{:S(2)}) copy-start(f32[1,6,64,128]{3,2,1,0:T(8,128)} %param.5) | copy-start | bytes 589828
  1.9 10.5 %collective-permute-start.3 = (f32[792,128]{1,0:T(8,128)S(1)}, f32[792,128]{1,0:T(8,128)S(1)}, u32[]{:S(2)}, u32[]{:S(2)}) collective-permute-start(f32[792,128]{1,0:T(8,128)S(1)} %get-tuple-element.35.pq_ref), channel_id=1, source_target_pairs={{0,1},{1,0},{2,3},{3,2},{4,5},{5,4},{6,7},{7,6},{8,9},{9,8},{10,11... | collective-permute-start | bytes 1216520 | tf_op jit(solution)/shard_map/ppermute | solution.py:615
  2.5 11.0 %collective-permute-start = (f32[536,128]{1,0:T(8,128)S(1)}, f32[536,128]{1,0:T(8,128)S(1)}, u32[]{:S(2)}, u32[]{:S(2)}) collective-permute-start(f32[536,128]{1,0:T(8,128)S(1)} %get-tuple-element.36), channel_id=1, source_target_pairs={{0,15},{1,2},{2,1},{3,4},{4,3},{5,6},{6,5},{7,8},{8,7},{9,10},{10,... | collective-permute-start | bytes 823304 | tf_op jit(solution)/shard_map/ppermute | solution.py:615
  8.1 7.2 %collective-permute-start.1 = (f32[256,128]{1,0:T(8,128)S(1)}, f32[256,128]{1,0:T(8,128)S(1)}, u32[]{:S(2)}, u32[]{:S(2)}) collective-permute-start(f32[256,128]{1,0:T(8,128)S(1)} %get-tuple-element.37), channel_id=1, source_target_pairs={{0,15},{1,2},{2,1},{3,4},{4,3},{5,6},{6,5},{7,8},{8,7},{9,10},{10,... | collective-permute-start | bytes 393224 | tf_op jit(solution)/shard_map/ppermute | solution.py:615
  8.2 4.3 %collective-permute-start.2 = (f32[4,32,128]{2,1,0:T(8,128)S(1)}, f32[4,32,128]{2,1,0:T(8,128)S(1)}, u32[]{:S(2)}, u32[]{:S(2)}) collective-permute-start(f32[4,32,128]{2,1,0:T(8,128)S(1)} %get-tuple-element.38), channel_id=1, source_target_pairs={{0,16},{1,17},{2,18},{3,19},{4,20},{5,21},{6,22},{7,23},{8,24},{9,... | collective-permute-start | bytes 196616 | tf_op jit(solution)/shard_map/ppermute | solution.py:615
  9.7 2.8 %copy-start.1 = (s32[3,128]{1,0:T(4,128)S(1)}, s32[3,128]{1,0:T(4,128)}, u32[]{:S(2)}) copy-start(s32[3,128]{1,0:T(4,128)} %nb_ref.11) | copy-start | bytes 4612
  15.6 10.9 %collective-permute-start.7 = (f32[792,128]{1,0:T(8,128)S(1)}, f32[792,128]{1,0:T(8,128)S(1)}, u32[]{:S(2)}, u32[]{:S(2)}) collective-permute-start(f32[792,128]{1,0:T(8,128)S(1)} %get-tuple-element.49.pq_ref), channel_id=1, source_target_pairs={{0,1},{1,0},{2,3},{3,2},{4,5},{5,4},{6,7},{7,6},{8,9},{9,8},{10,11... | collective-permute-start | bytes 1216520 | tf_op jit(solution)/shard_map/ppermute | solution.py:615
  15.7 11.8 %collective-permute-start.4 = (f32[536,128]{1,0:T(8,128)S(1)}, f32[536,128]{1,0:T(8,128)S(1)}, u32[]{:S(2)}, u32[]{:S(2)}) collective-permute-start(f32[536,128]{1,0:T(8,128)S(1)} %get-tuple-element.46.done_ref.chl_ref), channel_id=1, source_target_pairs={{0,15},{1,2},{2,1},{3,4},{4,3},{5,6},{6,5},{7,8},{8,7},{9,10},{10,... | collective-permute-start | bytes 823304 | tf_op jit(solution)/shard_map/ppermute | solution.py:615
  20.3 9.2 %collective-permute-start.8 = (f32[264,128]{1,0:T(8,128)S(1)}, f32[264,128]{1,0:T(8,128)S(1)}, u32[]{:S(2)}, u32[]{:S(2)}) collective-permute-start(f32[264,128]{1,0:T(8,128)S(1)} %get-tuple-element.59), channel_id=1, source_target_pairs={{0,16},{1,17},{2,18},{3,19},{4,20},{5,21},{6,22},{7,23},{8,24},{9,... | collective-permute-start | bytes 405512 | tf_op jit(solution)/shard_map/ppermute | solution.py:615
  22.1 7.1 %collective-permute-start.5 = (f32[256,128]{1,0:T(8,128)S(1)}, f32[256,128]{1,0:T(8,128)S(1)}, u32[]{:S(2)}, u32[]{:S(2)}) collective-permute-start(f32[256,128]{1,0:T(8,128)S(1)} %get-tuple-element.50), channel_id=1, source_target_pairs={{0,15},{1,2},{2,1},{3,4},{4,3},{5,6},{6,5},{7,8},{8,7},{9,10},{10,... | collective-permute-start | bytes 393224 | tf_op jit(solution)/shard_map/ppermute | solution.py:615
  22.1 4.4 %collective-permute-start.6 = (f32[4,40,128]{2,1,0:T(8,128)S(1)}, f32[4,40,128]{2,1,0:T(8,128)S(1)}, u32[]{:S(2)}, u32[]{:S(2)}) collective-permute-start(f32[4,40,128]{2,1,0:T(8,128)S(1)} %get-tuple-element.51), channel_id=1, source_target_pairs={{0,16},{1,17},{2,18},{3,19},{4,20},{5,21},{6,22},{7,23},{8,24},{9,... | collective-permute-start | bytes 245768 | tf_op jit(solution)/shard_map/ppermute | solution.py:615
  28.0 3.8 %collective-permute-start.9 = (f32[32,128]{1,0:T(8,128)S(1)}, f32[32,128]{1,0:T(8,128)S(1)}, u32[]{:S(2)}, u32[]{:S(2)}) collective-permute-start(f32[32,128]{1,0:T(8,128)S(1)} %shard_map.75), channel_id=1, source_target_pairs={{0,16},{1,17},{2,18},{3,19},{4,20},{5,21},{6,22},{7,23},{8,24},{9,... | collective-permute-start | bytes 49160 | tf_op jit(solution)/shard_map/ppermute | solution.py:615

commit v6 on v5

--- a/solution.py
+++ b/solution.py
@@ -17,6 +17,7 @@
 F32 = jnp.float32
 BF16 = jnp.bfloat16
 GRANT = 8 << 20
+WIDTH = 2
 
 
 VMEM = pl.BlockSpec(memory_space=pltpu.VMEM)
@@ -341,32 +342,44 @@
         for j, v in enumerate(far_moves(parts, own, cross, [far] * plan.nt, self.index)):
             self.h[j, at : at + SUB, :] = v
 
-    def react(self, r, react_ref, put):
+    def mix(self, r):
         plan, at = self.plan, self.at(r)
-        active = (level_block(plan.level(self.comp, r), self.cols) < self.wet).astype(F32)
         down, up = self.l[at : at + SUB, :], self.l[at - 1 : at - 1 + SUB, :]
-        ys, ts = [], []
+        ys = []
         for j in range(plan.nt):
             v = self.h[j, at : at + SUB, :]
-            y = v + down * (self.h[j, at + 1 : at + 1 + SUB, :] - v) - up * (v - self.h[j, at - 1 : at - 1 + SUB, :])
-            ys.append(y)
-            ts.append(jnp.tanh(y))
-        growth = self.aux[1, r]
-        if self.second:
-            total = react_ref[0:1, :] * ts[0]
-            for j in range(1, plan.nt):
-                total = total + react_ref[j : j + 1, :] * ts[j]
-            put(0, r, (ys[0] + growth * total) * active)
-            return
-        n = react_ref.shape[1]
-        ts += [jnp.zeros_like(ts[0])] * (n // SUB - plan.nt)
-        stack = jnp.concatenate(ts, axis=0)
-        high = stack.astype(BF16)
-        rest = (stack - high.astype(F32)).astype(BF16)
-        both = jnp.dot(react_ref[...], high, preferred_element_type=F32)
-        total = both[:n] + both[n:] + jnp.dot(react_ref[0:n, :], rest, preferred_element_type=F32)
-        for i in range(plan.nt):
-            put(i, r, (ys[i] + growth * total[i * SUB : (i + 1) * SUB]) * active)
+            ys.append(
+                v + down * (self.h[j, at + 1 : at + 1 + SUB, :] - v) - up * (v - self.h[j, at - 1 : at - 1 + SUB, :])
+            )
+        return ys
+
+    def react(self, rs, react_ref, put):
+        plan = self.plan
+        ys = [self.mix(r) for r in rs]
+        ts = [[jnp.tanh(y) for y in block] for block in ys]
+        if not self.second:
+            n = react_ref.shape[1]
+            pad = [jnp.zeros_like(ts[0][0])] * (n // SUB - plan.nt)
+            stack = jnp.concatenate([jnp.concatenate(t + pad, axis=0) for t in ts], axis=1)
+            high = stack.astype(BF16)
+            rest = (stack - high.astype(F32)).astype(BF16)
+            both = jnp.dot(react_ref[...], high, preferred_element_type=F32)
+            total = both[:n] + both[n:] + jnp.dot(react_ref[0:n, :], rest, preferred_element_type=F32)
+        for b, r in enumerate(rs):
+            active = (level_block(plan.level(self.comp, r), self.cols) < self.wet).astype(F32)
+            growth = self.aux[1, r]
+            if self.second:
+                sums = [react_ref[0:1, :] * ts[b][0]]
+                for j in range(1, plan.nt):
+                    sums[0] = sums[0] + react_ref[j : j + 1, :] * ts[b][j]
+            else:
+                sums = [total[i * SUB : (i + 1) * SUB, b * self.cols : (b + 1) * self.cols] for i in range(plan.nt)]
+            for i, v in enumerate(sums):
+                put(i, r, (ys[b][i] + growth * v) * active)
+
+    def react_all(self, rs, react_ref, put, width=WIDTH):
+        for i in range(0, len(rs), width):
+            self.react(rs[i : i + width], react_ref, put)
 
 
 def nothing(offset):
@@ -393,8 +406,7 @@
                 at = plan.halves + plan.half * i
                 out_ref[at : at + plan.half, :] = value[0 : plan.half]
 
-        for r in plan.rs(0):
-            work.react(r, react_ref, put)
+        work.react_all(plan.rs(0), react_ref, put)
 
     @on_side(1)
     def _():
@@ -415,8 +427,7 @@
                 at = plan.halves + plan.half * i
                 out_ref[at : at + plan.half, :] = value[0 : plan.half]
 
-        for r in range(plan.full + 1):
-            work.react(r, react_ref, put)
+        work.react_all(list(range(plan.full + 1)), react_ref, put)
 
 
 def ocean_far(plan, nb_ref, f_ref, pq_ref, p_ref, q_ref, opart_ref, ofar_ref, oaux_ref, w_ref, l_ref, put):
@@ -517,8 +528,7 @@
             if i == 0:
                 over_ref[0, SUB * r : SUB * (r + 1), :] = value
 
-        for r in rs:
-            work.react(r, react_ref, put)
+        work.react_all(rs, react_ref, put)
         for r in range(plan.full):
             over_ref[0, SUB * r : SUB * (r + 1), :] = done_ref[SUB * r : SUB * (r + 1), :]
 
@@ -534,8 +544,7 @@
         def put(i, r, value):
             out_ref[SUB * (r - 1) : SUB * r, :] = value
 
-        for r in plan.rs(0):
-            work.react(r, react_ref, put)
+        work.react_all(plan.rs(0), react_ref, put, 1)
 
 
 def second_kernel(
@@ -559,8 +568,7 @@
         def put(i, r, value):
             mine_ref[SUB * r : SUB * (r + 1), :] = value
 
-        for r in plan.rs(1):
-            work.react(r, react_ref, put)
+        work.react_all(plan.rs(1), react_ref, put, 1)
 
 
 def merge_kernel(plan, ocean_ref, over_ref, rest_ref, chl_ref, mine_ref, upper_ref, out_ref, chl_out_ref):

time: 32.7 us -> 32.6 us (level)
  no operation moved by 1% of the time
where the time goes in v6:
time: 32.6 us; the launch traced here: 32.5 us
  starting transfers between devices  15.3 us (47%)
  waiting for transfers between devices  9.89 us (30%)
  Pallas kernels  6.47 us (20%)
  between operations  0.74 us (2%)
    ppermute x10, starting transfers between devices, sent(): return lax.ppermute(v, AXES, pairs)  15.3 us
    ppermute x10, waiting for transfers between devices, sent(): return lax.ppermute(v, AXES, pairs)  9.89 us
    pallas_call x9, Pallas kernels, call(): pl.pallas_call(kernel, out_shape=outs, in_specs=specs or [VMEM] * len(ins...  6.47 us
  transfers between devices with their start and end apart: 10, of which 5 were waited for; matrix products, arithmetic and copies ran while one was open for 0% of the time, Pallas kernels for 13%

profile of v6, /device:TPU:0, one launch (start us, length us, event | category | flops | bytes accessed | tf_op | source)
XLA Modules:
  0.0 32.5 jit_solution(13349347985624459004)
XLA Ops:
  0.6 0.0 copy-start.2
  0.6 0.0 copy-start
  0.7 1.3 %shard_map.69 = (f32[536,128]{1,0:T(8,128)S(1)}, f32[256,128]{1,0:T(8,128)S(1)}, f32[792,128]{1,0:T(8,128)S(1)}, f32[4,32,128]{2,1,0:T(8,128)S(1)}, f32[64,128]{1,0:T(8,128)S(1)}) custom-call(s32[1,128]{1,0:T(1,128)} %bitcast.8, f32[6,64,128]{2,1,0:T(8,128)} %bitcast.4, f32[19,64,128]{2,1,0:T(8,128)} %t_ref.1), custom_call_target="tpu_custom_call" | custom-call | flops 1000000 | bytes 1000000 | tf_op jit(solution)/shard_map/pallas_call | solution.py:598
  1.9 0.6 %collective-permute-start.3 = (f32[792,128]{1,0:T(8,128)S(1)}, f32[792,128]{1,0:T(8,128)S(1)}, u32[]{:S(2)}, u32[]{:S(2)}) collective-permute-start(f32[792,128]{1,0:T(8,128)S(1)} %get-tuple-element.35.pq_ref), channel_id=1, source_target_pairs={{0,1},{1,0},{2,3},{3,2},{4,5},{5,4},{6,7},{7,6},{8,9},{9,8},{10,11... | collective-permute-start | bytes 1216520 | tf_op jit(solution)/shard_map/ppermute | solution.py:623
  2.5 5.7 %collective-permute-start = (f32[536,128]{1,0:T(8,128)S(1)}, f32[536,128]{1,0:T(8,128)S(1)}, u32[]{:S(2)}, u32[]{:S(2)}) collective-permute-start(f32[536,128]{1,0:T(8,128)S(1)} %get-tuple-element.36), channel_id=1, source_target_pairs={{0,15},{1,2},{2,1},{3,4},{4,3},{5,6},{6,5},{7,8},{8,7},{9,10},{10,... | collective-permute-start | bytes 823304 | tf_op jit(solution)/shard_map/ppermute | solution.py:623
  8.1 0.0 collective-permute-start.1
  8.2 1.5 %collective-permute-start.2 = (f32[4,32,128]{2,1,0:T(8,128)S(1)}, f32[4,32,128]{2,1,0:T(8,128)S(1)}, u32[]{:S(2)}, u32[]{:S(2)}) collective-permute-start(f32[4,32,128]{2,1,0:T(8,128)S(1)} %get-tuple-element.38), channel_id=1, source_target_pairs={{0,16},{1,17},{2,18},{3,19},{4,20},{5,21},{6,22},{7,23},{8,24},{9,... | collective-permute-start | bytes 196616 | tf_op jit(solution)/shard_map/ppermute | solution.py:623
  9.7 0.6 %shard_map.68 = (bf16[320,160]{1,0:T(8,128)(2,1)S(1)}, f32[19,128]{1,0:T(8,128)S(1)}) custom-call(f32[19,19]{1,0:T(8,128)S(1)} %copy-done.2), custom_call_target="tpu_custom_call" | custom-call | flops 1000000 | bytes 1000000 | tf_op jit(solution)/shard_map/pallas_call | solution.py:598
  10.3 2.2 %collective-permute-done.2.ga_ref = f32[4,32,128]{2,1,0:T(8,128)S(1)} collective-permute-done((f32[4,32,128]{2,1,0:T(8,128)S(1)}, f32[4,32,128]{2,1,0:T(8,128)S(1)}, u32[]{:S(2)}, u32[]{:S(2)}) %collective-permute-start.2) | collective-permute-done | bytes 65568 | tf_op jit(solution)/shard_map/ppermute | solution.py:623
  12.4 0.0 collective-permute-done.3.core_ref
  12.4 0.0 copy-done
  12.5 1.0 %shard_map.70 = (f32[19,5,8,128]{3,2,1,0:T(8,128)S(1)}, f32[3,5,8,128]{3,2,1,0:T(8,128)S(1)}, f32[2,5,8,128]{3,2,1,0:T(8,128)S(1)}, f32[4,8,8,128]{3,2,1,0:T(8,1...) custom-call(s32[3,128]{1,0:T(4,128)S(1)} %copy-done.1, f32[6,64,128]{2,1,0:T(8,128)S(1)} %bitcast.5, ...), custom_call_target="tpu_custom_call" | custom-call | flops 8000000 | bytes 1000000 | tf_op jit(solution)/shard_map/pallas_call | solution.py:598
  13.4 0.0 collective-permute-done.p_ref
  13.5 0.9 %shard_map.71 = (f32[536,128]{1,0:T(8,128)S(1)}, f32[19,8,128]{2,1,0:T(8,128)S(1)}) custom-call(bf16[320,160]{1,0:T(8,128)(2,1)S(1)} %get-tuple-element.34.react_ref, s32[3,128]{1,0:T(4,128)S(1)} %copy-done.1, f32[792,128]{1,0:T(8,128)S(1)} %get-tuple-element.35.pq_ref, f32[536,128]{1,0:T(8,128)S(1)} %collective-permute-done.p_ref, ...), custom_call_target="tpu_custom_call" | custom-call | flops 8000000 | bytes 1000000 | tf_op jit(solution)/shard_map/pallas_call | solution.py:598
  14.3 1.0 %collective-permute-done.1.q_ref = f32[256,128]{1,0:T(8,128)S(1)} collective-permute-done((f32[256,128]{1,0:T(8,128)S(1)}, f32[256,128]{1,0:T(8,128)S(1)}, u32[]{:S(2)}, u32[]{:S(2)}) %collective-permute-start.1) | collective-permute-done | bytes 131104 | tf_op jit(solution)/shard_map/ppermute | solution.py:623
  15.3 0.3 shard_map.72
  15.6 0.1 collective-permute-start.7
  15.7 4.6 %collective-permute-start.4 = (f32[536,128]{1,0:T(8,128)S(1)}, f32[536,128]{1,0:T(8,128)S(1)}, u32[]{:S(2)}, u32[]{:S(2)}) collective-permute-start(f32[536,128]{1,0:T(8,128)S(1)} %get-tuple-element.46.done_ref.chl_ref), channel_id=1, source_target_pairs={{0,15},{1,2},{2,1},{3,4},{4,3},{5,6},{6,5},{7,8},{8,7},{9,10},{10,... | collective-permute-start | bytes 823304 | tf_op jit(solution)/shard_map/ppermute | solution.py:623
  20.3 1.8 %collective-permute-start.8 = (f32[264,128]{1,0:T(8,128)S(1)}, f32[264,128]{1,0:T(8,128)S(1)}, u32[]{:S(2)}, u32[]{:S(2)}) collective-permute-start(f32[264,128]{1,0:T(8,128)S(1)} %get-tuple-element.59), channel_id=1, source_target_pairs={{0,16},{1,17},{2,18},{3,19},{4,20},{5,21},{6,22},{7,23},{8,24},{9,... | collective-permute-start | bytes 405512 | tf_op jit(solution)/shard_map/ppermute | solution.py:623
  22.0 0.0 collective-permute-start.5
  22.1 0.3 collective-permute-start.6
  22.3 4.2 %collective-permute-done.6.gb_ref.refs_0_.over_ref = f32[4,40,128]{2,1,0:T(8,128)S(1)} collective-permute-done((f32[4,40,128]{2,1,0:T(8,128)S(1)}, f32[4,40,128]{2,1,0:T(8,128)S(1)}, u32[]{:S(2)}, u32[]{:S(2)}) %collective-permute-start.6) | collective-permute-done | bytes 81952 | tf_op jit(solution)/shard_map/ppermute | solution.py:623
  26.5 0.0 collective-permute-done.7.core_ref
  26.5 1.0 %shard_map.73 = (f32[19,5,8,128]{3,2,1,0:T(8,128)S(1)}, f32[3,5,8,128]{3,2,1,0:T(8,128)S(1)}, f32[2,5,8,128]{3,2,1,0:T(8,128)S(1)}, f32[4,8,8,128]{3,2,1,0:T(8,1...) custom-call(s32[3,128]{1,0:T(4,128)S(1)} %copy-done.1, ...), custom_call_target="tpu_custom_call" | custom-call | flops 8000000 | bytes 1000000 | tf_op jit(solution)/shard_map/pallas_call | solution.py:598
  27.5 0.0 collective-permute-done.4.p_ref
  27.5 0.5 %shard_map.75 = f32[32,128]{1,0:T(8,128)S(1)} custom-call(f32[19,128]{1,0:T(8,128)S(1)} %get-tuple-element.33.react_ref, s32[3,128]{1,0:T(4,128)S(1)} %copy-done.1, f32[792,128]{1,0:T(8,128)S(1)} %get-tuple-element.49.pq_ref, f32[536,128]{1,0:T(8,128)S(1)} %collective-permute-done.4.p_ref, f32[19,5,8,128]{3,2,1,0:T(8,128)S(1)} %get-tuple-element.52.part_ref, ...), custom_call_target="tpu_custom_call" | custom-call | flops 8000000 | bytes 1000000 | tf_op jit(solution)/shard_map/pallas_call | solution.py:598
  28.0 0.9 %collective-permute-start.9 = (f32[32,128]{1,0:T(8,128)S(1)}, f32[32,128]{1,0:T(8,128)S(1)}, u32[]{:S(2)}, u32[]{:S(2)}) collective-permute-start(f32[32,128]{1,0:T(8,128)S(1)} %shard_map.75), channel_id=1, source_target_pairs={{0,16},{1,17},{2,18},{3,19},{4,20},{5,21},{6,22},{7,23},{8,24},{9,... | collective-permute-start | bytes 49160 | tf_op jit(solution)/shard_map/ppermute | solution.py:623
  28.9 0.3 collective-permute-done.5.q_ref
  29.1 0.3 shard_map.74
  29.5 0.0 collective-permute-done.8.rest_ref
  29.5 2.3 %collective-permute-done.9.upper_ref = f32[32,128]{1,0:T(8,128)S(1)} collective-permute-done((f32[32,128]{1,0:T(8,128)S(1)}, f32[32,128]{1,0:T(8,128)S(1)}, u32[]{:S(2)}, u32[]{:S(2)}) %collective-permute-start.9) | collective-permute-done | bytes 16416 | tf_op jit(solution)/shard_map/ppermute | solution.py:623
  31.8 0.7 %shard_map.76 = (f32[6,64,128]{2,1,0:T(8,128)}, f32[64,128]{1,0:T(8,128)}) custom-call(f32[6,64,128]{2,1,0:T(8,128)S(1)} %get-tuple-element.58.ocean_ref, f32[4,40,128]{2,1,0:T(8,128)S(1)} %collective-permute-done.6.gb_ref.refs_0_.over_ref, f32[264,128]{1,0:T(8,128)S(1)} %collective-permute-done.8.rest_ref, f32[64,128]{1,0:T(8,128)S(1)} %get-tuple-element.60.chl_ref, ...), custom_call_target="tpu_custom_call" | custom-call | flops 1000000 | bytes 1000000 | tf_op jit(solution)/shard_map/pallas_call | solution.py:598
  (3 shorter events, 0.0 us)
Async XLA Ops:
  0.6 9.0 %copy-start.2 = (f32[19,19]{1,0:T(8,128)S(1)}, f32[19,19]{1,0:T(8,128)}, u32[]{:S(2)}) copy-start(f32[19,19]{1,0:T(8,128)} %r_ref.1) | copy-start | bytes 4336
  0.6 11.8 %copy-start = (f32[1,6,64,128]{3,2,1,0:T(8,128)S(1)}, f32[1,6,64,128]{3,2,1,0:T(8,128)}, u32[]{:S(2)}) copy-start(f32[1,6,64,128]{3,2,1,0:T(8,128)} %param.5) | copy-start | bytes 589828
  1.9 10.5 %collective-permute-start.3 = (f32[792,128]{1,0:T(8,128)S(1)}, f32[792,128]{1,0:T(8,128)S(1)}, u32[]{:S(2)}, u32[]{:S(2)}) collective-permute-start(f32[792,128]{1,0:T(8,128)S(1)} %get-tuple-element.35.pq_ref), channel_id=1, source_target_pairs={{0,1},{1,0},{2,3},{3,2},{4,5},{5,4},{6,7},{7,6},{8,9},{9,8},{10,11... | collective-permute-start | bytes 1216520 | tf_op jit(solution)/shard_map/ppermute | solution.py:623
  2.5 11.0 %collective-permute-start = (f32[536,128]{1,0:T(8,128)S(1)}, f32[536,128]{1,0:T(8,128)S(1)}, u32[]{:S(2)}, u32[]{:S(2)}) collective-permute-start(f32[536,128]{1,0:T(8,128)S(1)} %get-tuple-element.36), channel_id=1, source_target_pairs={{0,15},{1,2},{2,1},{3,4},{4,3},{5,6},{6,5},{7,8},{8,7},{9,10},{10,... | collective-permute-start | bytes 823304 | tf_op jit(solution)/shard_map/ppermute | solution.py:623
  8.1 7.2 %collective-permute-start.1 = (f32[256,128]{1,0:T(8,128)S(1)}, f32[256,128]{1,0:T(8,128)S(1)}, u32[]{:S(2)}, u32[]{:S(2)}) collective-permute-start(f32[256,128]{1,0:T(8,128)S(1)} %get-tuple-element.37), channel_id=1, source_target_pairs={{0,15},{1,2},{2,1},{3,4},{4,3},{5,6},{6,5},{7,8},{8,7},{9,10},{10,... | collective-permute-start | bytes 393224 | tf_op jit(solution)/shard_map/ppermute | solution.py:623
  8.2 4.3 %collective-permute-start.2 = (f32[4,32,128]{2,1,0:T(8,128)S(1)}, f32[4,32,128]{2,1,0:T(8,128)S(1)}, u32[]{:S(2)}, u32[]{:S(2)}) collective-permute-start(f32[4,32,128]{2,1,0:T(8,128)S(1)} %get-tuple-element.38), channel_id=1, source_target_pairs={{0,16},{1,17},{2,18},{3,19},{4,20},{5,21},{6,22},{7,23},{8,24},{9,... | collective-permute-start | bytes 196616 | tf_op jit(solution)/shard_map/ppermute | solution.py:623
  9.7 2.8 %copy-start.1 = (s32[3,128]{1,0:T(4,128)S(1)}, s32[3,128]{1,0:T(4,128)}, u32[]{:S(2)}) copy-start(s32[3,128]{1,0:T(4,128)} %nb_ref.11) | copy-start | bytes 4612
  15.6 10.9 %collective-permute-start.7 = (f32[792,128]{1,0:T(8,128)S(1)}, f32[792,128]{1,0:T(8,128)S(1)}, u32[]{:S(2)}, u32[]{:S(2)}) collective-permute-start(f32[792,128]{1,0:T(8,128)S(1)} %get-tuple-element.49.pq_ref), channel_id=1, source_target_pairs={{0,1},{1,0},{2,3},{3,2},{4,5},{5,4},{6,7},{7,6},{8,9},{9,8},{10,11... | collective-permute-start | bytes 1216520 | tf_op jit(solution)/shard_map/ppermute | solution.py:623
  15.7 11.8 %collective-permute-start.4 = (f32[536,128]{1,0:T(8,128)S(1)}, f32[536,128]{1,0:T(8,128)S(1)}, u32[]{:S(2)}, u32[]{:S(2)}) collective-permute-start(f32[536,128]{1,0:T(8,128)S(1)} %get-tuple-element.46.done_ref.chl_ref), channel_id=1, source_target_pairs={{0,15},{1,2},{2,1},{3,4},{4,3},{5,6},{6,5},{7,8},{8,7},{9,10},{10,... | collective-permute-start | bytes 823304 | tf_op jit(solution)/shard_map/ppermute | solution.py:623
  20.3 9.2 %collective-permute-start.8 = (f32[264,128]{1,0:T(8,128)S(1)}, f32[264,128]{1,0:T(8,128)S(1)}, u32[]{:S(2)}, u32[]{:S(2)}) collective-permute-start(f32[264,128]{1,0:T(8,128)S(1)} %get-tuple-element.59), channel_id=1, source_target_pairs={{0,16},{1,17},{2,18},{3,19},{4,20},{5,21},{6,22},{7,23},{8,24},{9,... | collective-permute-start | bytes 405512 | tf_op jit(solution)/shard_map/ppermute | solution.py:623
  22.0 7.1 %collective-permute-start.5 = (f32[256,128]{1,0:T(8,128)S(1)}, f32[256,128]{1,0:T(8,128)S(1)}, u32[]{:S(2)}, u32[]{:S(2)}) collective-permute-start(f32[256,128]{1,0:T(8,128)S(1)} %get-tuple-element.50), channel_id=1, source_target_pairs={{0,15},{1,2},{2,1},{3,4},{4,3},{5,6},{6,5},{7,8},{8,7},{9,10},{10,... | collective-permute-start | bytes 393224 | tf_op jit(solution)/shard_map/ppermute | solution.py:623
  22.1 4.4 %collective-permute-start.6 = (f32[4,40,128]{2,1,0:T(8,128)S(1)}, f32[4,40,128]{2,1,0:T(8,128)S(1)}, u32[]{:S(2)}, u32[]{:S(2)}) collective-permute-start(f32[4,40,128]{2,1,0:T(8,128)S(1)} %get-tuple-element.51), channel_id=1, source_target_pairs={{0,16},{1,17},{2,18},{3,19},{4,20},{5,21},{6,22},{7,23},{8,24},{9,... | collective-permute-start | bytes 245768 | tf_op jit(solution)/shard_map/ppermute | solution.py:623
  28.0 3.8 %collective-permute-start.9 = (f32[32,128]{1,0:T(8,128)S(1)}, f32[32,128]{1,0:T(8,128)S(1)}, u32[]{:S(2)}, u32[]{:S(2)}) collective-permute-start(f32[32,128]{1,0:T(8,128)S(1)} %shard_map.75), channel_id=1, source_target_pairs={{0,16},{1,17},{2,18},{3,19},{4,20},{5,21},{6,22},{7,23},{8,24},{9,... | collective-permute-start | bytes 49160 | tf_op jit(solution)/shard_map/ppermute | solution.py:623

commit v7 on v6

--- a/solution.py
+++ b/solution.py
@@ -17,7 +17,7 @@
 F32 = jnp.float32
 BF16 = jnp.bfloat16
 GRANT = 8 << 20
-WIDTH = 2
+WIDTH = 4
 
 
 VMEM = pl.BlockSpec(memory_space=pltpu.VMEM)
@@ -125,16 +125,20 @@
         (t_ref.at[:, pl.ds(first, tall)], p_ref.at[pl.ds(0, plan.halves)].reshape(nt, tall, p_ref.shape[1])),
         (t_ref.at[:, pl.ds(pl.multiple_of(first + tall, SUB), SUB)], half_buf),
         (wet_ref, wet_buf),
-        (f_ref.at[:, pl.ds(0, top_ref.shape[1])], top_buf),
-        (t_ref.at[0], chl_ref),
     ]
     copies = [pltpu.make_async_copy(s, d, sems.at[i]) for i, (s, d) in enumerate(copies)]
     for c in copies:
         c.start()
     base = len(copies)
     slab = lambda n, rows: q_ref.at[pl.ds(0, n * rows)].reshape(n, rows, q_ref.shape[1])
-    ocean = [pltpu.make_async_copy(f_ref.at[pl.ds(0, 4)], slab(4, lev), sems.at[base])]
-    deep = [pltpu.make_async_copy(t_ref.at[:, pl.ds(lev - SUB, SUB)], slab(nt, SUB), sems.at[base])]
+    ocean = [
+        pltpu.make_async_copy(f_ref.at[pl.ds(0, 4)], slab(4, lev), sems.at[base]),
+        pltpu.make_async_copy(t_ref.at[0], chl_ref, sems.at[base + 1]),
+    ]
+    deep = [
+        pltpu.make_async_copy(t_ref.at[:, pl.ds(lev - SUB, SUB)], slab(nt, SUB), sems.at[base]),
+        pltpu.make_async_copy(f_ref.at[:, pl.ds(0, top_ref.shape[1])], top_buf, sems.at[base + 1]),
+    ]
 
     @on_side(0)
     def _():

time: 32.6 us -> 32.6 us (level)
  no operation moved by 1% of the time
where the time goes in v7:
time: 32.6 us; the launch traced here: 32.4 us
  starting transfers between devices  15.4 us (47%)
  waiting for transfers between devices  9.89 us (30%)
  Pallas kernels  6.41 us (20%)
  between operations  0.74 us (2%)
    ppermute x10, starting transfers between devices, sent(): return lax.ppermute(v, AXES, pairs)  15.4 us
    ppermute x10, waiting for transfers between devices, sent(): return lax.ppermute(v, AXES, pairs)  9.89 us
    pallas_call x9, Pallas kernels, call(): pl.pallas_call(kernel, out_shape=outs, in_specs=specs or [VMEM] * len(ins...  6.41 us
  transfers between devices with their start and end apart: 10, of which 5 were waited for; matrix products, arithmetic and copies ran while one was open for 0% of the time, Pallas kernels for 13%

profile of v7, /device:TPU:0, one launch (start us, length us, event | category | flops | bytes accessed | tf_op | source)
XLA Modules:
  0.0 32.4 jit_solution(6229599804612357686)
XLA Ops:
  0.6 0.0 copy-start.2
  0.6 0.0 copy-start
  0.7 1.2 %shard_map.69 = (f32[536,128]{1,0:T(8,128)S(1)}, f32[256,128]{1,0:T(8,128)S(1)}, f32[792,128]{1,0:T(8,128)S(1)}, f32[4,32,128]{2,1,0:T(8,128)S(1)}, f32[64,128]{1,0:T(8,128)S(1)}) custom-call(s32[1,128]{1,0:T(1,128)} %bitcast.8, f32[6,64,128]{2,1,0:T(8,128)} %bitcast.4, f32[19,64,128]{2,1,0:T(8,128)} %t_ref.1), custom_call_target="tpu_custom_call" | custom-call | flops 1000000 | bytes 1000000 | tf_op jit(solution)/shard_map/pallas_call | solution.py:602
  1.9 0.6 %collective-permute-start.3 = (f32[792,128]{1,0:T(8,128)S(1)}, f32[792,128]{1,0:T(8,128)S(1)}, u32[]{:S(2)}, u32[]{:S(2)}) collective-permute-start(f32[792,128]{1,0:T(8,128)S(1)} %get-tuple-element.35.pq_ref), channel_id=1, source_target_pairs={{0,1},{1,0},{2,3},{3,2},{4,5},{5,4},{6,7},{7,6},{8,9},{9,8},{10,11... | collective-permute-start | bytes 1216520 | tf_op jit(solution)/shard_map/ppermute | solution.py:627
  2.4 5.7 %collective-permute-start = (f32[536,128]{1,0:T(8,128)S(1)}, f32[536,128]{1,0:T(8,128)S(1)}, u32[]{:S(2)}, u32[]{:S(2)}) collective-permute-start(f32[536,128]{1,0:T(8,128)S(1)} %get-tuple-element.36), channel_id=1, source_target_pairs={{0,15},{1,2},{2,1},{3,4},{4,3},{5,6},{6,5},{7,8},{8,7},{9,10},{10,... | collective-permute-start | bytes 823304 | tf_op jit(solution)/shard_map/ppermute | solution.py:627
  8.1 0.0 collective-permute-start.1
  8.1 1.5 %collective-permute-start.2 = (f32[4,32,128]{2,1,0:T(8,128)S(1)}, f32[4,32,128]{2,1,0:T(8,128)S(1)}, u32[]{:S(2)}, u32[]{:S(2)}) collective-permute-start(f32[4,32,128]{2,1,0:T(8,128)S(1)} %get-tuple-element.38), channel_id=1, source_target_pairs={{0,16},{1,17},{2,18},{3,19},{4,20},{5,21},{6,22},{7,23},{8,24},{9,... | collective-permute-start | bytes 196616 | tf_op jit(solution)/shard_map/ppermute | solution.py:627
  9.6 0.6 %shard_map.68 = (bf16[320,160]{1,0:T(8,128)(2,1)S(1)}, f32[19,128]{1,0:T(8,128)S(1)}) custom-call(f32[19,19]{1,0:T(8,128)S(1)} %copy-done.2), custom_call_target="tpu_custom_call" | custom-call | flops 1000000 | bytes 1000000 | tf_op jit(solution)/shard_map/pallas_call | solution.py:602
  10.2 2.1 %collective-permute-done.2.ga_ref = f32[4,32,128]{2,1,0:T(8,128)S(1)} collective-permute-done((f32[4,32,128]{2,1,0:T(8,128)S(1)}, f32[4,32,128]{2,1,0:T(8,128)S(1)}, u32[]{:S(2)}, u32[]{:S(2)}) %collective-permute-start.2) | collective-permute-done | bytes 65568 | tf_op jit(solution)/shard_map/ppermute | solution.py:627
  12.4 0.0 collective-permute-done.3.core_ref
  12.4 0.0 copy-done.1
  12.4 1.0 %shard_map.70 = (f32[19,5,8,128]{3,2,1,0:T(8,128)S(1)}, f32[3,5,8,128]{3,2,1,0:T(8,128)S(1)}, f32[2,5,8,128]{3,2,1,0:T(8,128)S(1)}, f32[4,8,8,128]{3,2,1,0:T(8,1...) custom-call(s32[3,128]{1,0:T(4,128)S(1)} %copy-done.1, f32[6,64,128]{2,1,0:T(8,128)S(1)} %bitcast.5, ...), custom_call_target="tpu_custom_call" | custom-call | flops 8000000 | bytes 1000000 | tf_op jit(solution)/shard_map/pallas_call | solution.py:602
  13.4 0.0 collective-permute-done.p_ref
  13.4 0.9 %shard_map.71 = (f32[536,128]{1,0:T(8,128)S(1)}, f32[19,8,128]{2,1,0:T(8,128)S(1)}) custom-call(bf16[320,160]{1,0:T(8,128)(2,1)S(1)} %get-tuple-element.34.react_ref, s32[3,128]{1,0:T(4,128)S(1)} %copy-done.1, f32[792,128]{1,0:T(8,128)S(1)} %get-tuple-element.35.pq_ref, f32[536,128]{1,0:T(8,128)S(1)} %collective-permute-done.p_ref, ...), custom_call_target="tpu_custom_call" | custom-call | flops 8000000 | bytes 1000000 | tf_op jit(solution)/shard_map/pallas_call | solution.py:602
  14.3 1.0 %collective-permute-done.1.q_ref = f32[256,128]{1,0:T(8,128)S(1)} collective-permute-done((f32[256,128]{1,0:T(8,128)S(1)}, f32[256,128]{1,0:T(8,128)S(1)}, u32[]{:S(2)}, u32[]{:S(2)}) %collective-permute-start.1) | collective-permute-done | bytes 131104 | tf_op jit(solution)/shard_map/ppermute | solution.py:627
  15.2 0.3 shard_map.72
  15.6 0.1 collective-permute-start.7
  15.6 4.6 %collective-permute-start.4 = (f32[536,128]{1,0:T(8,128)S(1)}, f32[536,128]{1,0:T(8,128)S(1)}, u32[]{:S(2)}, u32[]{:S(2)}) collective-permute-start(f32[536,128]{1,0:T(8,128)S(1)} %get-tuple-element.46.done_ref.chl_ref), channel_id=1, source_target_pairs={{0,15},{1,2},{2,1},{3,4},{4,3},{5,6},{6,5},{7,8},{8,7},{9,10},{10,... | collective-permute-start | bytes 823304 | tf_op jit(solution)/shard_map/ppermute | solution.py:627
  20.2 1.8 %collective-permute-start.8 = (f32[264,128]{1,0:T(8,128)S(1)}, f32[264,128]{1,0:T(8,128)S(1)}, u32[]{:S(2)}, u32[]{:S(2)}) collective-permute-start(f32[264,128]{1,0:T(8,128)S(1)} %get-tuple-element.59), channel_id=1, source_target_pairs={{0,16},{1,17},{2,18},{3,19},{4,20},{5,21},{6,22},{7,23},{8,24},{9,... | collective-permute-start | bytes 405512 | tf_op jit(solution)/shard_map/ppermute | solution.py:627
  22.0 0.0 collective-permute-start.5
  22.0 0.2 collective-permute-start.6
  22.3 4.2 %collective-permute-done.6.gb_ref.refs_0_.over_ref = f32[4,40,128]{2,1,0:T(8,128)S(1)} collective-permute-done((f32[4,40,128]{2,1,0:T(8,128)S(1)}, f32[4,40,128]{2,1,0:T(8,128)S(1)}, u32[]{:S(2)}, u32[]{:S(2)}) %collective-permute-start.6) | collective-permute-done | bytes 81952 | tf_op jit(solution)/shard_map/ppermute | solution.py:627
  26.5 0.0 collective-permute-done.7.core_ref
  26.5 1.0 %shard_map.73 = (f32[19,5,8,128]{3,2,1,0:T(8,128)S(1)}, f32[3,5,8,128]{3,2,1,0:T(8,128)S(1)}, f32[2,5,8,128]{3,2,1,0:T(8,128)S(1)}, f32[4,8,8,128]{3,2,1,0:T(8,1...) custom-call(s32[3,128]{1,0:T(4,128)S(1)} %copy-done.1, ...), custom_call_target="tpu_custom_call" | custom-call | flops 8000000 | bytes 1000000 | tf_op jit(solution)/shard_map/pallas_call | solution.py:602
  27.5 0.0 collective-permute-done.4.p_ref
  27.5 0.5 %shard_map.75 = f32[32,128]{1,0:T(8,128)S(1)} custom-call(f32[19,128]{1,0:T(8,128)S(1)} %get-tuple-element.33.react_ref, s32[3,128]{1,0:T(4,128)S(1)} %copy-done.1, f32[792,128]{1,0:T(8,128)S(1)} %get-tuple-element.49.pq_ref, f32[536,128]{1,0:T(8,128)S(1)} %collective-permute-done.4.p_ref, f32[19,5,8,128]{3,2,1,0:T(8,128)S(1)} %get-tuple-element.52.part_ref, ...), custom_call_target="tpu_custom_call" | custom-call | flops 8000000 | bytes 1000000 | tf_op jit(solution)/shard_map/pallas_call | solution.py:602
  27.9 0.9 %collective-permute-start.9 = (f32[32,128]{1,0:T(8,128)S(1)}, f32[32,128]{1,0:T(8,128)S(1)}, u32[]{:S(2)}, u32[]{:S(2)}) collective-permute-start(f32[32,128]{1,0:T(8,128)S(1)} %shard_map.75), channel_id=1, source_target_pairs={{0,16},{1,17},{2,18},{3,19},{4,20},{5,21},{6,22},{7,23},{8,24},{9,... | collective-permute-start | bytes 49160 | tf_op jit(solution)/shard_map/ppermute | solution.py:627
  28.9 0.3 collective-permute-done.5.q_ref
  29.1 0.3 shard_map.74
  29.4 0.0 collective-permute-done.8.rest_ref
  29.5 2.3 %collective-permute-done.9.upper_ref = f32[32,128]{1,0:T(8,128)S(1)} collective-permute-done((f32[32,128]{1,0:T(8,128)S(1)}, f32[32,128]{1,0:T(8,128)S(1)}, u32[]{:S(2)}, u32[]{:S(2)}) %collective-permute-start.9) | collective-permute-done | bytes 16416 | tf_op jit(solution)/shard_map/ppermute | solution.py:627
  31.7 0.7 %shard_map.76 = (f32[6,64,128]{2,1,0:T(8,128)}, f32[64,128]{1,0:T(8,128)}) custom-call(f32[6,64,128]{2,1,0:T(8,128)S(1)} %get-tuple-element.58.ocean_ref, f32[4,40,128]{2,1,0:T(8,128)S(1)} %collective-permute-done.6.gb_ref.refs_0_.over_ref, f32[264,128]{1,0:T(8,128)S(1)} %collective-permute-done.8.rest_ref, f32[64,128]{1,0:T(8,128)S(1)} %get-tuple-element.60.chl_ref, ...), custom_call_target="tpu_custom_call" | custom-call | flops 1000000 | bytes 1000000 | tf_op jit(solution)/shard_map/pallas_call | solution.py:602
  (3 shorter events, 0.0 us)
Async XLA Ops:
  0.6 9.0 %copy-start.2 = (f32[19,19]{1,0:T(8,128)S(1)}, f32[19,19]{1,0:T(8,128)}, u32[]{:S(2)}) copy-start(f32[19,19]{1,0:T(8,128)} %r_ref.1) | copy-start | bytes 4336
  0.6 11.7 %copy-start = (f32[1,6,64,128]{3,2,1,0:T(8,128)S(1)}, f32[1,6,64,128]{3,2,1,0:T(8,128)}, u32[]{:S(2)}) copy-start(f32[1,6,64,128]{3,2,1,0:T(8,128)} %param.5) | copy-start | bytes 589828
  1.9 10.5 %collective-permute-start.3 = (f32[792,128]{1,0:T(8,128)S(1)}, f32[792,128]{1,0:T(8,128)S(1)}, u32[]{:S(2)}, u32[]{:S(2)}) collective-permute-start(f32[792,128]{1,0:T(8,128)S(1)} %get-tuple-element.35.pq_ref), channel_id=1, source_target_pairs={{0,1},{1,0},{2,3},{3,2},{4,5},{5,4},{6,7},{7,6},{8,9},{9,8},{10,11... | collective-permute-start | bytes 1216520 | tf_op jit(solution)/shard_map/ppermute | solution.py:627
  2.4 11.0 %collective-permute-start = (f32[536,128]{1,0:T(8,128)S(1)}, f32[536,128]{1,0:T(8,128)S(1)}, u32[]{:S(2)}, u32[]{:S(2)}) collective-permute-start(f32[536,128]{1,0:T(8,128)S(1)} %get-tuple-element.36), channel_id=1, source_target_pairs={{0,15},{1,2},{2,1},{3,4},{4,3},{5,6},{6,5},{7,8},{8,7},{9,10},{10,... | collective-permute-start | bytes 823304 | tf_op jit(solution)/shard_map/ppermute | solution.py:627
  8.1 7.2 %collective-permute-start.1 = (f32[256,128]{1,0:T(8,128)S(1)}, f32[256,128]{1,0:T(8,128)S(1)}, u32[]{:S(2)}, u32[]{:S(2)}) collective-permute-start(f32[256,128]{1,0:T(8,128)S(1)} %get-tuple-element.37), channel_id=1, source_target_pairs={{0,15},{1,2},{2,1},{3,4},{4,3},{5,6},{6,5},{7,8},{8,7},{9,10},{10,... | collective-permute-start | bytes 393224 | tf_op jit(solution)/shard_map/ppermute | solution.py:627
  8.1 4.3 %collective-permute-start.2 = (f32[4,32,128]{2,1,0:T(8,128)S(1)}, f32[4,32,128]{2,1,0:T(8,128)S(1)}, u32[]{:S(2)}, u32[]{:S(2)}) collective-permute-start(f32[4,32,128]{2,1,0:T(8,128)S(1)} %get-tuple-element.38), channel_id=1, source_target_pairs={{0,16},{1,17},{2,18},{3,19},{4,20},{5,21},{6,22},{7,23},{8,24},{9,... | collective-permute-start | bytes 196616 | tf_op jit(solution)/shard_map/ppermute | solution.py:627
  9.6 2.7 %copy-start.1 = (s32[3,128]{1,0:T(4,128)S(1)}, s32[3,128]{1,0:T(4,128)}, u32[]{:S(2)}) copy-start(s32[3,128]{1,0:T(4,128)} %nb_ref.11) | copy-start | bytes 4612
  15.6 10.9 %collective-permute-start.7 = (f32[792,128]{1,0:T(8,128)S(1)}, f32[792,128]{1,0:T(8,128)S(1)}, u32[]{:S(2)}, u32[]{:S(2)}) collective-permute-start(f32[792,128]{1,0:T(8,128)S(1)} %get-tuple-element.49.pq_ref), channel_id=1, source_target_pairs={{0,1},{1,0},{2,3},{3,2},{4,5},{5,4},{6,7},{7,6},{8,9},{9,8},{10,11... | collective-permute-start | bytes 1216520 | tf_op jit(solution)/shard_map/ppermute | solution.py:627
  15.6 11.8 %collective-permute-start.4 = (f32[536,128]{1,0:T(8,128)S(1)}, f32[536,128]{1,0:T(8,128)S(1)}, u32[]{:S(2)}, u32[]{:S(2)}) collective-permute-start(f32[536,128]{1,0:T(8,128)S(1)} %get-tuple-element.46.done_ref.chl_ref), channel_id=1, source_target_pairs={{0,15},{1,2},{2,1},{3,4},{4,3},{5,6},{6,5},{7,8},{8,7},{9,10},{10,... | collective-permute-start | bytes 823304 | tf_op jit(solution)/shard_map/ppermute | solution.py:627
  20.2 9.2 %collective-permute-start.8 = (f32[264,128]{1,0:T(8,128)S(1)}, f32[264,128]{1,0:T(8,128)S(1)}, u32[]{:S(2)}, u32[]{:S(2)}) collective-permute-start(f32[264,128]{1,0:T(8,128)S(1)} %get-tuple-element.59), channel_id=1, source_target_pairs={{0,16},{1,17},{2,18},{3,19},{4,20},{5,21},{6,22},{7,23},{8,24},{9,... | collective-permute-start | bytes 405512 | tf_op jit(solution)/shard_map/ppermute | solution.py:627
  22.0 7.1 %collective-permute-start.5 = (f32[256,128]{1,0:T(8,128)S(1)}, f32[256,128]{1,0:T(8,128)S(1)}, u32[]{:S(2)}, u32[]{:S(2)}) collective-permute-start(f32[256,128]{1,0:T(8,128)S(1)} %get-tuple-element.50), channel_id=1, source_target_pairs={{0,15},{1,2},{2,1},{3,4},{4,3},{5,6},{6,5},{7,8},{8,7},{9,10},{10,... | collective-permute-start | bytes 393224 | tf_op jit(solution)/shard_map/ppermute | solution.py:627
  22.0 4.4 %collective-permute-start.6 = (f32[4,40,128]{2,1,0:T(8,128)S(1)}, f32[4,40,128]{2,1,0:T(8,128)S(1)}, u32[]{:S(2)}, u32[]{:S(2)}) collective-permute-start(f32[4,40,128]{2,1,0:T(8,128)S(1)} %get-tuple-element.51), channel_id=1, source_target_pairs={{0,16},{1,17},{2,18},{3,19},{4,20},{5,21},{6,22},{7,23},{8,24},{9,... | collective-permute-start | bytes 245768 | tf_op jit(solution)/shard_map/ppermute | solution.py:627
  27.9 3.8 %collective-permute-start.9 = (f32[32,128]{1,0:T(8,128)S(1)}, f32[32,128]{1,0:T(8,128)S(1)}, u32[]{:S(2)}, u32[]{:S(2)}) collective-permute-start(f32[32,128]{1,0:T(8,128)S(1)} %shard_map.75), channel_id=1, source_target_pairs={{0,16},{1,17},{2,18},{3,19},{4,20},{5,21},{6,22},{7,23},{8,24},{9,... | collective-permute-start | bytes 49160 | tf_op jit(solution)/shard_map/ppermute | solution.py:627
